TPU v7x, 32 devices: a whole 2x2x4 slice. The times are simulated.
32 devices in a mesh: slab: 2 (over y), gx: 4 (over z), gy: 4 (over x, core).
Axes of the slice: x: 2, y: 2, z: 4, core: 2. Of those that a mesh axis runs over, the one named last changes fastest.
Arguments:
- charge: float32 [32, 512, 512], P(None, ('slab', 'gx'), 'gy'), parts along dimension 1, may hold values from -6 to 6
- surface_charge: float32 [2, 512, 512], P(None, ('slab', 'gx'), 'gy'), parts along dimension 1, may hold values from -6 to 6
Outputs:
- potential: float32 [32, 512, 512], P(None, ('slab', 'gx'), 'gy'), parts along dimension 1
- interface_residual: float32 [32, 512, 512], P(None, ('slab', 'gx'), 'gy'), parts along dimension 1
There are 2 independent parts, one for each index of `slab`. A program takes and returns all parts, laid end to end along the dimension named above; each array names one. Nothing has to cross between parts.
All inputs are finite; a program needn't handle non-finite values.
Results may differ from a plain program's by a relative error of at most 0.0003.
Values sent between devices are 32-bit elements; how exact they have to be, the bound alone decides.
No kernel may reach another device: no remote copies, remote signals or barrier semaphores. Data moves between devices by JAX's collectives and lax.ppermute only.
A program may use at most 64 MiB of HBM per device.

v0:
```python
import numpy as np
import jax
import jax.numpy as jnp
from jax import lax
from jax.experimental import pallas as pl
from jax.experimental.pallas import tpu as pltpu
from jax.sharding import PartitionSpec as P
import ml_dtypes

SCREEN = 0.02
BF16 = jnp.bfloat16
F32 = jnp.float32


def sine_ext(n):
    i = np.arange(n)
    table = np.sqrt(2.0 / n) * np.sin(np.pi * np.outer(i, i) / n)
    table[0, 0] = 1.0
    return table


def split_bf16(table):
    hi = table.astype(np.float32).astype(ml_dtypes.bfloat16)
    lo = (table - hi.astype(np.float64)).astype(np.float32).astype(ml_dtypes.bfloat16)
    return hi, lo


def make_tables(depth, width, height):
    lanes = 128
    groups = lanes // depth
    rows = height // groups
    tab = {}
    hi, lo = split_bf16(sine_ext(height))
    tab["eyw"] = np.block([[hi, lo], [hi, np.zeros_like(lo)]])
    hi, lo = split_bf16(sine_ext(width))
    tab["exw"] = np.concatenate([hi, lo, hi], 1)
    z = np.arange(depth)
    cos = np.cos(np.pi * np.outer(z + 0.5, z) / depth) * np.sqrt(2.0 / depth)
    cos[:, 0] = np.sqrt(1.0 / depth)
    tab["cz"] = cos.astype(np.float32)
    czt = np.zeros((lanes, lanes))
    czt[:depth, :depth] = cos.T
    tab["czt"] = czt.astype(np.float32)
    lz = SCREEN + 2.0 - 2.0 * np.cos(np.pi * z / depth)
    a = np.arange(width)
    b = np.arange(height)
    lx = 2.0 - 2.0 * np.cos(np.pi * a / width)
    ly = 2.0 - 2.0 * np.cos(np.pi * b / height)
    sx = np.sqrt(2.0 / width) * np.sin(np.pi * a / width)
    sy = np.sqrt(2.0 / height) * np.sin(np.pi * b / height)
    sga = np.where(a % 2 == 1, 1.0, -1.0)
    sgb = np.where(b % 2 == 1, 1.0, -1.0)
    inside = (a[:, None] > 0) & (b[None, :] > 0)
    inv = np.where(inside[None], 1.0 / (lz[:, None, None] + lx[None, :, None] + ly[None, None, :]), 0.0)
    tab["inv"] = inv.astype(np.float32)

    def to_rows(kb):
        return kb.T.reshape(groups, rows, depth).transpose(1, 0, 2).reshape(rows, lanes)

    def to_cols(ka):
        return np.tile(ka.T, (1, groups))

    inv2 = inv.transpose(2, 1, 0).reshape(groups, rows, width, depth)
    tab["inv2"] = inv2.transpose(1, 2, 0, 3).reshape(rows, width, lanes).astype(np.float32)
    ones = np.ones((depth, 1))
    odd_a, odd_b = sga > 0, sgb > 0
    sx2, sy2 = (sx**2)[None, :, None] * inv, (sy**2)[None, None, :] * inv
    tab["rowt"] = np.stack([
        to_rows(ones * sy),
        to_rows(ones * (sy * sgb)),
        to_rows(sx2[:, odd_a].sum(1)),
        to_rows(sx2[:, ~odd_a].sum(1)),
        to_rows((lz[:, None] + 2.0 + ly) * (b > 0)),
    ]).astype(np.float32)
    tab["colt"] = np.stack([
        to_cols(ones * sx),
        to_cols(ones * (sx * sga)),
        to_cols(sy2[:, :, odd_b].sum(2)),
        to_cols(sy2[:, :, ~odd_b].sum(2)),
        to_cols((lz[:, None] + 2.0 + lx) * (a > 0)),
    ]).astype(np.float32)
    tab["crnt"] = np.tile(np.tile(lz + 4.0, groups)[None], (8, 1)).astype(np.float32)
    tab["sx0"] = np.tile(sx[:, None], (1, height)).astype(np.float32)
    lane = np.zeros((8, height))
    lane[0], lane[1] = sy, sy * sgb
    lane[2], lane[3] = np.where(b > 0, sy, 1.0), sy * sgb
    tab["sy0"] = lane.astype(np.float32)
    return tab


def cosine_fwd(xs, scale):
    n = len(xs)
    if n == 1:
        return [xs[0] * (scale / np.sqrt(2.0))]
    half = n // 2
    even = cosine_fwd([xs[j] + xs[n - 1 - j] for j in range(half)], scale)
    diff = [xs[j] - xs[n - 1 - j] for j in range(half)]
    out = [None] * n
    for m in range(half):
        out[2 * m] = even[m]
        acc = None
        for j in range(half):
            term = diff[j] * float(scale * np.cos(np.pi * (2 * m + 1) * (2 * j + 1) / (2 * n)))
            acc = term if acc is None else acc + term
        out[2 * m + 1] = acc
    return out


def cosine_back(ys, scale):
    n = len(ys)
    if n == 1:
        return [ys[0] * (scale / np.sqrt(2.0))]
    half = n // 2
    even = cosine_back(ys[0::2], scale)
    out = [None] * n
    for j in range(half):
        acc = None
        for m in range(half):
            term = ys[2 * m + 1] * float(scale * np.cos(np.pi * (2 * m + 1) * (2 * j + 1) / (2 * n)))
            acc = term if acc is None else acc + term
        out[j] = even[j] + acc
        out[n - 1 - j] = even[j] - acc
    return out


def halves(x):
    hi = x.astype(BF16)
    return hi, (x - hi.astype(F32)).astype(BF16)


def times_sy(x, eyw):
    hi, lo = halves(x)
    n = x.shape[1]
    out = jnp.dot(jnp.concatenate([hi, lo], 1), eyw, preferred_element_type=F32)
    return out[:, :n] + out[:, n:]


def sx_times(exw, x):
    hi, lo = halves(x)
    return jnp.dot(exw, jnp.concatenate([hi, hi, lo], 0), preferred_element_type=F32)


def lane_id(shape):
    return lax.broadcasted_iota(jnp.int32, shape, 1)


def by_group(pieces, depth):
    group = lane_id(pieces[0].shape) // depth
    out = pieces[0]
    for h in range(1, len(pieces)):
        out = jnp.where(group == h, pieces[h], out)
    return out


def spread(x, depth):
    width = x.shape[1] // 2
    while width >= depth:
        x = x + pltpu.roll(x, width, 1)
        width //= 2
    return x


def pack(col, depth):
    groups = 128 // depth
    size = col.shape[0] // groups
    return by_group([col[h * size:(h + 1) * size] for h in range(groups)], depth)


def unpack(packed, depth):
    groups = 128 // depth
    group = lane_id(packed.shape) // depth
    return jnp.concatenate(
        [spread(jnp.where(group == h, packed, 0.0), depth) for h in range(groups)], 0
    )


def copies_t(kb):
    groups = 128 // kb.shape[0]
    return jnp.concatenate([kb] * groups, 0).T


def rows_from(kbt, depth):
    groups = 128 // depth
    size = kbt.shape[0] // groups
    return by_group([kbt[h * size:(h + 1) * size] for h in range(groups)], depth)


def rows_back(row, depth):
    groups = 128 // depth
    parts = [row] + [pltpu.roll(row, 128 - h * depth, 1) for h in range(1, groups)]
    return jnp.concatenate(parts, 0).T[:depth]


def total(x):
    return jnp.sum(x, 0, keepdims=True)


def sub_sums(ref):
    plus = minus = None
    for s in range(8):
        part = ref[:, s, :]
        if s % 2 == 1:
            plus = part if plus is None else plus + part
        else:
            minus = part if minus is None else minus + part
    return plus + minus, plus - minus


def with_tail(body, tails):
    width = body.shape[1]
    rows = list(tails) + [jnp.zeros((8 - len(tails), width), F32)]
    return jnp.concatenate([body, jnp.concatenate(rows, 0)], 0)


def front_kernel(charge, surf, eyw, exw, inv, sx0, sy0, base, px, nx, py, ny, work, part, first):
    depth, width, height = charge.shape
    scale = np.sqrt(2.0 / depth)

    def columns(i, carry):
        at = pl.ds(pl.multiple_of(i * 8, 8), 8)
        xs = [charge[z, at, :] for z in range(depth)]
        xs[0] = xs[0] + surf[0, at, :]
        xs[-1] = xs[-1] + surf[1, at, :]
        for k, value in enumerate(cosine_fwd(xs, scale)):
            work[k, at, :] = value
        return carry

    lax.fori_loop(0, width // 8, columns, 0)
    step = 4
    for c in range(0, depth, step):
        block = work[c:c + step].reshape(step * width, height)
        work[c:c + step] = times_sy(block, eyw[...]).reshape(step, width, height)
    lane = lane_id((width, 128))
    zero = jnp.zeros((width, 128), F32)
    near, far, own = zero, zero, zero
    for c in range(0, depth, 2):
        pair = sx_times(exw[...], jnp.concatenate([work[c], work[c + 1]], 1))
        for k in (c, c + 1):
            spec = pair[:, (k - c) * height:(k - c + 1) * height]
            inner = spec * inv[k]
            base[k] = inner
            first[k] = spec[0:8]
            part[k] = jnp.sum((inner * sx0[...]).reshape(width // 8, 8, height), 0)
            here = lane % depth == k
            near = jnp.where(here, jnp.sum(inner * sy0[0:1, :], 1, keepdims=True), near)
            far = jnp.where(here, jnp.sum(inner * sy0[1:2, :], 1, keepdims=True), far)
            own = jnp.where(here, spec[:, 0:1], own)
    row_near, row_far = sub_sums(part)
    own_t = copies_t(first[:, 0, :])
    corner = own_t[0:1]
    row = rows_from(own_t + copies_t(row_near), depth)
    at_zero = (lax.broadcasted_iota(jnp.int32, row.shape, 0) == 0) & (lane_id(row.shape) < depth)
    row = jnp.where(at_zero, 0.0, row)
    col = jnp.where(lax.broadcasted_iota(jnp.int32, own.shape, 0) == 0, 0.0, own + near)
    px[...] = with_tail(row, [corner])
    nx[...] = with_tail(rows_from(copies_t(row_far), depth), [])
    py[...] = with_tail(pack(col, depth), [corner])
    ny[...] = with_tail(pack(far, depth), [])


def assemble(depth, own, got):
    (px, nx, py, ny), (from_nx, from_px, from_ny, from_py) = own, got
    rows, cols = px.shape[0] - 8, py.shape[0] - 8
    row = px[:rows] + from_px[:rows]
    row_n = from_nx[:rows] + nx[:rows]
    col = unpack(py[:cols] + from_py[:cols], depth)
    col_n = unpack(from_ny[:cols] + ny[:cols], depth)
    c00 = px[rows:rows + 1] + from_px[rows:rows + 1] + from_py[cols:cols + 1]
    cx0 = from_nx[rows:rows + 1] + nx[rows:rows + 1] + from_py[cols + 1:cols + 2]
    c0y = from_ny[cols:cols + 1] + ny[cols:cols + 1] + from_px[rows + 1:rows + 2]
    return row, row_n, col, col_n, c00, cx0, c0y


def sizes(rows, cols):
    offs = np.cumsum([0, rows, rows, cols, cols])
    return [slice(int(offs[i]), int(offs[i + 1])) for i in range(4)] + [int(offs[4])]


def unpacked_state(state, rows, cols):
    s = sizes(rows, cols)
    at = s[4]
    return tuple(state[s[i], :] for i in range(4)) + tuple(state[at + i:at + i + 1, :] for i in range(3))


def schur_kernel(depth, want_moments, *refs):
    own, got = [r[...] for r in refs[0:4]], [r[...] for r in refs[4:8]]
    inv2, rowt, colt, crnt = refs[8:12]
    rest = list(refs[12:])
    before = rest.pop(0) if want_moments else None
    state, px, nx, py, ny = rest[:5]
    moments = rest[5] if want_moments else None
    part, odd_rows, even_rows = rest[-3:]
    row, row_n, col, col_n, c00, cx0, c0y = assemble(depth, own, got)
    rows, cols = row.shape[0], col.shape[0]
    s = sizes(rows, cols)
    for i, piece in enumerate((row, row_n, col, col_n)):
        state[s[i], :] = piece
    state[s[4]:s[4] + 8, :] = jnp.concatenate([c00, cx0, c0y, jnp.zeros((5, 128), F32)], 0)
    sy, sys, g_odd, g_even, d_row = (rowt[i] for i in range(5))
    sx, sxs, h_odd, h_even, d_col = (colt[i] for i in range(5))
    row_p, row_m, col_p, col_m = row + row_n, row - row_n, col + col_n, col - col_n
    odd_rows[...] = row_p * sy
    even_rows[...] = row_m * sy
    col_w = (col_m * sx, col_p * sx)
    odd = lax.broadcasted_iota(jnp.int32, (8, 128), 0) % 2 == 1
    acc = [None, None]
    for r in range(rows):
        table = inv2[r].reshape(cols // 8, 8, 128)
        part[r] = jnp.sum(table * col_w[r % 2].reshape(cols // 8, 8, 128), 0)
        pick = jnp.where(odd, odd_rows[r:r + 1, :], even_rows[r:r + 1, :])
        term = table * pick[None]
        acc[r % 2] = term if acc[r % 2] is None else acc[r % 2] + term
    row_s, row_d = sub_sums(part)
    acc_s = spread((acc[1] + acc[0]).reshape(cols, 128), depth)
    acc_d = spread((acc[1] - acc[0]).reshape(cols, 128), depth)
    diag_o, diag_e = g_odd * row_p, g_even * row_m
    x_near = sy * row_s + (diag_o + diag_e)
    x_far = sy * row_d + (diag_o - diag_e)
    diag_o, diag_e = h_odd * col_p, h_even * col_m
    y_near = sx * acc_s + (diag_o + diag_e)
    y_far = sx * acc_d + (diag_o - diag_e)
    row_img = d_row * row - sy * c00 - sys * c0y - x_near
    col_img = d_col * col - sx * c00 - sxs * cx0 - y_near
    row_end0 = spread(total(sy * row), depth)
    row_end1 = spread(total(sys * row), depth)
    row_end1n = spread(total(sys * row_n), depth)
    col_end0 = total(sx * col)
    col_end1 = total(sxs * col)
    col_end1n = total(sxs * col_n)
    q00 = crnt[0:1, :] * c00 - row_end0 - col_end0
    px[...] = with_tail(row_img, [q00])
    nx[...] = with_tail(-x_far, [-col_end1, -col_end1n])
    py[...] = with_tail(pack(col_img, depth), [q00])
    ny[...] = with_tail(pack(-y_far, depth), [-row_end1, -row_end1n])
    if want_moments:
        row0, _, col0, _, c000, _, _ = unpacked_state(before, rows, cols)
        share = depth / 128.0

        def dot(x, y):
            return total(x[0] * y[0]) + share * (total(x[1] * y[1]) + x[2] * y[2])

        v0, v1 = (row0, col0, c000), (row, col, c00)
        m3 = total(row * row_img - row_n * x_far) + share * (
            total(col * col_img - col_n * y_far) + c00 * q00 - c0y * row_end1 - cx0 * col_end1
        )
        moments[...] = jnp.concatenate([dot(v0, v0), dot(v0, v1), dot(v1, v1), m3, jnp.zeros((4, 128), F32)], 0)


def back_kernel(depth, n_moments, *refs):
    base, s0, s1, px, py, from_px, from_py = refs[:7]
    moms = refs[7:7 + n_moments]
    eyw, exw, inv, sx0, sy0, cz, czt = refs[7 + n_moments:14 + n_moments]
    potential, residual, work = refs[14 + n_moments:]
    _, width, height = base.shape
    rows, cols = px.shape[0] - 8, width
    packed = py.shape[0] - 8
    m = moms[0][...]
    for other in moms[1:]:
        m = m + other[...]
    m = jnp.broadcast_to(jnp.sum(m, 1, keepdims=True), (8, 128))
    m0 = m[0:1]
    n1, n2, n3 = m[1:2] / m0, m[2:3] / m0, m[3:4] / m0
    det = n1 * n3 - n2 * n2
    fine = det > 1e-6 * (n1 * n3)
    safe = jnp.where(fine, det, 1.0)
    c0 = jnp.where(fine, (n3 - n1 * n2) / safe, 1.0 / n1)
    c1 = jnp.where(fine, (n1 * n1 - n2) / safe, 0.0)
    v0 = unpacked_state(s0, rows, cols)
    v1 = unpacked_state(s1, rows, cols)
    row, row_n, col, col_n, c00 = (c0 * v0[i] + c1 * v1[i] for i in range(5))
    row2 = px[:rows, :] + from_px[:rows, :]
    col2 = unpack(py[:packed, :] + from_py[:packed, :], depth)
    c2 = px[rows:rows + 1, :] + from_px[rows:rows + 1, :] + from_py[packed:packed + 1, :]
    res_row = v0[0] - c0 * v1[0] - c1 * row2
    res_col = v0[2] - c0 * v1[2] - c1 * col2
    res_c = v0[4] - c0 * v1[4] - c1 * c2
    at_zero = (lax.broadcasted_iota(jnp.int32, row.shape, 0) == 0) & (lane_id(row.shape) < depth)
    row_p = rows_back(row + row_n, depth)
    row_m = rows_back(row - row_n, depth)
    row_full = rows_back(jnp.where(at_zero, c00, row), depth)
    res_row = rows_back(jnp.where(at_zero, res_c, res_row), depth)
    odd = lax.broadcasted_iota(jnp.int32, (8, height), 0) % 2 == 1
    top = lax.broadcasted_iota(jnp.int32, (width, height), 0) == 0
    lane0 = lane_id((width, height)) == 0
    for c in range(0, depth, 2):
        pieces = []
        for k in (c, c + 1):
            pick = jnp.where(odd, row_p[k:k + 1], row_m[k:k + 1])
            pick = jnp.broadcast_to(pick[None], (width // 8, 8, height)).reshape(width, height)
            rim = sx0[...] * pick + col[:, k:k + 1] * sy0[2:3, :] + col_n[:, k:k + 1] * sy0[3:4, :]
            weight = jnp.where(lane0, 1.0, inv[k])
            pieces.append(jnp.where(top, row_full[k:k + 1], base[k] + weight * rim))
        pair = sx_times(exw[...], jnp.concatenate(pieces, 1))
        work[c] = pair[:, :height]
        work[c + 1] = pair[:, height:]
    step = 4
    for c in range(0, depth, step):
        block = work[c:c + step].reshape(step * width, height)
        work[c:c + step] = times_sy(block, eyw[...]).reshape(step, width, height)
    scale = np.sqrt(2.0 / depth)

    def columns(i, carry):
        at = pl.ds(pl.multiple_of(i * 8, 8), 8)
        for z, value in enumerate(cosine_back([work[k, at, :] for k in range(depth)], scale)):
            potential[z, at, :] = value
        return carry

    lax.fori_loop(0, width // 8, columns, 0)
    high = lax.Precision.HIGHEST
    rim_row = jnp.dot(cz[...], times_sy(res_row, eyw[...]), precision=high, preferred_element_type=F32)
    res_col = sx_times(exw[...], res_col)
    rim_col = jnp.dot(res_col, czt[...], precision=high, preferred_element_type=F32)
    for z in range(depth):
        residual[z] = jnp.where(top, rim_row[z:z + 1], jnp.where(lane0, rim_col[:, z:z + 1], 0.0))


def shifted(value, axis, by):
    n = lax.axis_size(axis)
    return lax.ppermute(value, axis, [(i, (i + by) % n) for i in range(n)])


def exchange(px, nx, py, ny):
    return (shifted(px, "gx", -1), shifted(nx, "gx", 1), shifted(py, "gy", -1), shifted(ny, "gy", 1))


def pieces_over(value, axis):
    n, stride = lax.axis_size(axis), 1
    while True:
        radix = 4 if n % 4 == 0 else 2 if n % 2 == 0 else n
        parts = [value] + [shifted(value, axis, stride * j) for j in range(1, radix)]
        n, stride = n // radix, stride * radix
        if n == 1:
            return parts
        value = sum(parts[1:], parts[0])


def call(kernel, outs, scratch):
    return pl.pallas_call(
        kernel,
        out_shape=[jax.ShapeDtypeStruct(shape, F32) for shape in outs],
        scratch_shapes=[pltpu.VMEM(shape, F32) for shape in scratch],
        compiler_params=pltpu.CompilerParams(vmem_limit_bytes=48 * 1024 * 1024),
    )


def on_device(charge, surface_charge):
    depth, width, height = charge.shape
    tab = {name: jnp.asarray(value) for name, value in make_tables(depth, width, height).items()}
    rows, packed = height * depth // 128, width * depth // 128
    msgs = [(rows + 8, 128)] * 2 + [(packed + 8, 128)] * 2
    state = (2 * rows + 2 * width + 8, 128)
    block = (depth, width, height)
    base, *own = call(front_kernel, [block] + msgs, [block, (depth, 8, height), (depth, 8, height)])(
        charge, surface_charge, tab["eyw"], tab["exw"], tab["inv"], tab["sx0"], tab["sy0"]
    )
    got = exchange(*own)
    tables = (tab["inv2"], tab["rowt"], tab["colt"], tab["crnt"])
    scratch = [(rows, 8, 128), (rows, 128), (rows, 128)]
    s0, *own = call(lambda *r: schur_kernel(depth, False, *r), [state] + msgs, scratch)(*own, *got, *tables)
    got = exchange(*own)
    s1, px, nx, py, ny, moments = call(
        lambda *r: schur_kernel(depth, True, *r), [state] + msgs + [(8, 128)], scratch
    )(*own, *got, *tables, s0)
    parts = pieces_over(moments, "gx")
    from_px, from_py = shifted(nx, "gx", 1), shifted(ny, "gy", 1)
    parts = pieces_over(sum(parts[1:], parts[0]), "gy")
    return call(lambda *r: back_kernel(depth, len(parts), *r), [block, block], [block])(
        base, s0, s1, px, py, from_px, from_py, *parts,
        tab["eyw"], tab["exw"], tab["inv"], tab["sx0"], tab["sy0"], tab["cz"], tab["czt"],
    )


def solution(mesh):
    spec = P(None, ("slab", "gx"), "gy")
    return jax.shard_map(
        on_device, mesh=mesh, in_specs=(spec, spec), out_specs=(spec, spec), check_vma=False
    )
```

profile of v0, /device:TPU:0, one launch (start us, length us, event | category | flops | bytes accessed | tf_op | source)
XLA Modules:
  0.0 43.9 jit_solution(11822769346102336987)
XLA Ops:
  0.6 0.0 copy-start.14
  0.6 0.7 %copy-done.14 = f32[8,128]{1,0:T(8,128)S(1)} copy-done((f32[8,128]{1,0:T(8,128)S(1)}, f32[8,128]{1,0:T(8,128)}, u32[]{:S(2)}) %copy-start.14) | copy-done | bytes 4120
  1.3 1.2 %copy-done = f32[32,64,128]{2,1,0:T(8,128)S(1)} copy-done((f32[32,64,128]{2,1,0:T(8,128)S(1)}, f32[32,64,128]{2,1,0:T(8,128)}, u32[]{:S(2)}) %copy-start) | copy-done | bytes 1048600
  2.5 1.2 %copy-done.3 = f32[32,64,128]{2,1,0:T(8,128)S(1)} copy-done((f32[32,64,128]{2,1,0:T(8,128)S(1)}, f32[32,64,128]{2,1,0:T(8,128)}, u32[]{:S(2)}) %copy-start.3) | copy-done | bytes 1048600
  3.8 0.9 %copy-done.5 = bf16[256,256]{1,0:T(8,128)(2,1)S(1)} copy-done((bf16[256,256]{1,0:T(8,128)(2,1)S(1)}, bf16[256,256]{1,0:T(8,128)(2,1)}, u32[]{:S(2)}) %copy-start.5) | copy-done | bytes 131096
  4.7 0.8 %copy-done.8 = f32[64,128]{1,0:T(8,128)S(1)} copy-done((f32[64,128]{1,0:T(8,128)S(1)}, f32[64,128]{1,0:T(8,128)}, u32[]{:S(2)}) %copy-start.8) | copy-done | bytes 32792
  5.4 0.8 %copy-done.9 = bf16[64,192]{1,0:T(8,128)(2,1)S(1)} copy-done((bf16[64,192]{1,0:T(8,128)(2,1)S(1)}, bf16[64,192]{1,0:T(8,128)(2,1)}, u32[]{:S(2)}) %copy-start.9) | copy-done | bytes 24600
  6.2 0.8 %copy-done.11 = f32[2,64,128]{2,1,0:T(8,128)S(1)} copy-done((f32[2,64,128]{2,1,0:T(8,128)S(1)}, f32[2,64,128]{2,1,0:T(8,128)}, u32[]{:S(2)}) %copy-start.11) | copy-done | bytes 65560
  7.0 2.5 %shard_map.140 = (f32[32,64,128]{2,1,0:T(8,128)S(1)}, f32[40,128]{1,0:T(8,128)S(1)}, f32[40,128]{1,0:T(8,128)S(1)}, f32[24,128]{1,0:T(8,128)S(1)}, f32[24,128]{1,0:T(8,128)S(1)}) custom-call(f32[32,64,128]{2,1,0:T(8,128)S(1)} %copy-done.3, f32[2,64,128]{2,1,0:T(8,128)S(1)} %copy-done.11, bf16[256,256]{1,0:T(8,128)(2,1)S(1)} %copy-done.5, ...), custom_call_target="tpu_custom_call" | custom-call | tf_op jit(solution)/shard_map/pallas_call | solution.py:453
  9.5 0.0 copy-start.15
  9.5 5.1 %collective-permute-start = (f32[40,128]{1,0:T(8,128)S(1)}, f32[40,128]{1,0:T(8,128)S(1)}, u32[]{:S(2)}, u32[]{:S(2)}) collective-permute-start(f32[40,128]{1,0:T(8,128)S(1)} %get-tuple-element.19.r_0_), channel_id=1, source_target_pairs={{0,12},{4,0},{8,4},{12,8},{1,13},{5,1},{9,5},{13,9},{2,14},{6,2},{... | collective-permute-start | bytes 61448 | tf_op jit(solution)/shard_map/ppermute | solution.py:419
  14.7 0.0 collective-permute-start.1
  14.7 0.7 %collective-permute-start.2 = (f32[24,128]{1,0:T(8,128)S(1)}, f32[24,128]{1,0:T(8,128)S(1)}, u32[]{:S(2)}, u32[]{:S(2)}) collective-permute-start(f32[24,128]{1,0:T(8,128)S(1)} %get-tuple-element.21.r_2_), channel_id=1, source_target_pairs={{0,3},{1,0},{2,1},{3,2},{4,7},{5,4},{6,5},{7,6},{8,11},{9,8},{10,9... | collective-permute-start | bytes 36872 | tf_op jit(solution)/shard_map/ppermute | solution.py:419
  15.3 0.0 collective-permute-start.3
  15.3 1.4 %collective-permute-done.2.r_6_ = f32[24,128]{1,0:T(8,128)S(1)} collective-permute-done((f32[24,128]{1,0:T(8,128)S(1)}, f32[24,128]{1,0:T(8,128)S(1)}, u32[]{:S(2)}, u32[]{:S(2)}) %collective-permute-start.2) | collective-permute-done | bytes 12320 | tf_op jit(solution)/shard_map/ppermute | solution.py:419
  16.7 1.7 %collective-permute-done.3.r_7_ = f32[24,128]{1,0:T(8,128)S(1)} collective-permute-done((f32[24,128]{1,0:T(8,128)S(1)}, f32[24,128]{1,0:T(8,128)S(1)}, u32[]{:S(2)}, u32[]{:S(2)}) %collective-permute-start.3) | collective-permute-done | bytes 12320 | tf_op jit(solution)/shard_map/ppermute | solution.py:419
  18.4 0.0 collective-permute-done.r_4_
  18.4 1.8 %collective-permute-done.1.r_5_ = f32[40,128]{1,0:T(8,128)S(1)} collective-permute-done((f32[40,128]{1,0:T(8,128)S(1)}, f32[40,128]{1,0:T(8,128)S(1)}, u32[]{:S(2)}, u32[]{:S(2)}) %collective-permute-start.1) | collective-permute-done | bytes 20512 | tf_op jit(solution)/shard_map/ppermute | solution.py:419
  20.2 0.0 copy-done.15
  20.3 0.4 shard_map.141
  20.7 0.0 copy-start.1
  20.7 1.8 %collective-permute-start.4 = (f32[40,128]{1,0:T(8,128)S(1)}, f32[40,128]{1,0:T(8,128)S(1)}, u32[]{:S(2)}, u32[]{:S(2)}) collective-permute-start(f32[40,128]{1,0:T(8,128)S(1)} %get-tuple-element.24.r_0_), channel_id=1, source_target_pairs={{0,12},{4,0},{8,4},{12,8},{1,13},{5,1},{9,5},{13,9},{2,14},{6,2},{... | collective-permute-start | bytes 61448 | tf_op jit(solution)/shard_map/ppermute | solution.py:419
  22.5 0.3 collective-permute-start.5
  22.8 0.0 collective-permute-start.6
  22.8 0.5 %collective-permute-start.7 = (f32[24,128]{1,0:T(8,128)S(1)}, f32[24,128]{1,0:T(8,128)S(1)}, u32[]{:S(2)}, u32[]{:S(2)}) collective-permute-start(f32[24,128]{1,0:T(8,128)S(1)} %get-tuple-element.27.r_3_), channel_id=1, source_target_pairs={{0,1},{1,2},{2,3},{3,0},{4,5},{5,6},{6,7},{7,4},{8,9},{9,10},{10,1... | collective-permute-start | bytes 36872 | tf_op jit(solution)/shard_map/ppermute | solution.py:419
  23.3 0.9 %collective-permute-done.6.r_6_ = f32[24,128]{1,0:T(8,128)S(1)} collective-permute-done((f32[24,128]{1,0:T(8,128)S(1)}, f32[24,128]{1,0:T(8,128)S(1)}, u32[]{:S(2)}, u32[]{:S(2)}) %collective-permute-start.6) | collective-permute-done | bytes 12320 | tf_op jit(solution)/shard_map/ppermute | solution.py:419
  24.2 1.7 %collective-permute-done.7.r_7_ = f32[24,128]{1,0:T(8,128)S(1)} collective-permute-done((f32[24,128]{1,0:T(8,128)S(1)}, f32[24,128]{1,0:T(8,128)S(1)}, u32[]{:S(2)}, u32[]{:S(2)}) %collective-permute-start.7) | collective-permute-done | bytes 12320 | tf_op jit(solution)/shard_map/ppermute | solution.py:419
  25.9 0.0 collective-permute-done.4.r_4_
  25.9 2.2 %collective-permute-done.5.r_5_ = f32[40,128]{1,0:T(8,128)S(1)} collective-permute-done((f32[40,128]{1,0:T(8,128)S(1)}, f32[40,128]{1,0:T(8,128)S(1)}, u32[]{:S(2)}, u32[]{:S(2)}) %collective-permute-start.5) | collective-permute-done | bytes 20512 | tf_op jit(solution)/shard_map/ppermute | solution.py:419
  28.1 0.4 %shard_map.142 = (f32[200,128]{1,0:T(8,128)S(1)}, f32[40,128]{1,0:T(8,128)S(1)}, f32[40,128]{1,0:T(8,128)S(1)}, f32[24,128]{1,0:T(8,128)S(1)}, f32[24,128]{1,0:T(8,128)S(1)}, /*index=5*/f32[8,128]{1,0:T(8,128)S(1)}) custom-call(f32[40,128]{1,0:T(8,128)S(1)} %get-tuple-element.24.r_0_, f32[40,128]{1,0:T(8,128)S(1)} %get-tuple-element.25.r_1_, ...), custom_call_target="tpu_custom_call" | custom-call | tf_op jit(solution)/shard_map/pallas_call | solution.py:461
  28.5 0.0 copy-start.10
  28.5 1.5 %collective-permute-start.12 = (f32[8,128]{1,0:T(8,128)S(1)}, f32[8,128]{1,0:T(8,128)S(1)}, u32[]{:S(2)}, u32[]{:S(2)}) collective-permute-start(f32[8,128]{1,0:T(8,128)S(1)} %get-tuple-element.33), channel_id=1, source_target_pairs={{0,12},{4,0},{8,4},{12,8},{1,13},{5,1},{9,5},{13,9},{2,14},{6,2},{... | collective-permute-start | bytes 12296 | tf_op jit(solution)/shard_map/ppermute | solution.py:419
  30.0 0.0 collective-permute-start.11
  30.0 0.6 %collective-permute-start.10 = (f32[8,128]{1,0:T(8,128)S(1)}, f32[8,128]{1,0:T(8,128)S(1)}, u32[]{:S(2)}, u32[]{:S(2)}) collective-permute-start(f32[8,128]{1,0:T(8,128)S(1)} %get-tuple-element.33), channel_id=1, source_target_pairs={{0,4},{4,8},{8,12},{12,0},{1,5},{5,9},{9,13},{13,1},{2,6},{6,10},{... | collective-permute-start | bytes 12296 | tf_op jit(solution)/shard_map/ppermute | solution.py:419
  30.6 0.0 collective-permute-start.9
  30.6 2.8 %collective-permute-start.8 = (f32[40,128]{1,0:T(8,128)S(1)}, f32[40,128]{1,0:T(8,128)S(1)}, u32[]{:S(2)}, u32[]{:S(2)}) collective-permute-start(f32[40,128]{1,0:T(8,128)S(1)} %get-tuple-element.31), channel_id=1, source_target_pairs={{0,4},{4,8},{8,12},{12,0},{1,5},{5,9},{9,13},{13,1},{2,6},{6,10},{... | collective-permute-start | bytes 61448 | tf_op jit(solution)/shard_map/ppermute | solution.py:419
  33.5 0.0 collective-permute-done.12
  33.5 1.0 %collective-permute-done.11 = f32[8,128]{1,0:T(8,128)S(1)} collective-permute-done((f32[8,128]{1,0:T(8,128)S(1)}, f32[8,128]{1,0:T(8,128)S(1)}, u32[]{:S(2)}, u32[]{:S(2)}) %collective-permute-start.11) | collective-permute-done | bytes 4128 | tf_op jit(solution)/shard_map/ppermute | solution.py:419
  34.5 0.9 %collective-permute-done.10 = f32[8,128]{1,0:T(8,128)S(1)} collective-permute-done((f32[8,128]{1,0:T(8,128)S(1)}, f32[8,128]{1,0:T(8,128)S(1)}, u32[]{:S(2)}, u32[]{:S(2)}) %collective-permute-start.10) | collective-permute-done | bytes 4128 | tf_op jit(solution)/shard_map/ppermute | solution.py:419
  35.4 0.0 collective-permute-start.15
  35.4 1.2 %collective-permute-start.14 = (f32[8,128]{1,0:T(8,128)S(1)}, f32[8,128]{1,0:T(8,128)S(1)}, u32[]{:S(2)}, u32[]{:S(2)}) collective-permute-start(f32[8,128]{1,0:T(8,128)S(1)} %add_add_fusion.r_7_), channel_id=1, source_target_pairs={{0,2},{1,3},{2,0},{3,1},{4,6},{5,7},{6,4},{7,5},{8,10},{9,11},{10,... | collective-permute-start | bytes 12296 | tf_op jit(solution)/shard_map/ppermute | solution.py:419
  36.6 0.2 collective-permute-start.13
  36.8 0.0 collective-permute-done.15.r_10_
  36.8 2.3 %collective-permute-done.14.r_9_ = f32[8,128]{1,0:T(8,128)S(1)} collective-permute-done((f32[8,128]{1,0:T(8,128)S(1)}, f32[8,128]{1,0:T(8,128)S(1)}, u32[]{:S(2)}, u32[]{:S(2)}) %collective-permute-start.14) | collective-permute-done | bytes 4128 | tf_op jit(solution)/shard_map/ppermute | solution.py:419
  39.1 0.5 %collective-permute-done.13.r_8_ = f32[8,128]{1,0:T(8,128)S(1)} collective-permute-done((f32[8,128]{1,0:T(8,128)S(1)}, f32[8,128]{1,0:T(8,128)S(1)}, u32[]{:S(2)}, u32[]{:S(2)}) %collective-permute-start.13) | collective-permute-done | bytes 4128 | tf_op jit(solution)/shard_map/ppermute | solution.py:419
  39.6 0.0 collective-permute-done.9.r_6_
  39.6 0.0 collective-permute-done.8.r_5_
  39.7 4.2 %shard_map.143 = (f32[32,64,128]{2,1,0:T(8,128)}, f32[32,64,128]{2,1,0:T(8,128)}) custom-call(f32[32,64,128]{2,1,0:T(8,128)S(1)} %get-tuple-element.18.r_0_, f32[200,128]{1,0:T(8,128)S(1)} %get-tuple-element.23.r_12_.r_1_, f32[200,128]{1,0:T(8,128)S(1)} %get-tuple-element.28.r_2_, f32[40,128]{1,0:T(8,128)S(1)} %get-tuple-element.29.r_3_, ...), custom_call_target="tpu_custom_call" | custom-call | tf_op jit(solution)/shard_map/pallas_call | solution.py:467
  (21 shorter events, 0.0 us)
Async XLA Ops:
  0.6 0.7 %copy-start.14 = (f32[8,128]{1,0:T(8,128)S(1)}, f32[8,128]{1,0:T(8,128)}, u32[]{:S(2)}) copy-start(f32[8,128]{1,0:T(8,128)} %constant.32.clone.sy0.r_15_) | copy-start | bytes 12292
  1.3 1.2 %copy-start = (f32[32,64,128]{2,1,0:T(8,128)S(1)}, f32[32,64,128]{2,1,0:T(8,128)}, u32[]{:S(2)}) copy-start(f32[32,64,128]{2,1,0:T(8,128)} %constant.26.clone.inv.r_13_) | copy-start | bytes 3145732
  2.5 1.2 %copy-start.3 = (f32[32,64,128]{2,1,0:T(8,128)S(1)}, f32[32,64,128]{2,1,0:T(8,128)}, u32[]{:S(2)}) copy-start(f32[32,64,128]{2,1,0:T(8,128)} %charge.1) | copy-start | bytes 3145732
  3.8 0.9 %copy-start.5 = (bf16[256,256]{1,0:T(8,128)(2,1)S(1)}, bf16[256,256]{1,0:T(8,128)(2,1)}, u32[]{:S(2)}) copy-start(bf16[256,256]{1,0:T(8,128)(2,1)} %constant.22.clone.eyw.r_11_) | copy-start | bytes 393220
  4.7 0.8 %copy-start.8 = (f32[64,128]{1,0:T(8,128)S(1)}, f32[64,128]{1,0:T(8,128)}, u32[]{:S(2)}) copy-start(f32[64,128]{1,0:T(8,128)} %constant.31.clone.sx0.r_14_) | copy-start | bytes 98308
  5.4 0.8 %copy-start.9 = (bf16[64,192]{1,0:T(8,128)(2,1)S(1)}, bf16[64,192]{1,0:T(8,128)(2,1)}, u32[]{:S(2)}) copy-start(bf16[64,192]{1,0:T(8,128)(2,1)} %constant.23.clone.exw.r_12_) | copy-start | bytes 73732
  6.2 0.8 %copy-start.11 = (f32[2,64,128]{2,1,0:T(8,128)S(1)}, f32[2,64,128]{2,1,0:T(8,128)}, u32[]{:S(2)}) copy-start(f32[2,64,128]{2,1,0:T(8,128)} %surf.1) | copy-start | bytes 196612
  7.0 13.2 %copy-start.2 = (f32[32,64,128]{2,1,0:T(8,128)S(1)}, f32[32,64,128]{2,1,0:T(8,128)}, u32[]{:S(2)}) copy-start(f32[32,64,128]{2,1,0:T(8,128)} %constant.27.clone.r_8_) | copy-start | bytes 3145732
  7.0 13.2 %copy-start.4 = (f32[5,64,128]{2,1,0:T(8,128)S(1)}, f32[5,64,128]{2,1,0:T(8,128)}, u32[]{:S(2)}) copy-start(f32[5,64,128]{2,1,0:T(8,128)} %constant.29.clone.r_10_) | copy-start | bytes 491524
  7.0 13.2 %copy-start.7 = (f32[5,32,128]{2,1,0:T(8,128)S(1)}, f32[5,32,128]{2,1,0:T(8,128)}, u32[]{:S(2)}) copy-start(f32[5,32,128]{2,1,0:T(8,128)} %constant.28.clone.r_9_) | copy-start | bytes 245764
  9.5 10.7 %copy-start.15 = (f32[8,128]{1,0:T(8,128)S(1)}, f32[8,128]{1,0:T(8,128)}, u32[]{:S(2)}) copy-start(f32[8,128]{1,0:T(8,128)} %constant.30.clone.r_11_) | copy-start | bytes 12292
  9.5 8.9 %collective-permute-start = (f32[40,128]{1,0:T(8,128)S(1)}, f32[40,128]{1,0:T(8,128)S(1)}, u32[]{:S(2)}, u32[]{:S(2)}) collective-permute-start(f32[40,128]{1,0:T(8,128)S(1)} %get-tuple-element.19.r_0_), channel_id=1, source_target_pairs={{0,12},{4,0},{8,4},{12,8},{1,13},{5,1},{9,5},{13,9},{2,14},{6,2},{... | collective-permute-start | bytes 61448 | tf_op jit(solution)/shard_map/ppermute | solution.py:419
  14.7 5.6 %collective-permute-start.1 = (f32[40,128]{1,0:T(8,128)S(1)}, f32[40,128]{1,0:T(8,128)S(1)}, u32[]{:S(2)}, u32[]{:S(2)}) collective-permute-start(f32[40,128]{1,0:T(8,128)S(1)} %get-tuple-element.20.r_1_), channel_id=1, source_target_pairs={{0,4},{4,8},{8,12},{12,0},{1,5},{5,9},{9,13},{13,1},{2,6},{6,10},{... | collective-permute-start | bytes 61448 | tf_op jit(solution)/shard_map/ppermute | solution.py:419
  14.7 2.1 %collective-permute-start.2 = (f32[24,128]{1,0:T(8,128)S(1)}, f32[24,128]{1,0:T(8,128)S(1)}, u32[]{:S(2)}, u32[]{:S(2)}) collective-permute-start(f32[24,128]{1,0:T(8,128)S(1)} %get-tuple-element.21.r_2_), channel_id=1, source_target_pairs={{0,3},{1,0},{2,1},{3,2},{4,7},{5,4},{6,5},{7,6},{8,11},{9,8},{10,9... | collective-permute-start | bytes 36872 | tf_op jit(solution)/shard_map/ppermute | solution.py:419
  15.3 3.1 %collective-permute-start.3 = (f32[24,128]{1,0:T(8,128)S(1)}, f32[24,128]{1,0:T(8,128)S(1)}, u32[]{:S(2)}, u32[]{:S(2)}) collective-permute-start(f32[24,128]{1,0:T(8,128)S(1)} %get-tuple-element.22.r_3_), channel_id=1, source_target_pairs={{0,1},{1,2},{2,3},{3,0},{4,5},{5,6},{6,7},{7,4},{8,9},{9,10},{10,1... | collective-permute-start | bytes 36872 | tf_op jit(solution)/shard_map/ppermute | solution.py:419
  20.7 19.0 %copy-start.1 = (f32[32,64,128]{2,1,0:T(8,128)S(1)}, f32[32,64,128]{2,1,0:T(8,128)}, u32[]{:S(2)}) copy-start(f32[32,64,128]{2,1,0:T(8,128)} %constant.26.clone.inv.r_13_) | copy-start | bytes 3145732
  20.7 5.2 %collective-permute-start.4 = (f32[40,128]{1,0:T(8,128)S(1)}, f32[40,128]{1,0:T(8,128)S(1)}, u32[]{:S(2)}, u32[]{:S(2)}) collective-permute-start(f32[40,128]{1,0:T(8,128)S(1)} %get-tuple-element.24.r_0_), channel_id=1, source_target_pairs={{0,12},{4,0},{8,4},{12,8},{1,13},{5,1},{9,5},{13,9},{2,14},{6,2},{... | collective-permute-start | bytes 61448 | tf_op jit(solution)/shard_map/ppermute | solution.py:419
  22.5 5.6 %collective-permute-start.5 = (f32[40,128]{1,0:T(8,128)S(1)}, f32[40,128]{1,0:T(8,128)S(1)}, u32[]{:S(2)}, u32[]{:S(2)}) collective-permute-start(f32[40,128]{1,0:T(8,128)S(1)} %get-tuple-element.25.r_1_), channel_id=1, source_target_pairs={{0,4},{4,8},{8,12},{12,0},{1,5},{5,9},{9,13},{13,1},{2,6},{6,10},{... | collective-permute-start | bytes 61448 | tf_op jit(solution)/shard_map/ppermute | solution.py:419
  22.8 1.4 %collective-permute-start.6 = (f32[24,128]{1,0:T(8,128)S(1)}, f32[24,128]{1,0:T(8,128)S(1)}, u32[]{:S(2)}, u32[]{:S(2)}) collective-permute-start(f32[24,128]{1,0:T(8,128)S(1)} %get-tuple-element.26.r_2_), channel_id=1, source_target_pairs={{0,3},{1,0},{2,1},{3,2},{4,7},{5,4},{6,5},{7,6},{8,11},{9,8},{10,9... | collective-permute-start | bytes 36872 | tf_op jit(solution)/shard_map/ppermute | solution.py:419
  22.8 3.1 %collective-permute-start.7 = (f32[24,128]{1,0:T(8,128)S(1)}, f32[24,128]{1,0:T(8,128)S(1)}, u32[]{:S(2)}, u32[]{:S(2)}) collective-permute-start(f32[24,128]{1,0:T(8,128)S(1)} %get-tuple-element.27.r_3_), channel_id=1, source_target_pairs={{0,1},{1,2},{2,3},{3,0},{4,5},{5,6},{6,7},{7,4},{8,9},{9,10},{10,1... | collective-permute-start | bytes 36872 | tf_op jit(solution)/shard_map/ppermute | solution.py:419
  28.1 11.6 %copy-start.6 = (bf16[256,256]{1,0:T(8,128)(2,1)S(1)}, bf16[256,256]{1,0:T(8,128)(2,1)}, u32[]{:S(2)}) copy-start(bf16[256,256]{1,0:T(8,128)(2,1)} %constant.22.clone.eyw.r_11_) | copy-start | bytes 393220
  28.1 11.6 %copy-start.12 = (f32[128,128]{1,0:T(8,128)S(1)}, f32[128,128]{1,0:T(8,128)}, u32[]{:S(2)}) copy-start(f32[128,128]{1,0:T(8,128)} %constant.25.clone.r_17_) | copy-start | bytes 196612
  28.1 11.6 %copy-start.13 = (f32[32,32]{1,0:T(8,128)S(1)}, f32[32,32]{1,0:T(8,128)}, u32[]{:S(2)}) copy-start(f32[32,32]{1,0:T(8,128)} %constant.24.clone.r_16_) | copy-start | bytes 12292
  28.5 11.2 %copy-start.10 = (bf16[64,192]{1,0:T(8,128)(2,1)S(1)}, bf16[64,192]{1,0:T(8,128)(2,1)}, u32[]{:S(2)}) copy-start(bf16[64,192]{1,0:T(8,128)(2,1)} %constant.23.clone.exw.r_12_) | copy-start | bytes 73732
  28.5 5.0 %collective-permute-start.12 = (f32[8,128]{1,0:T(8,128)S(1)}, f32[8,128]{1,0:T(8,128)S(1)}, u32[]{:S(2)}, u32[]{:S(2)}) collective-permute-start(f32[8,128]{1,0:T(8,128)S(1)} %get-tuple-element.33), channel_id=1, source_target_pairs={{0,12},{4,0},{8,4},{12,8},{1,13},{5,1},{9,5},{13,9},{2,14},{6,2},{... | collective-permute-start | bytes 12296 | tf_op jit(solution)/shard_map/ppermute | solution.py:419
  30.0 4.5 %collective-permute-start.11 = (f32[8,128]{1,0:T(8,128)S(1)}, f32[8,128]{1,0:T(8,128)S(1)}, u32[]{:S(2)}, u32[]{:S(2)}) collective-permute-start(f32[8,128]{1,0:T(8,128)S(1)} %get-tuple-element.33), channel_id=1, source_target_pairs={{0,8},{4,12},{8,0},{12,4},{1,9},{5,13},{9,1},{13,5},{2,10},{6,14},... | collective-permute-start | bytes 12296 | tf_op jit(solution)/shard_map/ppermute | solution.py:419
  30.0 5.4 %collective-permute-start.10 = (f32[8,128]{1,0:T(8,128)S(1)}, f32[8,128]{1,0:T(8,128)S(1)}, u32[]{:S(2)}, u32[]{:S(2)}) collective-permute-start(f32[8,128]{1,0:T(8,128)S(1)} %get-tuple-element.33), channel_id=1, source_target_pairs={{0,4},{4,8},{8,12},{12,0},{1,5},{5,9},{9,13},{13,1},{2,6},{6,10},{... | collective-permute-start | bytes 12296 | tf_op jit(solution)/shard_map/ppermute | solution.py:419
  30.6 9.0 %collective-permute-start.9 = (f32[24,128]{1,0:T(8,128)S(1)}, f32[24,128]{1,0:T(8,128)S(1)}, u32[]{:S(2)}, u32[]{:S(2)}) collective-permute-start(f32[24,128]{1,0:T(8,128)S(1)} %get-tuple-element.32), channel_id=1, source_target_pairs={{0,1},{1,2},{2,3},{3,0},{4,5},{5,6},{6,7},{7,4},{8,9},{9,10},{10,1... | collective-permute-start | bytes 36872 | tf_op jit(solution)/shard_map/ppermute | solution.py:419
  30.6 9.0 %collective-permute-start.8 = (f32[40,128]{1,0:T(8,128)S(1)}, f32[40,128]{1,0:T(8,128)S(1)}, u32[]{:S(2)}, u32[]{:S(2)}) collective-permute-start(f32[40,128]{1,0:T(8,128)S(1)} %get-tuple-element.31), channel_id=1, source_target_pairs={{0,4},{4,8},{8,12},{12,0},{1,5},{5,9},{9,13},{13,1},{2,6},{6,10},{... | collective-permute-start | bytes 61448 | tf_op jit(solution)/shard_map/ppermute | solution.py:419
  35.4 1.4 %collective-permute-start.15 = (f32[8,128]{1,0:T(8,128)S(1)}, f32[8,128]{1,0:T(8,128)S(1)}, u32[]{:S(2)}, u32[]{:S(2)}) collective-permute-start(f32[8,128]{1,0:T(8,128)S(1)} %add_add_fusion.r_7_), channel_id=1, source_target_pairs={{0,3},{1,0},{2,1},{3,2},{4,7},{5,4},{6,5},{7,6},{8,11},{9,8},{10,9... | collective-permute-start | bytes 12296 | tf_op jit(solution)/shard_map/ppermute | solution.py:419
  35.4 3.7 %collective-permute-start.14 = (f32[8,128]{1,0:T(8,128)S(1)}, f32[8,128]{1,0:T(8,128)S(1)}, u32[]{:S(2)}, u32[]{:S(2)}) collective-permute-start(f32[8,128]{1,0:T(8,128)S(1)} %add_add_fusion.r_7_), channel_id=1, source_target_pairs={{0,2},{1,3},{2,0},{3,1},{4,6},{5,7},{6,4},{7,5},{8,10},{9,11},{10,... | collective-permute-start | bytes 12296 | tf_op jit(solution)/shard_map/ppermute | solution.py:419
  36.6 3.0 %collective-permute-start.13 = (f32[8,128]{1,0:T(8,128)S(1)}, f32[8,128]{1,0:T(8,128)S(1)}, u32[]{:S(2)}, u32[]{:S(2)}) collective-permute-start(f32[8,128]{1,0:T(8,128)S(1)} %add_add_fusion.r_7_), channel_id=1, source_target_pairs={{0,1},{1,2},{2,3},{3,0},{4,5},{5,6},{6,7},{7,4},{8,9},{9,10},{10,1... | collective-permute-start | bytes 12296 | tf_op jit(solution)/shard_map/ppermute | solution.py:419
where the time goes:
time: 44.3 us; the launch traced here: 43.9 us
  starting transfers between devices  14.6 us (33%)
  waiting for transfers between devices  14.5 us (33%)
  Pallas kernels  7.55 us (17%)
  local copies, waits for them, and re-layouts  6.43 us (15%)
  between operations  0.75 us (2%)
    ppermute x16, starting transfers between devices, shifted(): return lax.ppermute(value, axis, [(i, (i + by) % n) for i in range(n)])  14.6 us
    ppermute x16, waiting for transfers between devices, shifted(): return lax.ppermute(value, axis, [(i, (i + by) % n) for i in range(n)])  14.5 us
    unnamed x32, local copies, waits for them, and re-layouts  6.43 us
    pallas_call x1, Pallas kernels, on_device(): call(lambda *r: back_kernel(depth, len(parts), *r), [block, block], [block])  4.21 us
    pallas_call x1, Pallas kernels, on_device(): call(front_kernel, [block] + msgs, [block, (depth, 8, height), (depth, 8,...  2.49 us
  transfers between devices with their start and end apart: 16, of which 10 were waited for; matrix products, arithmetic and copies ran while one was open for 0% of the time, Pallas kernels for 0%

commit v1 on v0

--- a/solution.py
+++ b/solution.py
@@ -206,26 +206,34 @@
     return plus + minus, plus - minus
 
 
-def with_tail(body, tails):
+def with_tail(body, tails, size=8):
     width = body.shape[1]
-    rows = list(tails) + [jnp.zeros((8 - len(tails), width), F32)]
+    rows = list(tails) + [jnp.zeros((size - len(tails), width), F32)]
     return jnp.concatenate([body, jnp.concatenate(rows, 0)], 0)
 
 
-def front_kernel(charge, surf, eyw, exw, inv, sx0, sy0, base, px, nx, py, ny, work, part, first):
+def front_kernel(charge_h, surf_h, eyw_h, exw_h, inv_h, sx0_h, sy0_h, base, px, nx, py, ny,
+                 charge, surf, eyw, exw, inv, sx0, sy0, work, part, first, sems):
     depth, width, height = charge.shape
     scale = np.sqrt(2.0 / depth)
-
-    def columns(i, carry):
-        at = pl.ds(pl.multiple_of(i * 8, 8), 8)
+    tiles = width // 8
+    pairs = [(surf_h, surf)]
+    pairs += [(charge_h.at[:, 8 * i:8 * i + 8, :], charge.at[:, 8 * i:8 * i + 8, :]) for i in range(tiles)]
+    pairs += [(eyw_h, eyw), (exw_h, exw), (sx0_h, sx0), (sy0_h, sy0), (inv_h, inv)]
+    copies = [pltpu.make_async_copy(src, dst, sems.at[i]) for i, (src, dst) in enumerate(pairs)]
+    for copy in copies:
+        copy.start()
+    copies[0].wait()
+    for i in range(tiles):
+        copies[1 + i].wait()
+        at = slice(8 * i, 8 * i + 8)
         xs = [charge[z, at, :] for z in range(depth)]
         xs[0] = xs[0] + surf[0, at, :]
         xs[-1] = xs[-1] + surf[1, at, :]
         for k, value in enumerate(cosine_fwd(xs, scale)):
             work[k, at, :] = value
-        return carry
-
-    lax.fori_loop(0, width // 8, columns, 0)
+    for copy in copies[1 + tiles:]:
+        copy.wait()
     step = 4
     for c in range(0, depth, step):
         block = work[c:c + step].reshape(step * width, height)
@@ -346,14 +354,79 @@
         moments[...] = jnp.concatenate([dot(v0, v0), dot(v0, v1), dot(v1, v1), m3, jnp.zeros((4, 128), F32)], 0)
 
 
-def back_kernel(depth, n_moments, *refs):
-    base, s0, s1, px, py, from_px, from_py = refs[:7]
-    moms = refs[7:7 + n_moments]
-    eyw, exw, inv, sx0, sy0, cz, czt = refs[7 + n_moments:14 + n_moments]
-    potential, residual, work = refs[14 + n_moments:]
-    _, width, height = base.shape
-    rows, cols = px.shape[0] - 8, width
+def cells_from(out, work, spectrum, exw, eyw):
+    depth, width, height = work.shape
+    for c in range(0, depth, 2):
+        pair = sx_times(exw, jnp.concatenate([spectrum(c), spectrum(c + 1)], 1))
+        work[c] = pair[:, :height]
+        work[c + 1] = pair[:, height:]
+    step = 4
+    for c in range(0, depth, step):
+        block = work[c:c + step].reshape(step * width, height)
+        work[c:c + step] = times_sy(block, eyw).reshape(step, width, height)
+    scale = np.sqrt(2.0 / depth)
+    for i in range(width // 8):
+        at = slice(8 * i, 8 * i + 8)
+        for z, value in enumerate(cosine_back([work[k, at, :] for k in range(depth)], scale)):
+            out[z, at, :] = value
+
+
+def base_kernel(base, eyw, exw, out, work):
+    cells_from(out, work, lambda k: base[k], exw[...], eyw[...])
+
+
+def extend_kernel(state, eyw, exw, inv, sx0, sy0, out, work):
+    depth, width, height = work.shape
+    rows = height * depth // 128
+    row, row_n, col, col_n, c00 = unpacked_state(state, rows, width)[:5]
+    at_zero = (lax.broadcasted_iota(jnp.int32, row.shape, 0) == 0) & (lane_id(row.shape) < depth)
+    row_p = rows_back(row + row_n, depth)
+    row_m = rows_back(row - row_n, depth)
+    row_full = rows_back(jnp.where(at_zero, c00, row), depth)
+    odd = lax.broadcasted_iota(jnp.int32, (8, height), 0) % 2 == 1
+    top = lax.broadcasted_iota(jnp.int32, (width, height), 0) == 0
+    lane0 = lane_id((width, height)) == 0
+
+    def spectrum(k):
+        pick = jnp.where(odd, row_p[k:k + 1], row_m[k:k + 1])
+        pick = jnp.broadcast_to(pick[None], (width // 8, 8, height)).reshape(width, height)
+        rim = sx0[...] * pick + col[:, k:k + 1] * sy0[2:3, :] + col_n[:, k:k + 1] * sy0[3:4, :]
+        return jnp.where(top, row_full[k:k + 1], jnp.where(lane0, 1.0, inv[k]) * rim)
+
+    cells_from(out, work, spectrum, exw[...], eyw[...])
+
+
+def rims_kernel(depth, s0, s1, px, py, from_px, from_py, eyw, exw, cz, czt, out_rows, out_cols):
     packed = py.shape[0] - 8
+    rows = px.shape[0] - 8
+    width = packed * 128 // depth
+    v0 = unpacked_state(s0, rows, width)
+    v1 = unpacked_state(s1, rows, width)
+    v2 = (
+        px[:rows, :] + from_px[:rows, :], None,
+        unpack(py[:packed, :] + from_py[:packed, :], depth), None,
+        px[rows:rows + 1, :] + from_px[rows:rows + 1, :] + from_py[packed:packed + 1, :],
+    )
+    at_zero = (lax.broadcasted_iota(jnp.int32, (rows, 128), 0) == 0) & (lane_id((rows, 128)) < depth)
+    lines = [rows_back(jnp.where(at_zero, v[4], v[0]), depth) for v in (v0, v1, v2)]
+    high = lax.Precision.HIGHEST
+    lines = times_sy(jnp.concatenate(lines, 0), eyw[...])
+    lines = jnp.concatenate([lines[i * depth:(i + 1) * depth] for i in range(3)], 1)
+    lines = jnp.dot(cz[...], lines, precision=high, preferred_element_type=F32)
+    for i in range(3):
+        out_rows[i] = lines[:, i * 128:(i + 1) * 128]
+    sides = sx_times(exw[...], jnp.concatenate([v[2] for v in (v0, v1, v2)], 1))
+    sides = jnp.concatenate([sides[:, i * 128:(i + 1) * 128] for i in range(3)], 0)
+    sides = jnp.dot(sides, czt[...], precision=high, preferred_element_type=F32)
+    for i in range(3):
+        out_cols[i] = sides[i * width:(i + 1) * width]
+
+
+def final_kernel(n_moments, *refs):
+    cells_b, cells_0, cells_1, in_rows, in_cols = refs[:5]
+    moms = refs[5:5 + n_moments]
+    potential_h, residual_h, potential, residual, sems = refs[5 + n_moments:]
+    depth, width, height = cells_b.shape
     m = moms[0][...]
     for other in moms[1:]:
         m = m + other[...]
@@ -365,53 +438,26 @@
     safe = jnp.where(fine, det, 1.0)
     c0 = jnp.where(fine, (n3 - n1 * n2) / safe, 1.0 / n1)
     c1 = jnp.where(fine, (n1 * n1 - n2) / safe, 0.0)
-    v0 = unpacked_state(s0, rows, cols)
-    v1 = unpacked_state(s1, rows, cols)
-    row, row_n, col, col_n, c00 = (c0 * v0[i] + c1 * v1[i] for i in range(5))
-    row2 = px[:rows, :] + from_px[:rows, :]
-    col2 = unpack(py[:packed, :] + from_py[:packed, :], depth)
-    c2 = px[rows:rows + 1, :] + from_px[rows:rows + 1, :] + from_py[packed:packed + 1, :]
-    res_row = v0[0] - c0 * v1[0] - c1 * row2
-    res_col = v0[2] - c0 * v1[2] - c1 * col2
-    res_c = v0[4] - c0 * v1[4] - c1 * c2
-    at_zero = (lax.broadcasted_iota(jnp.int32, row.shape, 0) == 0) & (lane_id(row.shape) < depth)
-    row_p = rows_back(row + row_n, depth)
-    row_m = rows_back(row - row_n, depth)
-    row_full = rows_back(jnp.where(at_zero, c00, row), depth)
-    res_row = rows_back(jnp.where(at_zero, res_c, res_row), depth)
-    odd = lax.broadcasted_iota(jnp.int32, (8, height), 0) % 2 == 1
+    rim_row = in_rows[0] - c0 * in_rows[1] - c1 * in_rows[2]
+    rim_col = in_cols[0] - c0 * in_cols[1] - c1 * in_cols[2]
     top = lax.broadcasted_iota(jnp.int32, (width, height), 0) == 0
     lane0 = lane_id((width, height)) == 0
-    for c in range(0, depth, 2):
-        pieces = []
-        for k in (c, c + 1):
-            pick = jnp.where(odd, row_p[k:k + 1], row_m[k:k + 1])
-            pick = jnp.broadcast_to(pick[None], (width // 8, 8, height)).reshape(width, height)
-            rim = sx0[...] * pick + col[:, k:k + 1] * sy0[2:3, :] + col_n[:, k:k + 1] * sy0[3:4, :]
-            weight = jnp.where(lane0, 1.0, inv[k])
-            pieces.append(jnp.where(top, row_full[k:k + 1], base[k] + weight * rim))
-        pair = sx_times(exw[...], jnp.concatenate(pieces, 1))
-        work[c] = pair[:, :height]
-        work[c + 1] = pair[:, height:]
-    step = 4
+    step = depth // 4
+    copies = []
     for c in range(0, depth, step):
-        block = work[c:c + step].reshape(step * width, height)
-        work[c:c + step] = times_sy(block, eyw[...]).reshape(step, width, height)
-    scale = np.sqrt(2.0 / depth)
-
-    def columns(i, carry):
-        at = pl.ds(pl.multiple_of(i * 8, 8), 8)
-        for z, value in enumerate(cosine_back([work[k, at, :] for k in range(depth)], scale)):
-            potential[z, at, :] = value
-        return carry
-
-    lax.fori_loop(0, width // 8, columns, 0)
-    high = lax.Precision.HIGHEST
-    rim_row = jnp.dot(cz[...], times_sy(res_row, eyw[...]), precision=high, preferred_element_type=F32)
-    res_col = sx_times(exw[...], res_col)
-    rim_col = jnp.dot(res_col, czt[...], precision=high, preferred_element_type=F32)
-    for z in range(depth):
-        residual[z] = jnp.where(top, rim_row[z:z + 1], jnp.where(lane0, rim_col[:, z:z + 1], 0.0))
+        for z in range(c, c + step):
+            potential[z] = cells_b[z] + c0 * cells_0[z] + c1 * cells_1[z]
+        copies.append((potential.at[c:c + step], potential_h.at[c:c + step]))
+        copies[-1] = pltpu.make_async_copy(*copies[-1], sems.at[len(copies) - 1])
+        copies[-1].start()
+    for c in range(0, depth, step):
+        for z in range(c, c + step):
+            residual[z] = jnp.where(top, rim_row[z:z + 1], jnp.where(lane0, rim_col[:, z:z + 1], 0.0))
+        copies.append((residual.at[c:c + step], residual_h.at[c:c + step]))
+        copies[-1] = pltpu.make_async_copy(*copies[-1], sems.at[len(copies) - 1])
+        copies[-1].start()
+    for copy in copies:
+        copy.wait()
 
 
 def shifted(value, axis, by):
@@ -420,7 +466,11 @@
 
 
 def exchange(px, nx, py, ny):
-    return (shifted(px, "gx", -1), shifted(nx, "gx", 1), shifted(py, "gy", -1), shifted(ny, "gy", 1))
+    from_py = shifted(ny, "gy", 1)
+    from_ny = shifted(py, "gy", -1)
+    from_px = shifted(nx, "gx", 1)
+    from_nx = shifted(px, "gx", -1)
+    return from_nx, from_px, from_ny, from_py
 
 
 def pieces_over(value, axis):
@@ -434,12 +484,18 @@
         value = sum(parts[1:], parts[0])
 
 
-def call(kernel, outs, scratch):
+def call(kernel, outs, scratch, in_specs=None, out_specs=None):
+    specs = {}
+    if in_specs is not None:
+        specs["in_specs"] = in_specs
+    if out_specs is not None:
+        specs["out_specs"] = out_specs
     return pl.pallas_call(
         kernel,
         out_shape=[jax.ShapeDtypeStruct(shape, F32) for shape in outs],
-        scratch_shapes=[pltpu.VMEM(shape, F32) for shape in scratch],
+        scratch_shapes=[pltpu.VMEM(s, F32) if isinstance(s, tuple) else s for s in scratch],
         compiler_params=pltpu.CompilerParams(vmem_limit_bytes=48 * 1024 * 1024),
+        **specs,
     )
 
 
@@ -450,24 +506,42 @@
     msgs = [(rows + 8, 128)] * 2 + [(packed + 8, 128)] * 2
     state = (2 * rows + 2 * width + 8, 128)
     block = (depth, width, height)
-    base, *own = call(front_kernel, [block] + msgs, [block, (depth, 8, height), (depth, 8, height)])(
-        charge, surface_charge, tab["eyw"], tab["exw"], tab["inv"], tab["sx0"], tab["sy0"]
-    )
+    anywhere = pl.BlockSpec(memory_space=pltpu.HBM)
+    whole = pl.BlockSpec(memory_space=pltpu.VMEM)
+    fronts = (charge, surface_charge) + tuple(tab[n] for n in ("eyw", "exw", "inv", "sx0", "sy0"))
+    landing = [pltpu.VMEM(x.shape, x.dtype) for x in fronts]
+    fronts = [pltpu.with_memory_space_constraint(x, pltpu.HBM) for x in fronts]
+    base, *own = call(
+        front_kernel, [block] + msgs,
+        landing + [block, (depth, 8, height), (depth, 8, height), pltpu.SemaphoreType.DMA((6 + width // 8,))],
+        in_specs=[anywhere] * 7,
+    )(*fronts)
     got = exchange(*own)
+    cells_b = call(base_kernel, [block], [block])(base, tab["eyw"], tab["exw"])[0]
+    *got, cells_b = lax.optimization_barrier((*got, cells_b))
     tables = (tab["inv2"], tab["rowt"], tab["colt"], tab["crnt"])
     scratch = [(rows, 8, 128), (rows, 128), (rows, 128)]
     s0, *own = call(lambda *r: schur_kernel(depth, False, *r), [state] + msgs, scratch)(*own, *got, *tables)
     got = exchange(*own)
+    extend = call(extend_kernel, [block], [block])
+    backs = tuple(tab[n] for n in ("eyw", "exw", "inv", "sx0", "sy0"))
+    cells_0 = extend(s0, *backs)[0]
+    *got, cells_0 = lax.optimization_barrier((*got, cells_0))
     s1, px, nx, py, ny, moments = call(
         lambda *r: schur_kernel(depth, True, *r), [state] + msgs + [(8, 128)], scratch
     )(*own, *got, *tables, s0)
     parts = pieces_over(moments, "gx")
-    from_px, from_py = shifted(nx, "gx", 1), shifted(ny, "gy", 1)
+    from_py, from_px = shifted(ny, "gy", 1), shifted(nx, "gx", 1)
+    cells_1 = extend(s1, *backs)[0]
+    *parts, cells_1 = lax.optimization_barrier((*parts, cells_1))
     parts = pieces_over(sum(parts[1:], parts[0]), "gy")
-    return call(lambda *r: back_kernel(depth, len(parts), *r), [block, block], [block])(
-        base, s0, s1, px, py, from_px, from_py, *parts,
-        tab["eyw"], tab["exw"], tab["inv"], tab["sx0"], tab["sy0"], tab["cz"], tab["czt"],
+    rim = call(lambda *r: rims_kernel(depth, *r), [(3, depth, height), (3, width, 128)], [])(
+        s0, s1, px, py, from_px, from_py, tab["eyw"], tab["exw"], tab["cz"], tab["czt"]
     )
+    return call(
+        lambda *r: final_kernel(len(parts), *r), [block, block], [block, block, pltpu.SemaphoreType.DMA((8,))],
+        in_specs=[whole] * (5 + len(parts)), out_specs=[anywhere, anywhere],
+    )(cells_b, cells_0, cells_1, *rim, *parts)
 
 
 def solution(mesh):

time: 44.3 us -> 37.9 us (0.86)
  local copies, waits for them, and re-layouts: 6.43 us -> 0.07 us
  waiting for transfers between devices: 14.5 us -> 8.23 us
  Pallas kernels: 7.55 us -> 12.7 us
  starting transfers between devices: 14.6 us -> 15.9 us
    unnamed x32 -> x22, local copies, waits for them, and re-layouts: 6.43 us -> 0.07 us
    ppermute x16, waiting for transfers between devices: 14.5 us -> 8.23 us  [shifted(): return lax.ppermute(value, axis, [(i, (i + by) % n) for i in range(n)])]
    pallas_call x2 -> x6, Pallas kernels: 6.7 us -> 11.8 us  [the longest x1 3.64 us: on_device(): call(front_kernel, [block] + msgs, landing + [block, (depth, 8, height),...]
    ppermute x16, starting transfers between devices: 14.6 us -> 15.9 us  [shifted(): return lax.ppermute(value, axis, [(i, (i + by) % n) for i in range(n)])]
  transfers between devices with their start and end apart: 16 -> 16, of which waited for: 10 -> 6; matrix products, arithmetic and copies ran while one was open for 0% -> 0% of each run, Pallas kernels for 0% -> 18%
where the time goes in v1:
time: 37.9 us; the launch traced here: 37.8 us
  starting transfers between devices  15.9 us (42%)
  Pallas kernels  12.7 us (34%)
  waiting for transfers between devices  8.23 us (22%)
  between operations  0.86 us (2%)
    ppermute x16, starting transfers between devices, shifted(): return lax.ppermute(value, axis, [(i, (i + by) % n) for i in range(n)])  15.9 us
    ppermute x16, waiting for transfers between devices, shifted(): return lax.ppermute(value, axis, [(i, (i + by) % n) for i in range(n)])  8.23 us
    pallas_call x1, Pallas kernels, on_device(): call(front_kernel, [block] + msgs, landing + [block, (depth, 8, height),...  3.64 us
    pallas_call x1, Pallas kernels, on_device(): cells_0 = extend(s0, *backs)[0]  2.27 us
    pallas_call x1, Pallas kernels, on_device(): cells_1 = extend(s1, *backs)[0]  2.26 us
    pallas_call x1, Pallas kernels, on_device(): call(lambda *r: final_kernel(len(parts), *r), [block, block], [block, blo...  1.53 us
    pallas_call x1, Pallas kernels, on_device(): call(base_kernel, [block], [block])(base, tab['eyw'], tab['exw'])[0]  1.48 us
  transfers between devices with their start and end apart: 16, of which 6 were waited for; matrix products, arithmetic and copies ran while one was open for 0% of the time, Pallas kernels for 18%

profile of v1, /device:TPU:0, one launch (start us, length us, event | category | flops | bytes accessed | tf_op | source)
XLA Modules:
  0.0 37.8 jit_solution(5247669273877472943)
XLA Ops:
  0.6 0.0 copy-start.2
  0.6 0.0 copy-start.3
  0.7 3.6 %shard_map.140 = (f32[32,64,128]{2,1,0:T(8,128)S(1)}, f32[40,128]{1,0:T(8,128)S(1)}, f32[40,128]{1,0:T(8,128)S(1)}, f32[24,128]{1,0:T(8,128)S(1)}, f32[24,128]{1,0:T(8,128)S(1)}) custom-call(f32[32,64,128]{2,1,0:T(8,128)} %charge_h.1, f32[2,64,128]{2,1,0:T(8,128)} %surf_h.1, bf16[256,256]{1,0:T(8,128)(2,1)} %constant.22.clone.eyw_h.eyw.r_6_, ...), custom_call_target="tpu_custom_call" | custom-call | tf_op jit(solution)/shard_map/pallas_call | solution.py:514
  4.3 5.1 %collective-permute-start = (f32[40,128]{1,0:T(8,128)S(1)}, f32[40,128]{1,0:T(8,128)S(1)}, u32[]{:S(2)}, u32[]{:S(2)}) collective-permute-start(f32[40,128]{1,0:T(8,128)S(1)} %get-tuple-element.35.r_0_), channel_id=1, source_target_pairs={{0,12},{4,0},{8,4},{12,8},{1,13},{5,1},{9,5},{13,9},{2,14},{6,2},{... | collective-permute-start | bytes 61448 | tf_op jit(solution)/shard_map/ppermute | solution.py:465
  9.4 0.0 collective-permute-start.1
  9.4 0.6 %collective-permute-start.2 = (f32[24,128]{1,0:T(8,128)S(1)}, f32[24,128]{1,0:T(8,128)S(1)}, u32[]{:S(2)}, u32[]{:S(2)}) collective-permute-start(f32[24,128]{1,0:T(8,128)S(1)} %get-tuple-element.37.r_2_), channel_id=1, source_target_pairs={{0,3},{1,0},{2,1},{3,2},{4,7},{5,4},{6,5},{7,6},{8,11},{9,8},{10,9... | collective-permute-start | bytes 36872 | tf_op jit(solution)/shard_map/ppermute | solution.py:465
  10.1 0.0 collective-permute-start.3
  10.1 0.0 copy-start.1
  10.1 0.0 copy-start.4
  10.1 0.0 copy-start.5
  10.1 0.0 copy-start.9
  10.1 1.5 %shard_map.141.r_0_ = f32[32,64,128]{2,1,0:T(8,128)S(1)} custom-call(f32[32,64,128]{2,1,0:T(8,128)S(1)} %get-tuple-element.39.base, bf16[256,256]{1,0:T(8,128)(2,1)S(1)} %copy-done.2, bf16[64,192]{1,0:T(8,128)(2,1)S(1)} %copy-done.3), custom_call_target="tpu_custom_call" | custom-call | tf_op jit(solution)/shard_map/pallas_call | solution.py:520
  11.6 0.0 copy-start
  11.6 0.0 copy-start.6
  11.6 0.0 collective-permute-done.2.r_6_
  11.7 1.5 %collective-permute-done.3.r_7_ = f32[24,128]{1,0:T(8,128)S(1)} collective-permute-done((f32[24,128]{1,0:T(8,128)S(1)}, f32[24,128]{1,0:T(8,128)S(1)}, u32[]{:S(2)}, u32[]{:S(2)}) %collective-permute-start.3) | collective-permute-done | bytes 12320 | tf_op jit(solution)/shard_map/ppermute | solution.py:465
  13.2 0.0 collective-permute-done.r_4_
  13.2 1.8 %collective-permute-done.1.r_5_ = f32[40,128]{1,0:T(8,128)S(1)} collective-permute-done((f32[40,128]{1,0:T(8,128)S(1)}, f32[40,128]{1,0:T(8,128)S(1)}, u32[]{:S(2)}, u32[]{:S(2)}) %collective-permute-start.1) | collective-permute-done | bytes 20512 | tf_op jit(solution)/shard_map/ppermute | solution.py:465
  15.0 0.4 %shard_map.142 = (f32[200,128]{1,0:T(8,128)S(1)}, f32[40,128]{1,0:T(8,128)S(1)}, f32[40,128]{1,0:T(8,128)S(1)}, f32[24,128]{1,0:T(8,128)S(1)}, f32[24,128]{1,0:T(8,128)S(1)}) custom-call(f32[40,128]{1,0:T(8,128)S(1)} %get-tuple-element.35.r_0_, f32[40,128]{1,0:T(8,128)S(1)} %get-tuple-element.36.r_1_, f32[24,128]{1,0:T(8,128)S(1)} %get-tuple-element.37.r_2_, ...), custom_call_target="tpu_custom_call" | custom-call | tf_op jit(solution)/shard_map/pallas_call | solution.py:524
  15.4 0.0 copy-start.8
  15.5 1.8 %collective-permute-start.4 = (f32[40,128]{1,0:T(8,128)S(1)}, f32[40,128]{1,0:T(8,128)S(1)}, u32[]{:S(2)}, u32[]{:S(2)}) collective-permute-start(f32[40,128]{1,0:T(8,128)S(1)} %get-tuple-element.45.r_0_), channel_id=1, source_target_pairs={{0,12},{4,0},{8,4},{12,8},{1,13},{5,1},{9,5},{13,9},{2,14},{6,2},{... | collective-permute-start | bytes 61448 | tf_op jit(solution)/shard_map/ppermute | solution.py:465
  17.3 0.3 collective-permute-start.5
  17.5 0.0 collective-permute-start.6
  17.5 0.5 %collective-permute-start.7 = (f32[24,128]{1,0:T(8,128)S(1)}, f32[24,128]{1,0:T(8,128)S(1)}, u32[]{:S(2)}, u32[]{:S(2)}) collective-permute-start(f32[24,128]{1,0:T(8,128)S(1)} %get-tuple-element.48.r_3_), channel_id=1, source_target_pairs={{0,1},{1,2},{2,3},{3,0},{4,5},{5,6},{6,7},{7,4},{8,9},{9,10},{10,1... | collective-permute-start | bytes 36872 | tf_op jit(solution)/shard_map/ppermute | solution.py:465
  18.1 2.3 %shard_map.143.r_1_ = f32[32,64,128]{2,1,0:T(8,128)S(1)} custom-call(f32[200,128]{1,0:T(8,128)S(1)} %get-tuple-element.49.state.r_12_.r_0_, bf16[256,256]{1,0:T(8,128)(2,1)S(1)} %copy-done.2, bf16[64,192]{1,0:T(8,128)(2,1)S(1)} %copy-done.3, f32[32,64,128]{2,1,0:T(8,128)S(1)} %copy-done, f32[64,128]{1,0:T(8,128)S(1)} %copy-done.6, f32[8,128]{1,0:T(8,128)S(1)} %copy-done.8), custom_call_target="tpu_custom_call" | custom-call | tf_op jit(solution)/shard_map/pallas_call | solution.py:528
  20.3 0.0 collective-permute-done.6.r_6_
  20.3 0.3 collective-permute-done.7.r_7_
  20.7 0.0 collective-permute-done.4.r_4_
  20.7 2.2 %collective-permute-done.5.r_5_ = f32[40,128]{1,0:T(8,128)S(1)} collective-permute-done((f32[40,128]{1,0:T(8,128)S(1)}, f32[40,128]{1,0:T(8,128)S(1)}, u32[]{:S(2)}, u32[]{:S(2)}) %collective-permute-start.5) | collective-permute-done | bytes 20512 | tf_op jit(solution)/shard_map/ppermute | solution.py:465
  22.8 0.5 %shard_map.144 = (f32[200,128]{1,0:T(8,128)S(1)}, f32[40,128]{1,0:T(8,128)S(1)}, f32[40,128]{1,0:T(8,128)S(1)}, f32[24,128]{1,0:T(8,128)S(1)}, f32[24,128]{1,0:T(8,128)S(1)}, /*index=5*/f32[8,128]{1,0:T(8,128)S(1)}) custom-call(f32[40,128]{1,0:T(8,128)S(1)} %get-tuple-element.45.r_0_, f32[40,128]{1,0:T(8,128)S(1)} %get-tuple-element.46.r_1_, ...), custom_call_target="tpu_custom_call" | custom-call | tf_op jit(solution)/shard_map/pallas_call | solution.py:530
  23.3 1.4 %collective-permute-start.10 = (f32[8,128]{1,0:T(8,128)S(1)}, f32[8,128]{1,0:T(8,128)S(1)}, u32[]{:S(2)}, u32[]{:S(2)}) collective-permute-start(f32[8,128]{1,0:T(8,128)S(1)} %get-tuple-element.64), channel_id=1, source_target_pairs={{0,12},{4,0},{8,4},{12,8},{1,13},{5,1},{9,5},{13,9},{2,14},{6,2},{... | collective-permute-start | bytes 12296 | tf_op jit(solution)/shard_map/ppermute | solution.py:465
  24.7 0.0 collective-permute-start.9
  24.7 0.7 %collective-permute-start.8 = (f32[8,128]{1,0:T(8,128)S(1)}, f32[8,128]{1,0:T(8,128)S(1)}, u32[]{:S(2)}, u32[]{:S(2)}) collective-permute-start(f32[8,128]{1,0:T(8,128)S(1)} %get-tuple-element.64), channel_id=1, source_target_pairs={{0,4},{4,8},{8,12},{12,0},{1,5},{5,9},{9,13},{13,1},{2,6},{6,10},{... | collective-permute-start | bytes 12296 | tf_op jit(solution)/shard_map/ppermute | solution.py:465
  25.4 0.0 collective-permute-start.12
  25.4 2.8 %collective-permute-start.11 = (f32[40,128]{1,0:T(8,128)S(1)}, f32[40,128]{1,0:T(8,128)S(1)}, u32[]{:S(2)}, u32[]{:S(2)}) collective-permute-start(f32[40,128]{1,0:T(8,128)S(1)} %get-tuple-element.60), channel_id=1, source_target_pairs={{0,4},{4,8},{8,12},{12,0},{1,5},{5,9},{9,13},{13,1},{2,6},{6,10},{... | collective-permute-start | bytes 61448 | tf_op jit(solution)/shard_map/ppermute | solution.py:465
  28.2 2.3 %shard_map.145.r_2_ = f32[32,64,128]{2,1,0:T(8,128)S(1)} custom-call(f32[200,128]{1,0:T(8,128)S(1)} %get-tuple-element.56.state.r_1_, bf16[256,256]{1,0:T(8,128)(2,1)S(1)} %copy-done.2, bf16[64,192]{1,0:T(8,128)(2,1)S(1)} %copy-done.3, f32[32,64,128]{2,1,0:T(8,128)S(1)} %copy-done, f32[64,128]{1,0:T(8,128)S(1)} %copy-done.6, f32[8,128]{1,0:T(8,128)S(1)} %copy-done.8), custom_call_target="tpu_custom_call" | custom-call | tf_op jit(solution)/shard_map/pallas_call | solution.py:535
  30.5 0.0 copy-start.10
  30.5 0.0 collective-permute-done.8
  30.6 1.5 %collective-permute-start.15 = (f32[8,128]{1,0:T(8,128)S(1)}, f32[8,128]{1,0:T(8,128)S(1)}, u32[]{:S(2)}, u32[]{:S(2)}) collective-permute-start(f32[8,128]{1,0:T(8,128)S(1)} %add_add_fusion.r_5_), channel_id=1, source_target_pairs={{0,3},{1,0},{2,1},{3,2},{4,7},{5,4},{6,5},{7,6},{8,11},{9,8},{10,9... | collective-permute-start | bytes 12296 | tf_op jit(solution)/shard_map/ppermute | solution.py:465
  32.1 1.1 %collective-permute-start.14 = (f32[8,128]{1,0:T(8,128)S(1)}, f32[8,128]{1,0:T(8,128)S(1)}, u32[]{:S(2)}, u32[]{:S(2)}) collective-permute-start(f32[8,128]{1,0:T(8,128)S(1)} %add_add_fusion.r_5_), channel_id=1, source_target_pairs={{0,2},{1,3},{2,0},{3,1},{4,6},{5,7},{6,4},{7,5},{8,10},{9,11},{10,... | collective-permute-start | bytes 12296 | tf_op jit(solution)/shard_map/ppermute | solution.py:465
  33.2 0.0 collective-permute-start.13
  33.2 0.0 collective-permute-done.12.r_5_
  33.2 0.0 collective-permute-done.11.r_4_
  33.2 0.6 %shard_map.146 = (f32[3,32,128]{2,1,0:T(8,128)S(1)}, f32[3,64,128]{2,1,0:T(8,128)S(1)}) custom-call(f32[200,128]{1,0:T(8,128)S(1)} %get-tuple-element.49.state.r_12_.r_0_, f32[200,128]{1,0:T(8,128)S(1)} %get-tuple-element.56.state.r_1_, f32[40,128]{1,0:T(8,128)S(1)} %get-tuple-element.58.r_2_, f32[24,128]{1,0:T(8,128)S(1)} %get-tuple-element.59.r_3_, ...), custom_call_target="tpu_custom_call" | custom-call | tf_op jit(solution)/shard_map/pallas_call | solution.py:538
  33.9 0.0 collective-permute-done.15.r_8_
  33.9 1.8 %collective-permute-done.14.r_7_ = f32[8,128]{1,0:T(8,128)S(1)} collective-permute-done((f32[8,128]{1,0:T(8,128)S(1)}, f32[8,128]{1,0:T(8,128)S(1)}, u32[]{:S(2)}, u32[]{:S(2)}) %collective-permute-start.14) | collective-permute-done | bytes 4128 | tf_op jit(solution)/shard_map/ppermute | solution.py:465
  35.7 0.6 %collective-permute-done.13.r_6_ = f32[8,128]{1,0:T(8,128)S(1)} collective-permute-done((f32[8,128]{1,0:T(8,128)S(1)}, f32[8,128]{1,0:T(8,128)S(1)}, u32[]{:S(2)}, u32[]{:S(2)}) %collective-permute-start.13) | collective-permute-done | bytes 4128 | tf_op jit(solution)/shard_map/ppermute | solution.py:465
  36.2 1.5 %shard_map.147 = (f32[32,64,128]{2,1,0:T(8,128)}, f32[32,64,128]{2,1,0:T(8,128)}) custom-call(f32[32,64,128]{2,1,0:T(8,128)S(1)} %shard_map.141.r_0_, f32[32,64,128]{2,1,0:T(8,128)S(1)} %shard_map.143.r_1_, f32[32,64,128]{2,1,0:T(8,128)S(1)} %shard_map.145.r_2_, f32[3,32,128]{2,1,0:T(8,128)S(1)} %get-tuple-element.62.r_3_, ...), custom_call_target="tpu_custom_call" | custom-call | tf_op jit(solution)/shard_map/pallas_call | solution.py:541
  (15 shorter events, 0.0 us)
Async XLA Ops:
  0.6 9.4 %copy-start.2 = (bf16[256,256]{1,0:T(8,128)(2,1)S(1)}, bf16[256,256]{1,0:T(8,128)(2,1)}, u32[]{:S(2)}) copy-start(bf16[256,256]{1,0:T(8,128)(2,1)} %constant.22.clone.eyw_h.eyw.r_6_) | copy-start | bytes 393220
  0.6 9.4 %copy-start.3 = (bf16[64,192]{1,0:T(8,128)(2,1)S(1)}, bf16[64,192]{1,0:T(8,128)(2,1)}, u32[]{:S(2)}) copy-start(bf16[64,192]{1,0:T(8,128)(2,1)} %constant.23.clone.exw_h.exw.r_7_) | copy-start | bytes 73732
  4.3 8.9 %collective-permute-start = (f32[40,128]{1,0:T(8,128)S(1)}, f32[40,128]{1,0:T(8,128)S(1)}, u32[]{:S(2)}, u32[]{:S(2)}) collective-permute-start(f32[40,128]{1,0:T(8,128)S(1)} %get-tuple-element.35.r_0_), channel_id=1, source_target_pairs={{0,12},{4,0},{8,4},{12,8},{1,13},{5,1},{9,5},{13,9},{2,14},{6,2},{... | collective-permute-start | bytes 61448 | tf_op jit(solution)/shard_map/ppermute | solution.py:465
  9.4 5.6 %collective-permute-start.1 = (f32[40,128]{1,0:T(8,128)S(1)}, f32[40,128]{1,0:T(8,128)S(1)}, u32[]{:S(2)}, u32[]{:S(2)}) collective-permute-start(f32[40,128]{1,0:T(8,128)S(1)} %get-tuple-element.36.r_1_), channel_id=1, source_target_pairs={{0,4},{4,8},{8,12},{12,0},{1,5},{5,9},{9,13},{13,1},{2,6},{6,10},{... | collective-permute-start | bytes 61448 | tf_op jit(solution)/shard_map/ppermute | solution.py:465
  9.4 2.2 %collective-permute-start.2 = (f32[24,128]{1,0:T(8,128)S(1)}, f32[24,128]{1,0:T(8,128)S(1)}, u32[]{:S(2)}, u32[]{:S(2)}) collective-permute-start(f32[24,128]{1,0:T(8,128)S(1)} %get-tuple-element.37.r_2_), channel_id=1, source_target_pairs={{0,3},{1,0},{2,1},{3,2},{4,7},{5,4},{6,5},{7,6},{8,11},{9,8},{10,9... | collective-permute-start | bytes 36872 | tf_op jit(solution)/shard_map/ppermute | solution.py:465
  10.1 3.1 %collective-permute-start.3 = (f32[24,128]{1,0:T(8,128)S(1)}, f32[24,128]{1,0:T(8,128)S(1)}, u32[]{:S(2)}, u32[]{:S(2)}) collective-permute-start(f32[24,128]{1,0:T(8,128)S(1)} %get-tuple-element.38.r_3_), channel_id=1, source_target_pairs={{0,1},{1,2},{2,3},{3,0},{4,5},{5,6},{6,7},{7,4},{8,9},{9,10},{10,1... | collective-permute-start | bytes 36872 | tf_op jit(solution)/shard_map/ppermute | solution.py:465
  10.1 4.9 %copy-start.1 = (f32[32,64,128]{2,1,0:T(8,128)S(1)}, f32[32,64,128]{2,1,0:T(8,128)}, u32[]{:S(2)}) copy-start(f32[32,64,128]{2,1,0:T(8,128)} %constant.27.clone.r_8_) | copy-start | bytes 3145732
  10.1 4.9 %copy-start.4 = (f32[5,64,128]{2,1,0:T(8,128)S(1)}, f32[5,64,128]{2,1,0:T(8,128)}, u32[]{:S(2)}) copy-start(f32[5,64,128]{2,1,0:T(8,128)} %constant.29.clone.r_10_) | copy-start | bytes 491524
  10.1 4.9 %copy-start.5 = (f32[5,32,128]{2,1,0:T(8,128)S(1)}, f32[5,32,128]{2,1,0:T(8,128)}, u32[]{:S(2)}) copy-start(f32[5,32,128]{2,1,0:T(8,128)} %constant.28.clone.r_9_) | copy-start | bytes 245764
  10.1 4.9 %copy-start.9 = (f32[8,128]{1,0:T(8,128)S(1)}, f32[8,128]{1,0:T(8,128)}, u32[]{:S(2)}) copy-start(f32[8,128]{1,0:T(8,128)} %constant.30.clone.r_11_) | copy-start | bytes 12292
  11.6 6.4 %copy-start = (f32[32,64,128]{2,1,0:T(8,128)S(1)}, f32[32,64,128]{2,1,0:T(8,128)}, u32[]{:S(2)}) copy-start(f32[32,64,128]{2,1,0:T(8,128)} %constant.26.clone.inv_h.inv) | copy-start | bytes 3145732
  11.6 6.4 %copy-start.6 = (f32[64,128]{1,0:T(8,128)S(1)}, f32[64,128]{1,0:T(8,128)}, u32[]{:S(2)}) copy-start(f32[64,128]{1,0:T(8,128)} %constant.31.clone.sx0_h.sx0) | copy-start | bytes 98308
  15.4 2.6 %copy-start.8 = (f32[8,128]{1,0:T(8,128)S(1)}, f32[8,128]{1,0:T(8,128)}, u32[]{:S(2)}) copy-start(f32[8,128]{1,0:T(8,128)} %constant.32.clone.sy0_h.sy0) | copy-start | bytes 12292
  15.5 5.2 %collective-permute-start.4 = (f32[40,128]{1,0:T(8,128)S(1)}, f32[40,128]{1,0:T(8,128)S(1)}, u32[]{:S(2)}, u32[]{:S(2)}) collective-permute-start(f32[40,128]{1,0:T(8,128)S(1)} %get-tuple-element.45.r_0_), channel_id=1, source_target_pairs={{0,12},{4,0},{8,4},{12,8},{1,13},{5,1},{9,5},{13,9},{2,14},{6,2},{... | collective-permute-start | bytes 61448 | tf_op jit(solution)/shard_map/ppermute | solution.py:465
  17.3 5.6 %collective-permute-start.5 = (f32[40,128]{1,0:T(8,128)S(1)}, f32[40,128]{1,0:T(8,128)S(1)}, u32[]{:S(2)}, u32[]{:S(2)}) collective-permute-start(f32[40,128]{1,0:T(8,128)S(1)} %get-tuple-element.46.r_1_), channel_id=1, source_target_pairs={{0,4},{4,8},{8,12},{12,0},{1,5},{5,9},{9,13},{13,1},{2,6},{6,10},{... | collective-permute-start | bytes 61448 | tf_op jit(solution)/shard_map/ppermute | solution.py:465
  17.5 2.8 %collective-permute-start.6 = (f32[24,128]{1,0:T(8,128)S(1)}, f32[24,128]{1,0:T(8,128)S(1)}, u32[]{:S(2)}, u32[]{:S(2)}) collective-permute-start(f32[24,128]{1,0:T(8,128)S(1)} %get-tuple-element.47.r_2_), channel_id=1, source_target_pairs={{0,3},{1,0},{2,1},{3,2},{4,7},{5,4},{6,5},{7,6},{8,11},{9,8},{10,9... | collective-permute-start | bytes 36872 | tf_op jit(solution)/shard_map/ppermute | solution.py:465
  17.5 3.1 %collective-permute-start.7 = (f32[24,128]{1,0:T(8,128)S(1)}, f32[24,128]{1,0:T(8,128)S(1)}, u32[]{:S(2)}, u32[]{:S(2)}) collective-permute-start(f32[24,128]{1,0:T(8,128)S(1)} %get-tuple-element.48.r_3_), channel_id=1, source_target_pairs={{0,1},{1,2},{2,3},{3,0},{4,5},{5,6},{6,7},{7,4},{8,9},{9,10},{10,1... | collective-permute-start | bytes 36872 | tf_op jit(solution)/shard_map/ppermute | solution.py:465
  23.3 7.2 %collective-permute-start.10 = (f32[8,128]{1,0:T(8,128)S(1)}, f32[8,128]{1,0:T(8,128)S(1)}, u32[]{:S(2)}, u32[]{:S(2)}) collective-permute-start(f32[8,128]{1,0:T(8,128)S(1)} %get-tuple-element.64), channel_id=1, source_target_pairs={{0,12},{4,0},{8,4},{12,8},{1,13},{5,1},{9,5},{13,9},{2,14},{6,2},{... | collective-permute-start | bytes 12296 | tf_op jit(solution)/shard_map/ppermute | solution.py:465
  24.7 5.8 %collective-permute-start.9 = (f32[8,128]{1,0:T(8,128)S(1)}, f32[8,128]{1,0:T(8,128)S(1)}, u32[]{:S(2)}, u32[]{:S(2)}) collective-permute-start(f32[8,128]{1,0:T(8,128)S(1)} %get-tuple-element.64), channel_id=1, source_target_pairs={{0,8},{4,12},{8,0},{12,4},{1,9},{5,13},{9,1},{13,5},{2,10},{6,14},... | collective-permute-start | bytes 12296 | tf_op jit(solution)/shard_map/ppermute | solution.py:465
  24.7 5.8 %collective-permute-start.8 = (f32[8,128]{1,0:T(8,128)S(1)}, f32[8,128]{1,0:T(8,128)S(1)}, u32[]{:S(2)}, u32[]{:S(2)}) collective-permute-start(f32[8,128]{1,0:T(8,128)S(1)} %get-tuple-element.64), channel_id=1, source_target_pairs={{0,4},{4,8},{8,12},{12,0},{1,5},{5,9},{9,13},{13,1},{2,6},{6,10},{... | collective-permute-start | bytes 12296 | tf_op jit(solution)/shard_map/ppermute | solution.py:465
  25.4 7.8 %collective-permute-start.12 = (f32[24,128]{1,0:T(8,128)S(1)}, f32[24,128]{1,0:T(8,128)S(1)}, u32[]{:S(2)}, u32[]{:S(2)}) collective-permute-start(f32[24,128]{1,0:T(8,128)S(1)} %get-tuple-element.61), channel_id=1, source_target_pairs={{0,1},{1,2},{2,3},{3,0},{4,5},{5,6},{6,7},{7,4},{8,9},{9,10},{10,1... | collective-permute-start | bytes 36872 | tf_op jit(solution)/shard_map/ppermute | solution.py:465
  25.4 7.8 %collective-permute-start.11 = (f32[40,128]{1,0:T(8,128)S(1)}, f32[40,128]{1,0:T(8,128)S(1)}, u32[]{:S(2)}, u32[]{:S(2)}) collective-permute-start(f32[40,128]{1,0:T(8,128)S(1)} %get-tuple-element.60), channel_id=1, source_target_pairs={{0,4},{4,8},{8,12},{12,0},{1,5},{5,9},{9,13},{13,1},{2,6},{6,10},{... | collective-permute-start | bytes 61448 | tf_op jit(solution)/shard_map/ppermute | solution.py:465
  28.2 5.0 %copy-start.7 = (f32[128,128]{1,0:T(8,128)S(1)}, f32[128,128]{1,0:T(8,128)}, u32[]{:S(2)}) copy-start(f32[128,128]{1,0:T(8,128)} %constant.25.clone.r_9_) | copy-start | bytes 196612
  30.5 2.7 %copy-start.10 = (f32[32,32]{1,0:T(8,128)S(1)}, f32[32,32]{1,0:T(8,128)}, u32[]{:S(2)}) copy-start(f32[32,32]{1,0:T(8,128)} %constant.24.clone.r_8_) | copy-start | bytes 12292
  30.6 3.3 %collective-permute-start.15 = (f32[8,128]{1,0:T(8,128)S(1)}, f32[8,128]{1,0:T(8,128)S(1)}, u32[]{:S(2)}, u32[]{:S(2)}) collective-permute-start(f32[8,128]{1,0:T(8,128)S(1)} %add_add_fusion.r_5_), channel_id=1, source_target_pairs={{0,3},{1,0},{2,1},{3,2},{4,7},{5,4},{6,5},{7,6},{8,11},{9,8},{10,9... | collective-permute-start | bytes 12296 | tf_op jit(solution)/shard_map/ppermute | solution.py:465
  32.1 3.6 %collective-permute-start.14 = (f32[8,128]{1,0:T(8,128)S(1)}, f32[8,128]{1,0:T(8,128)S(1)}, u32[]{:S(2)}, u32[]{:S(2)}) collective-permute-start(f32[8,128]{1,0:T(8,128)S(1)} %add_add_fusion.r_5_), channel_id=1, source_target_pairs={{0,2},{1,3},{2,0},{3,1},{4,6},{5,7},{6,4},{7,5},{8,10},{9,11},{10,... | collective-permute-start | bytes 12296 | tf_op jit(solution)/shard_map/ppermute | solution.py:465
  33.2 3.0 %collective-permute-start.13 = (f32[8,128]{1,0:T(8,128)S(1)}, f32[8,128]{1,0:T(8,128)S(1)}, u32[]{:S(2)}, u32[]{:S(2)}) collective-permute-start(f32[8,128]{1,0:T(8,128)S(1)} %add_add_fusion.r_5_), channel_id=1, source_target_pairs={{0,1},{1,2},{2,3},{3,0},{4,5},{5,6},{6,7},{7,4},{8,9},{9,10},{10,1... | collective-permute-start | bytes 12296 | tf_op jit(solution)/shard_map/ppermute | solution.py:465

commit v2 on v1

--- a/solution.py
+++ b/solution.py
@@ -34,6 +34,7 @@
     tab["eyw"] = np.block([[hi, lo], [hi, np.zeros_like(lo)]])
     hi, lo = split_bf16(sine_ext(width))
     tab["exw"] = np.concatenate([hi, lo, hi], 1)
+    tab["ey"], tab["ex"] = sine_ext(height).astype(np.float32), sine_ext(width).astype(np.float32)
     z = np.arange(depth)
     cos = np.cos(np.pi * np.outer(z + 0.5, z) / depth) * np.sqrt(2.0 / depth)
     cos[:, 0] = np.sqrt(1.0 / depth)
@@ -208,12 +209,15 @@
 
 def with_tail(body, tails, size=8):
     width = body.shape[1]
-    rows = list(tails) + [jnp.zeros((size - len(tails), width), F32)]
+    rows = list(tails)
+    if len(rows) < size:
+        rows.append(jnp.zeros((size - len(rows), width), F32))
     return jnp.concatenate([body, jnp.concatenate(rows, 0)], 0)
 
 
-def front_kernel(charge_h, surf_h, eyw_h, exw_h, inv_h, sx0_h, sy0_h, base, px, nx, py, ny,
-                 charge, surf, eyw, exw, inv, sx0, sy0, work, part, first, sems):
+def front_kernel(charge_h, surf_h, eyw_h, exw_h, inv_h, sx0_h, sy0_h, base, *rest):
+    msgs = rest[:4]
+    charge, surf, eyw, exw, inv, sx0, sy0, work, part, first, sems = rest[4:]
     depth, width, height = charge.shape
     scale = np.sqrt(2.0 / depth)
     tiles = width // 8
@@ -260,14 +264,22 @@
     at_zero = (lax.broadcasted_iota(jnp.int32, row.shape, 0) == 0) & (lane_id(row.shape) < depth)
     row = jnp.where(at_zero, 0.0, row)
     col = jnp.where(lax.broadcasted_iota(jnp.int32, own.shape, 0) == 0, 0.0, own + near)
-    px[...] = with_tail(row, [corner])
-    nx[...] = with_tail(rows_from(copies_t(row_far), depth), [])
-    py[...] = with_tail(pack(col, depth), [corner])
-    ny[...] = with_tail(pack(far, depth), [])
+    px = with_tail(row, [corner])
+    nx = with_tail(rows_from(copies_t(row_far), depth), [])
+    py = with_tail(pack(col, depth), [corner])
+    ny = with_tail(pack(far, depth), [])
+    for ref, value in zip(msgs, swapped("gx", nx, px) + swapped("gy", ny, py)):
+        ref[...] = value
+
+
+def swapped(axis, after, before):
+    even = lax.axis_index(axis) % 2 == 0
+    return jnp.where(even, before, after), jnp.where(even, after, before)
 
 
 def assemble(depth, own, got):
-    (px, nx, py, ny), (from_nx, from_px, from_ny, from_py) = own, got
+    (nx, px), (ny, py) = swapped("gx", *own[:2]), swapped("gy", *own[2:])
+    (from_nx, from_px), (from_ny, from_py) = swapped("gx", *got[:2]), swapped("gy", *got[2:])
     rows, cols = px.shape[0] - 8, py.shape[0] - 8
     row = px[:rows] + from_px[:rows]
     row_n = from_nx[:rows] + nx[:rows]
@@ -295,7 +307,7 @@
     inv2, rowt, colt, crnt = refs[8:12]
     rest = list(refs[12:])
     before = rest.pop(0) if want_moments else None
-    state, px, nx, py, ny = rest[:5]
+    state, *outs = rest[:5]
     moments = rest[5] if want_moments else None
     part, odd_rows, even_rows = rest[-3:]
     row, row_n, col, col_n, c00, cx0, c0y = assemble(depth, own, got)
@@ -336,22 +348,29 @@
     col_end1 = total(sxs * col)
     col_end1n = total(sxs * col_n)
     q00 = crnt[0:1, :] * c00 - row_end0 - col_end0
-    px[...] = with_tail(row_img, [q00])
-    nx[...] = with_tail(-x_far, [-col_end1, -col_end1n])
-    py[...] = with_tail(pack(col_img, depth), [q00])
-    ny[...] = with_tail(pack(-y_far, depth), [-row_end1, -row_end1n])
-    if want_moments:
-        row0, _, col0, _, c000, _, _ = unpacked_state(before, rows, cols)
-        share = depth / 128.0
-
-        def dot(x, y):
-            return total(x[0] * y[0]) + share * (total(x[1] * y[1]) + x[2] * y[2])
-
-        v0, v1 = (row0, col0, c000), (row, col, c00)
-        m3 = total(row * row_img - row_n * x_far) + share * (
-            total(col * col_img - col_n * y_far) + c00 * q00 - c0y * row_end1 - cx0 * col_end1
-        )
-        moments[...] = jnp.concatenate([dot(v0, v0), dot(v0, v1), dot(v1, v1), m3, jnp.zeros((4, 128), F32)], 0)
+    px = with_tail(row_img, [q00])
+    nx = with_tail(-x_far, [-col_end1, -col_end1n])
+    py = with_tail(pack(col_img, depth), [q00])
+    ny = with_tail(pack(-y_far, depth), [-row_end1, -row_end1n])
+    if not want_moments:
+        for ref, value in zip(outs, swapped("gx", nx, px) + swapped("gy", ny, py)):
+            ref[...] = value
+        return
+    row0, _, col0, _, c000, _, _ = unpacked_state(before, rows, cols)
+    share = depth / 128.0
+
+    def dot(x, y):
+        return total(x[0] * y[0]) + share * (total(x[1] * y[1]) + x[2] * y[2])
+
+    v0, v1 = (row0, col0, c000), (row, col, c00)
+    m3 = total(row * row_img - row_n * x_far) + share * (
+        total(col * col_img - col_n * y_far) + c00 * q00 - c0y * row_end1 - cx0 * col_end1
+    )
+    tail = [-col_end1, -col_end1n, c00, c00, dot(v0, v0), dot(v0, v1), dot(v1, v1), m3]
+    nx = with_tail(-x_far, tail)
+    moments[...] = nx[rows:]
+    for ref, value in zip(outs, (px, nx, py, ny)):
+        ref[...] = value
 
 
 def cells_from(out, work, spectrum, exw, eyw):
@@ -396,7 +415,7 @@
     cells_from(out, work, spectrum, exw[...], eyw[...])
 
 
-def rims_kernel(depth, s0, s1, px, py, from_px, from_py, eyw, exw, cz, czt, out_rows, out_cols):
+def rims_kernel(depth, s0, s1, px, py, from_px, from_py, ey, ex, cz, czt, out_rows, out_cols):
     packed = py.shape[0] - 8
     rows = px.shape[0] - 8
     width = packed * 128 // depth
@@ -410,12 +429,13 @@
     at_zero = (lax.broadcasted_iota(jnp.int32, (rows, 128), 0) == 0) & (lane_id((rows, 128)) < depth)
     lines = [rows_back(jnp.where(at_zero, v[4], v[0]), depth) for v in (v0, v1, v2)]
     high = lax.Precision.HIGHEST
-    lines = times_sy(jnp.concatenate(lines, 0), eyw[...])
+    lines = jnp.dot(jnp.concatenate(lines, 0), ey[...], precision=high, preferred_element_type=F32)
     lines = jnp.concatenate([lines[i * depth:(i + 1) * depth] for i in range(3)], 1)
     lines = jnp.dot(cz[...], lines, precision=high, preferred_element_type=F32)
     for i in range(3):
         out_rows[i] = lines[:, i * 128:(i + 1) * 128]
-    sides = sx_times(exw[...], jnp.concatenate([v[2] for v in (v0, v1, v2)], 1))
+    sides = jnp.concatenate([v[2] for v in (v0, v1, v2)], 1)
+    sides = jnp.dot(ex[...], sides, precision=high, preferred_element_type=F32)
     sides = jnp.concatenate([sides[:, i * 128:(i + 1) * 128] for i in range(3)], 0)
     sides = jnp.dot(sides, czt[...], precision=high, preferred_element_type=F32)
     for i in range(3):
@@ -431,8 +451,8 @@
     for other in moms[1:]:
         m = m + other[...]
     m = jnp.broadcast_to(jnp.sum(m, 1, keepdims=True), (8, 128))
-    m0 = m[0:1]
-    n1, n2, n3 = m[1:2] / m0, m[2:3] / m0, m[3:4] / m0
+    m0 = m[4:5]
+    n1, n2, n3 = m[5:6] / m0, m[6:7] / m0, m[7:8] / m0
     det = n1 * n3 - n2 * n2
     fine = det > 1e-6 * (n1 * n3)
     safe = jnp.where(fine, det, 1.0)
@@ -465,22 +485,30 @@
     return lax.ppermute(value, axis, [(i, (i + by) % n) for i in range(n)])
 
 
-def exchange(px, nx, py, ny):
-    from_py = shifted(ny, "gy", 1)
-    from_ny = shifted(py, "gy", -1)
-    from_px = shifted(nx, "gx", 1)
-    from_nx = shifted(px, "gx", -1)
-    return from_nx, from_px, from_ny, from_py
-
-
-def pieces_over(value, axis):
-    n, stride = lax.axis_size(axis), 1
+def swap(value, axis, odd):
+    n = lax.axis_size(axis)
+    pairs = [(i, (i + 1) % n) for i in range(odd, n, 2)]
+    return lax.ppermute(value, axis, pairs + [(j, i) for i, j in pairs])
+
+
+def exchange(bx, ax, by, ay):
+    return swap(bx, "gx", 1), swap(ax, "gx", 0), swap(by, "gy", 1), swap(ay, "gy", 0)
+
+
+def pieces_over(value, axis, first=None):
+    n, stride, kept = lax.axis_size(axis), 1, None
     while True:
         radix = 4 if n % 4 == 0 else 2 if n % 2 == 0 else n
-        parts = [value] + [shifted(value, axis, stride * j) for j in range(1, radix)]
+        parts = [value]
+        for j in range(1, radix):
+            if first is not None and stride * j == 1:
+                kept = shifted(first, axis, 1)
+                parts.append(kept[-value.shape[0]:])
+            else:
+                parts.append(shifted(value, axis, stride * j))
         n, stride = n // radix, stride * radix
         if n == 1:
-            return parts
+            return parts, kept
         value = sum(parts[1:], parts[0])
 
 
@@ -530,13 +558,13 @@
     s1, px, nx, py, ny, moments = call(
         lambda *r: schur_kernel(depth, True, *r), [state] + msgs + [(8, 128)], scratch
     )(*own, *got, *tables, s0)
-    parts = pieces_over(moments, "gx")
-    from_py, from_px = shifted(ny, "gy", 1), shifted(nx, "gx", 1)
+    parts, from_px = pieces_over(moments, "gx", nx)
+    from_py = shifted(ny, "gy", 1)
     cells_1 = extend(s1, *backs)[0]
     *parts, cells_1 = lax.optimization_barrier((*parts, cells_1))
-    parts = pieces_over(sum(parts[1:], parts[0]), "gy")
+    parts, _ = pieces_over(sum(parts[1:], parts[0]), "gy")
     rim = call(lambda *r: rims_kernel(depth, *r), [(3, depth, height), (3, width, 128)], [])(
-        s0, s1, px, py, from_px, from_py, tab["eyw"], tab["exw"], tab["cz"], tab["czt"]
+        s0, s1, px, py, from_px, from_py, tab["ey"], tab["ex"], tab["cz"], tab["czt"]
     )
     return call(
         lambda *r: final_kernel(len(parts), *r), [block, block], [block, block, pltpu.SemaphoreType.DMA((8,))],

time: 37.9 us -> 34.6 us (0.913)
  waiting for transfers between devices: 8.23 us -> 4.07 us
  starting transfers between devices: 15.9 us -> 16.5 us
    ppermute x0 -> x8, starting transfers between devices: none -> 10.2 us  [swap(): return lax.ppermute(value, axis, pairs + [(j, i) for i, j in pairs])]
    ppermute x16 -> x7, starting transfers between devices: 15.9 us -> 6.33 us  [shifted(): return lax.ppermute(value, axis, [(i, (i + by) % n) for i in range(n)])]
    ppermute x16 -> x7, waiting for transfers between devices: 8.23 us -> 3.38 us  [shifted(): return lax.ppermute(value, axis, [(i, (i + by) % n) for i in range(n)])]
    ppermute x0 -> x8, waiting for transfers between devices: none -> 0.69 us  [swap(): return lax.ppermute(value, axis, pairs + [(j, i) for i, j in pairs])]
  transfers between devices with their start and end apart: 16 -> 15, of which waited for: 6 -> 5; matrix products, arithmetic and copies ran while one was open for 0% -> 0% of each run, Pallas kernels for 18% -> 20%
where the time goes in v2:
time: 34.6 us; the launch traced here: 34.5 us
  starting transfers between devices  16.5 us (48%)
  Pallas kernels  13 us (38%)
  waiting for transfers between devices  4.07 us (12%)
  between operations  0.86 us (2%)
    ppermute x8, starting transfers between devices, swap(): return lax.ppermute(value, axis, pairs + [(j, i) for i, j in pairs])  10.2 us
    ppermute x7, starting transfers between devices, shifted(): return lax.ppermute(value, axis, [(i, (i + by) % n) for i in range(n)])  6.33 us
    pallas_call x1, Pallas kernels, on_device(): call(front_kernel, [block] + msgs, landing + [block, (depth, 8, height),...  3.64 us
    ppermute x7, waiting for transfers between devices, shifted(): return lax.ppermute(value, axis, [(i, (i + by) % n) for i in range(n)])  3.38 us
    pallas_call x1, Pallas kernels, on_device(): cells_1 = extend(s1, *backs)[0]  2.27 us
    pallas_call x1, Pallas kernels, on_device(): cells_0 = extend(s0, *backs)[0]  2.27 us
    pallas_call x1, Pallas kernels, on_device(): call(lambda *r: final_kernel(len(parts), *r), [block, block], [block, blo...  1.53 us
    pallas_call x1, Pallas kernels, on_device(): call(base_kernel, [block], [block])(base, tab['eyw'], tab['exw'])[0]  1.48 us
  transfers between devices with their start and end apart: 15, of which 5 were waited for; matrix products, arithmetic and copies ran while one was open for 0% of the time, Pallas kernels for 20%

profile of v2, /device:TPU:0, one launch (start us, length us, event | category | flops | bytes accessed | tf_op | source)
XLA Modules:
  0.0 34.5 jit_solution(6354875567563173158)
XLA Ops:
  0.6 0.0 copy-start.2
  0.6 0.0 copy-start.4
  0.7 3.6 %shard_map.158 = (f32[32,64,128]{2,1,0:T(8,128)S(1)}, f32[40,128]{1,0:T(8,128)S(1)}, f32[40,128]{1,0:T(8,128)S(1)}, f32[24,128]{1,0:T(8,128)S(1)}, f32[24,128]{1,0:T(8,128)S(1)}) custom-call(f32[32,64,128]{2,1,0:T(8,128)} %charge_h.1, f32[2,64,128]{2,1,0:T(8,128)} %surf_h.1, bf16[256,256]{1,0:T(8,128)(2,1)} %constant.26.clone.eyw_h.eyw, ...), custom_call_target="tpu_custom_call" | custom-call | tf_op jit(solution)/shard_map/pallas_call | solution.py:542
  4.3 5.1 %collective-permute-start = (f32[40,128]{1,0:T(8,128)S(1)}, f32[40,128]{1,0:T(8,128)S(1)}, u32[]{:S(2)}, u32[]{:S(2)}) collective-permute-start(f32[40,128]{1,0:T(8,128)S(1)} %get-tuple-element.35.r_0_), channel_id=1, source_target_pairs={{4,8},{12,0},{8,4},{0,12},{5,9},{13,1},{9,5},{1,13},{6,10},{14,2},... | collective-permute-start | bytes 61448 | tf_op jit(solution)/shard_map/ppermute | solution.py:491
  9.4 0.0 collective-permute-start.1
  9.4 0.6 %collective-permute-start.2 = (f32[24,128]{1,0:T(8,128)S(1)}, f32[24,128]{1,0:T(8,128)S(1)}, u32[]{:S(2)}, u32[]{:S(2)}) collective-permute-start(f32[24,128]{1,0:T(8,128)S(1)} %get-tuple-element.37.r_2_), channel_id=1, source_target_pairs={{1,2},{3,0},{2,1},{0,3},{5,6},{7,4},{6,5},{4,7},{9,10},{11,8},{10,... | collective-permute-start | bytes 36872 | tf_op jit(solution)/shard_map/ppermute | solution.py:491
  10.1 1.0 %collective-permute-start.3 = (f32[24,128]{1,0:T(8,128)S(1)}, f32[24,128]{1,0:T(8,128)S(1)}, u32[]{:S(2)}, u32[]{:S(2)}) collective-permute-start(f32[24,128]{1,0:T(8,128)S(1)} %get-tuple-element.38.r_3_), channel_id=1, source_target_pairs={{0,1},{2,3},{1,0},{3,2},{4,5},{6,7},{5,4},{7,6},{8,9},{10,11},{9,8... | collective-permute-start | bytes 36872 | tf_op jit(solution)/shard_map/ppermute | solution.py:491
  11.0 0.0 copy-start.5
  11.1 0.0 copy-start.11
  11.1 1.5 %shard_map.159.r_0_ = f32[32,64,128]{2,1,0:T(8,128)S(1)} custom-call(f32[32,64,128]{2,1,0:T(8,128)S(1)} %get-tuple-element.39.base, bf16[256,256]{1,0:T(8,128)(2,1)S(1)} %copy-done.2, bf16[64,192]{1,0:T(8,128)(2,1)S(1)} %copy-done.4), custom_call_target="tpu_custom_call" | custom-call | tf_op jit(solution)/shard_map/pallas_call | solution.py:548
  12.6 0.0 copy-start
  12.6 0.0 copy-start.6
  12.6 0.0 collective-permute-done.2.r_6_
  12.6 0.0 collective-permute-done.3.r_7_
  12.6 0.0 collective-permute-done.r_4_
  12.6 0.6 %collective-permute-done.1.r_5_ = f32[40,128]{1,0:T(8,128)S(1)} collective-permute-done((f32[40,128]{1,0:T(8,128)S(1)}, f32[40,128]{1,0:T(8,128)S(1)}, u32[]{:S(2)}, u32[]{:S(2)}) %collective-permute-start.1) | collective-permute-done | bytes 20512 | tf_op jit(solution)/shard_map/ppermute | solution.py:491
  13.2 0.0 copy-done.5
  13.2 0.0 copy-done.11
  13.2 0.4 %shard_map.160 = (f32[200,128]{1,0:T(8,128)S(1)}, f32[40,128]{1,0:T(8,128)S(1)}, f32[40,128]{1,0:T(8,128)S(1)}, f32[24,128]{1,0:T(8,128)S(1)}, f32[24,128]{1,0:T(8,128)S(1)}) custom-call(f32[40,128]{1,0:T(8,128)S(1)} %get-tuple-element.35.r_0_, f32[40,128]{1,0:T(8,128)S(1)} %get-tuple-element.36.r_1_, f32[24,128]{1,0:T(8,128)S(1)} %get-tuple-element.37.r_2_, ...), custom_call_target="tpu_custom_call" | custom-call | tf_op jit(solution)/shard_map/pallas_call | solution.py:552
  13.7 0.0 copy-start.9
  13.7 1.9 %collective-permute-start.4 = (f32[40,128]{1,0:T(8,128)S(1)}, f32[40,128]{1,0:T(8,128)S(1)}, u32[]{:S(2)}, u32[]{:S(2)}) collective-permute-start(f32[40,128]{1,0:T(8,128)S(1)} %get-tuple-element.45.r_0_), channel_id=1, source_target_pairs={{4,8},{12,0},{8,4},{0,12},{5,9},{13,1},{9,5},{1,13},{6,10},{14,2},... | collective-permute-start | bytes 61448 | tf_op jit(solution)/shard_map/ppermute | solution.py:491
  15.6 0.0 collective-permute-start.5
  15.6 0.0 collective-permute-start.6
  15.6 1.6 %collective-permute-start.7 = (f32[24,128]{1,0:T(8,128)S(1)}, f32[24,128]{1,0:T(8,128)S(1)}, u32[]{:S(2)}, u32[]{:S(2)}) collective-permute-start(f32[24,128]{1,0:T(8,128)S(1)} %get-tuple-element.48.r_3_), channel_id=1, source_target_pairs={{0,1},{2,3},{1,0},{3,2},{4,5},{6,7},{5,4},{7,6},{8,9},{10,11},{9,8... | collective-permute-start | bytes 36872 | tf_op jit(solution)/shard_map/ppermute | solution.py:491
  17.2 2.3 %shard_map.161.r_1_ = f32[32,64,128]{2,1,0:T(8,128)S(1)} custom-call(f32[200,128]{1,0:T(8,128)S(1)} %get-tuple-element.49.state.r_12_.r_0_, bf16[256,256]{1,0:T(8,128)(2,1)S(1)} %copy-done.2, bf16[64,192]{1,0:T(8,128)(2,1)S(1)} %copy-done.4, f32[32,64,128]{2,1,0:T(8,128)S(1)} %copy-done, f32[64,128]{1,0:T(8,128)S(1)} %copy-done.6, f32[8,128]{1,0:T(8,128)S(1)} %copy-done.9), custom_call_target="tpu_custom_call" | custom-call | tf_op jit(solution)/shard_map/pallas_call | solution.py:556
  19.4 0.0 collective-permute-done.6.r_6_
  19.5 0.0 collective-permute-done.7.r_7_
  19.5 0.0 collective-permute-done.4.r_4_
  19.5 0.1 collective-permute-done.5.r_5_
  19.5 0.4 %shard_map.162 = (f32[200,128]{1,0:T(8,128)S(1)}, f32[40,128]{1,0:T(8,128)S(1)}, f32[40,128]{1,0:T(8,128)S(1)}, f32[24,128]{1,0:T(8,128)S(1)}, f32[24,128]{1,0:T(8,128)S(1)}, /*index=5*/f32[8,128]{1,0:T(8,128)S(1)}) custom-call(f32[40,128]{1,0:T(8,128)S(1)} %get-tuple-element.45.r_0_, f32[40,128]{1,0:T(8,128)S(1)} %get-tuple-element.46.r_1_, ...), custom_call_target="tpu_custom_call" | custom-call | tf_op jit(solution)/shard_map/pallas_call | solution.py:558
  20.0 2.0 %collective-permute-start.8 = (f32[40,128]{1,0:T(8,128)S(1)}, f32[40,128]{1,0:T(8,128)S(1)}, u32[]{:S(2)}, u32[]{:S(2)}) collective-permute-start(f32[40,128]{1,0:T(8,128)S(1)} %get-tuple-element.56), channel_id=1, source_target_pairs={{0,4},{4,8},{8,12},{12,0},{1,5},{5,9},{9,13},{13,1},{2,6},{6,10},{... | collective-permute-start | bytes 61448 | tf_op jit(solution)/shard_map/ppermute | solution.py:485
  22.0 1.8 %collective-permute-start.10 = (f32[8,128]{1,0:T(8,128)S(1)}, f32[8,128]{1,0:T(8,128)S(1)}, u32[]{:S(2)}, u32[]{:S(2)}) collective-permute-start(f32[8,128]{1,0:T(8,128)S(1)} %get-tuple-element.64), channel_id=1, source_target_pairs={{0,12},{4,0},{8,4},{12,8},{1,13},{5,1},{9,5},{13,9},{2,14},{6,2},{... | collective-permute-start | bytes 12296 | tf_op jit(solution)/shard_map/ppermute | solution.py:485
  23.9 0.7 %collective-permute-start.9 = (f32[8,128]{1,0:T(8,128)S(1)}, f32[8,128]{1,0:T(8,128)S(1)}, u32[]{:S(2)}, u32[]{:S(2)}) collective-permute-start(f32[8,128]{1,0:T(8,128)S(1)} %get-tuple-element.64), channel_id=1, source_target_pairs={{0,8},{4,12},{8,0},{12,4},{1,9},{5,13},{9,1},{13,5},{2,10},{6,14},... | collective-permute-start | bytes 12296 | tf_op jit(solution)/shard_map/ppermute | solution.py:485
  24.6 0.0 collective-permute-start.11
  24.6 2.3 %shard_map.163.r_2_ = f32[32,64,128]{2,1,0:T(8,128)S(1)} custom-call(f32[200,128]{1,0:T(8,128)S(1)} %get-tuple-element.57.state.r_1_, bf16[256,256]{1,0:T(8,128)(2,1)S(1)} %copy-done.2, bf16[64,192]{1,0:T(8,128)(2,1)S(1)} %copy-done.4, f32[32,64,128]{2,1,0:T(8,128)S(1)} %copy-done, f32[64,128]{1,0:T(8,128)S(1)} %copy-done.6, f32[8,128]{1,0:T(8,128)S(1)} %copy-done.9), custom_call_target="tpu_custom_call" | custom-call | tf_op jit(solution)/shard_map/pallas_call | solution.py:563
  26.9 0.0 copy-start.12
  26.9 0.0 collective-permute-done.8.r_4_
  26.9 0.0 collective-permute-done.10
  26.9 1.4 %collective-permute-done.9 = f32[8,128]{1,0:T(8,128)S(1)} collective-permute-done((f32[8,128]{1,0:T(8,128)S(1)}, f32[8,128]{1,0:T(8,128)S(1)}, u32[]{:S(2)}, u32[]{:S(2)}) %collective-permute-start.9) | collective-permute-done | bytes 4128 | tf_op jit(solution)/shard_map/ppermute | solution.py:485
  28.4 0.4 %collective-permute-start.14 = (f32[8,128]{1,0:T(8,128)S(1)}, f32[8,128]{1,0:T(8,128)S(1)}, u32[]{:S(2)}, u32[]{:S(2)}) collective-permute-start(f32[8,128]{1,0:T(8,128)S(1)} %add_add_fusion.r_5_), channel_id=1, source_target_pairs={{0,3},{1,0},{2,1},{3,2},{4,7},{5,4},{6,5},{7,6},{8,11},{9,8},{10,9... | collective-permute-start | bytes 12296 | tf_op jit(solution)/shard_map/ppermute | solution.py:485
  28.8 1.2 %collective-permute-start.13 = (f32[8,128]{1,0:T(8,128)S(1)}, f32[8,128]{1,0:T(8,128)S(1)}, u32[]{:S(2)}, u32[]{:S(2)}) collective-permute-start(f32[8,128]{1,0:T(8,128)S(1)} %add_add_fusion.r_5_), channel_id=1, source_target_pairs={{0,2},{1,3},{2,0},{3,1},{4,6},{5,7},{6,4},{7,5},{8,10},{9,11},{10,... | collective-permute-start | bytes 12296 | tf_op jit(solution)/shard_map/ppermute | solution.py:485
  29.9 0.2 collective-permute-start.12
  30.1 0.0 collective-permute-done.11.r_5_
  30.1 0.9 %shard_map.164 = (f32[3,32,128]{2,1,0:T(8,128)S(1)}, f32[3,64,128]{2,1,0:T(8,128)S(1)}) custom-call(f32[200,128]{1,0:T(8,128)S(1)} %get-tuple-element.49.state.r_12_.r_0_, f32[200,128]{1,0:T(8,128)S(1)} %get-tuple-element.57.state.r_1_, f32[40,128]{1,0:T(8,128)S(1)} %get-tuple-element.59.r_2_, f32[24,128]{1,0:T(8,128)S(1)} %get-tuple-element.60.r_3_, ...), custom_call_target="tpu_custom_call" | custom-call | tf_op jit(solution)/shard_map/pallas_call | solution.py:566
  31.0 0.0 collective-permute-done.14.r_8_
  31.0 1.3 %collective-permute-done.13.r_7_ = f32[8,128]{1,0:T(8,128)S(1)} collective-permute-done((f32[8,128]{1,0:T(8,128)S(1)}, f32[8,128]{1,0:T(8,128)S(1)}, u32[]{:S(2)}, u32[]{:S(2)}) %collective-permute-start.13) | collective-permute-done | bytes 4128 | tf_op jit(solution)/shard_map/ppermute | solution.py:485
  32.4 0.6 %collective-permute-done.12.r_6_ = f32[8,128]{1,0:T(8,128)S(1)} collective-permute-done((f32[8,128]{1,0:T(8,128)S(1)}, f32[8,128]{1,0:T(8,128)S(1)}, u32[]{:S(2)}, u32[]{:S(2)}) %collective-permute-start.12) | collective-permute-done | bytes 4128 | tf_op jit(solution)/shard_map/ppermute | solution.py:485
  33.0 1.5 %shard_map.165 = (f32[32,64,128]{2,1,0:T(8,128)}, f32[32,64,128]{2,1,0:T(8,128)}) custom-call(f32[32,64,128]{2,1,0:T(8,128)S(1)} %shard_map.159.r_0_, f32[32,64,128]{2,1,0:T(8,128)S(1)} %shard_map.161.r_1_, f32[32,64,128]{2,1,0:T(8,128)S(1)} %shard_map.163.r_2_, f32[3,32,128]{2,1,0:T(8,128)S(1)} %get-tuple-element.62.r_3_, ...), custom_call_target="tpu_custom_call" | custom-call | tf_op jit(solution)/shard_map/pallas_call | solution.py:569
  (18 shorter events, 0.0 us)
Async XLA Ops:
  0.6 10.4 %copy-start.2 = (bf16[256,256]{1,0:T(8,128)(2,1)S(1)}, bf16[256,256]{1,0:T(8,128)(2,1)}, u32[]{:S(2)}) copy-start(bf16[256,256]{1,0:T(8,128)(2,1)} %constant.26.clone.eyw_h.eyw) | copy-start | bytes 393220
  0.6 10.4 %copy-start.4 = (bf16[64,192]{1,0:T(8,128)(2,1)S(1)}, bf16[64,192]{1,0:T(8,128)(2,1)}, u32[]{:S(2)}) copy-start(bf16[64,192]{1,0:T(8,128)(2,1)} %constant.27.clone.exw_h.exw) | copy-start | bytes 73732
  4.3 8.3 %collective-permute-start = (f32[40,128]{1,0:T(8,128)S(1)}, f32[40,128]{1,0:T(8,128)S(1)}, u32[]{:S(2)}, u32[]{:S(2)}) collective-permute-start(f32[40,128]{1,0:T(8,128)S(1)} %get-tuple-element.35.r_0_), channel_id=1, source_target_pairs={{4,8},{12,0},{8,4},{0,12},{5,9},{13,1},{9,5},{1,13},{6,10},{14,2},... | collective-permute-start | bytes 61448 | tf_op jit(solution)/shard_map/ppermute | solution.py:491
  9.4 3.8 %collective-permute-start.1 = (f32[40,128]{1,0:T(8,128)S(1)}, f32[40,128]{1,0:T(8,128)S(1)}, u32[]{:S(2)}, u32[]{:S(2)}) collective-permute-start(f32[40,128]{1,0:T(8,128)S(1)} %get-tuple-element.36.r_1_), channel_id=1, source_target_pairs={{0,4},{8,12},{4,0},{12,8},{1,5},{9,13},{5,1},{13,9},{2,6},{10,14},... | collective-permute-start | bytes 61448 | tf_op jit(solution)/shard_map/ppermute | solution.py:491
  9.4 3.2 %collective-permute-start.2 = (f32[24,128]{1,0:T(8,128)S(1)}, f32[24,128]{1,0:T(8,128)S(1)}, u32[]{:S(2)}, u32[]{:S(2)}) collective-permute-start(f32[24,128]{1,0:T(8,128)S(1)} %get-tuple-element.37.r_2_), channel_id=1, source_target_pairs={{1,2},{3,0},{2,1},{0,3},{5,6},{7,4},{6,5},{4,7},{9,10},{11,8},{10,... | collective-permute-start | bytes 36872 | tf_op jit(solution)/shard_map/ppermute | solution.py:491
  10.1 2.6 %collective-permute-start.3 = (f32[24,128]{1,0:T(8,128)S(1)}, f32[24,128]{1,0:T(8,128)S(1)}, u32[]{:S(2)}, u32[]{:S(2)}) collective-permute-start(f32[24,128]{1,0:T(8,128)S(1)} %get-tuple-element.38.r_3_), channel_id=1, source_target_pairs={{0,1},{2,3},{1,0},{3,2},{4,5},{6,7},{5,4},{7,6},{8,9},{10,11},{9,8... | collective-permute-start | bytes 36872 | tf_op jit(solution)/shard_map/ppermute | solution.py:491
  11.0 2.2 %copy-start.1 = (f32[32,64,128]{2,1,0:T(8,128)S(1)}, f32[32,64,128]{2,1,0:T(8,128)}, u32[]{:S(2)}) copy-start(f32[32,64,128]{2,1,0:T(8,128)} %constant.33.clone.r_8_) | copy-start | bytes 3145732
  11.0 2.2 %copy-start.3 = (f32[5,64,128]{2,1,0:T(8,128)S(1)}, f32[5,64,128]{2,1,0:T(8,128)}, u32[]{:S(2)}) copy-start(f32[5,64,128]{2,1,0:T(8,128)} %constant.35.clone.r_10_) | copy-start | bytes 491524
  11.0 2.2 %copy-start.5 = (f32[5,32,128]{2,1,0:T(8,128)S(1)}, f32[5,32,128]{2,1,0:T(8,128)}, u32[]{:S(2)}) copy-start(f32[5,32,128]{2,1,0:T(8,128)} %constant.34.clone.r_9_) | copy-start | bytes 245764
  11.1 2.2 %copy-start.11 = (f32[8,128]{1,0:T(8,128)S(1)}, f32[8,128]{1,0:T(8,128)}, u32[]{:S(2)}) copy-start(f32[8,128]{1,0:T(8,128)} %constant.36.clone.r_11_) | copy-start | bytes 12292
  12.6 4.6 %copy-start = (f32[32,64,128]{2,1,0:T(8,128)S(1)}, f32[32,64,128]{2,1,0:T(8,128)}, u32[]{:S(2)}) copy-start(f32[32,64,128]{2,1,0:T(8,128)} %constant.32.clone.inv_h.inv) | copy-start | bytes 3145732
  12.6 4.6 %copy-start.6 = (f32[64,128]{1,0:T(8,128)S(1)}, f32[64,128]{1,0:T(8,128)}, u32[]{:S(2)}) copy-start(f32[64,128]{1,0:T(8,128)} %constant.37.clone.sx0_h.sx0) | copy-start | bytes 98308
  13.7 3.5 %copy-start.9 = (f32[8,128]{1,0:T(8,128)S(1)}, f32[8,128]{1,0:T(8,128)}, u32[]{:S(2)}) copy-start(f32[8,128]{1,0:T(8,128)} %constant.38.clone.sy0_h.sy0) | copy-start | bytes 12292
  13.7 5.8 %collective-permute-start.4 = (f32[40,128]{1,0:T(8,128)S(1)}, f32[40,128]{1,0:T(8,128)S(1)}, u32[]{:S(2)}, u32[]{:S(2)}) collective-permute-start(f32[40,128]{1,0:T(8,128)S(1)} %get-tuple-element.45.r_0_), channel_id=1, source_target_pairs={{4,8},{12,0},{8,4},{0,12},{5,9},{13,1},{9,5},{1,13},{6,10},{14,2},... | collective-permute-start | bytes 61448 | tf_op jit(solution)/shard_map/ppermute | solution.py:491
  15.6 4.0 %collective-permute-start.5 = (f32[40,128]{1,0:T(8,128)S(1)}, f32[40,128]{1,0:T(8,128)S(1)}, u32[]{:S(2)}, u32[]{:S(2)}) collective-permute-start(f32[40,128]{1,0:T(8,128)S(1)} %get-tuple-element.46.r_1_), channel_id=1, source_target_pairs={{0,4},{8,12},{4,0},{12,8},{1,5},{9,13},{5,1},{13,9},{2,6},{10,14},... | collective-permute-start | bytes 61448 | tf_op jit(solution)/shard_map/ppermute | solution.py:491
  15.6 3.9 %collective-permute-start.6 = (f32[24,128]{1,0:T(8,128)S(1)}, f32[24,128]{1,0:T(8,128)S(1)}, u32[]{:S(2)}, u32[]{:S(2)}) collective-permute-start(f32[24,128]{1,0:T(8,128)S(1)} %get-tuple-element.47.r_2_), channel_id=1, source_target_pairs={{1,2},{3,0},{2,1},{0,3},{5,6},{7,4},{6,5},{4,7},{9,10},{11,8},{10,... | collective-permute-start | bytes 36872 | tf_op jit(solution)/shard_map/ppermute | solution.py:491
  15.6 3.9 %collective-permute-start.7 = (f32[24,128]{1,0:T(8,128)S(1)}, f32[24,128]{1,0:T(8,128)S(1)}, u32[]{:S(2)}, u32[]{:S(2)}) collective-permute-start(f32[24,128]{1,0:T(8,128)S(1)} %get-tuple-element.48.r_3_), channel_id=1, source_target_pairs={{0,1},{2,3},{1,0},{3,2},{4,5},{6,7},{5,4},{7,6},{8,9},{10,11},{9,8... | collective-permute-start | bytes 36872 | tf_op jit(solution)/shard_map/ppermute | solution.py:491
  20.0 6.9 %collective-permute-start.8 = (f32[40,128]{1,0:T(8,128)S(1)}, f32[40,128]{1,0:T(8,128)S(1)}, u32[]{:S(2)}, u32[]{:S(2)}) collective-permute-start(f32[40,128]{1,0:T(8,128)S(1)} %get-tuple-element.56), channel_id=1, source_target_pairs={{0,4},{4,8},{8,12},{12,0},{1,5},{5,9},{9,13},{13,1},{2,6},{6,10},{... | collective-permute-start | bytes 61448 | tf_op jit(solution)/shard_map/ppermute | solution.py:485
  22.0 4.9 %collective-permute-start.10 = (f32[8,128]{1,0:T(8,128)S(1)}, f32[8,128]{1,0:T(8,128)S(1)}, u32[]{:S(2)}, u32[]{:S(2)}) collective-permute-start(f32[8,128]{1,0:T(8,128)S(1)} %get-tuple-element.64), channel_id=1, source_target_pairs={{0,12},{4,0},{8,4},{12,8},{1,13},{5,1},{9,5},{13,9},{2,14},{6,2},{... | collective-permute-start | bytes 12296 | tf_op jit(solution)/shard_map/ppermute | solution.py:485
  23.9 4.5 %collective-permute-start.9 = (f32[8,128]{1,0:T(8,128)S(1)}, f32[8,128]{1,0:T(8,128)S(1)}, u32[]{:S(2)}, u32[]{:S(2)}) collective-permute-start(f32[8,128]{1,0:T(8,128)S(1)} %get-tuple-element.64), channel_id=1, source_target_pairs={{0,8},{4,12},{8,0},{12,4},{1,9},{5,13},{9,1},{13,5},{2,10},{6,14},... | collective-permute-start | bytes 12296 | tf_op jit(solution)/shard_map/ppermute | solution.py:485
  24.6 5.5 %collective-permute-start.11 = (f32[24,128]{1,0:T(8,128)S(1)}, f32[24,128]{1,0:T(8,128)S(1)}, u32[]{:S(2)}, u32[]{:S(2)}) collective-permute-start(f32[24,128]{1,0:T(8,128)S(1)} %get-tuple-element.61), channel_id=1, source_target_pairs={{0,1},{1,2},{2,3},{3,0},{4,5},{5,6},{6,7},{7,4},{8,9},{9,10},{10,1... | collective-permute-start | bytes 36872 | tf_op jit(solution)/shard_map/ppermute | solution.py:485
  24.6 5.5 %copy-start.7 = (f32[128,128]{1,0:T(8,128)S(1)}, f32[128,128]{1,0:T(8,128)}, u32[]{:S(2)}) copy-start(f32[128,128]{1,0:T(8,128)} %constant.31.clone.r_9_) | copy-start | bytes 196612
  24.6 5.5 %copy-start.8 = (f32[128,128]{1,0:T(8,128)S(1)}, f32[128,128]{1,0:T(8,128)}, u32[]{:S(2)}) copy-start(f32[128,128]{1,0:T(8,128)} %constant.28.clone.r_6_) | copy-start | bytes 196612
  24.6 5.5 %copy-start.10 = (f32[64,64]{1,0:T(8,128)S(1)}, f32[64,64]{1,0:T(8,128)}, u32[]{:S(2)}) copy-start(f32[64,64]{1,0:T(8,128)} %constant.29.clone.r_7_) | copy-start | bytes 49156
  26.9 3.2 %copy-start.12 = (f32[32,32]{1,0:T(8,128)S(1)}, f32[32,32]{1,0:T(8,128)}, u32[]{:S(2)}) copy-start(f32[32,32]{1,0:T(8,128)} %constant.30.clone.r_8_) | copy-start | bytes 12292
  28.4 2.7 %collective-permute-start.14 = (f32[8,128]{1,0:T(8,128)S(1)}, f32[8,128]{1,0:T(8,128)S(1)}, u32[]{:S(2)}, u32[]{:S(2)}) collective-permute-start(f32[8,128]{1,0:T(8,128)S(1)} %add_add_fusion.r_5_), channel_id=1, source_target_pairs={{0,3},{1,0},{2,1},{3,2},{4,7},{5,4},{6,5},{7,6},{8,11},{9,8},{10,9... | collective-permute-start | bytes 12296 | tf_op jit(solution)/shard_map/ppermute | solution.py:485
  28.8 3.6 %collective-permute-start.13 = (f32[8,128]{1,0:T(8,128)S(1)}, f32[8,128]{1,0:T(8,128)S(1)}, u32[]{:S(2)}, u32[]{:S(2)}) collective-permute-start(f32[8,128]{1,0:T(8,128)S(1)} %add_add_fusion.r_5_), channel_id=1, source_target_pairs={{0,2},{1,3},{2,0},{3,1},{4,6},{5,7},{6,4},{7,5},{8,10},{9,11},{10,... | collective-permute-start | bytes 12296 | tf_op jit(solution)/shard_map/ppermute | solution.py:485
  29.9 3.0 %collective-permute-start.12 = (f32[8,128]{1,0:T(8,128)S(1)}, f32[8,128]{1,0:T(8,128)S(1)}, u32[]{:S(2)}, u32[]{:S(2)}) collective-permute-start(f32[8,128]{1,0:T(8,128)S(1)} %add_add_fusion.r_5_), channel_id=1, source_target_pairs={{0,1},{1,2},{2,3},{3,0},{4,5},{5,6},{6,7},{7,4},{8,9},{9,10},{10,1... | collective-permute-start | bytes 12296 | tf_op jit(solution)/shard_map/ppermute | solution.py:485

commit v3 on v2

--- a/solution.py
+++ b/solution.py
@@ -308,7 +308,6 @@
     rest = list(refs[12:])
     before = rest.pop(0) if want_moments else None
     state, *outs = rest[:5]
-    moments = rest[5] if want_moments else None
     part, odd_rows, even_rows = rest[-3:]
     row, row_n, col, col_n, c00, cx0, c0y = assemble(depth, own, got)
     rows, cols = row.shape[0], col.shape[0]
@@ -352,24 +351,22 @@
     nx = with_tail(-x_far, [-col_end1, -col_end1n])
     py = with_tail(pack(col_img, depth), [q00])
     ny = with_tail(pack(-y_far, depth), [-row_end1, -row_end1n])
-    if not want_moments:
-        for ref, value in zip(outs, swapped("gx", nx, px) + swapped("gy", ny, py)):
-            ref[...] = value
-        return
-    row0, _, col0, _, c000, _, _ = unpacked_state(before, rows, cols)
-    share = depth / 128.0
-
-    def dot(x, y):
-        return total(x[0] * y[0]) + share * (total(x[1] * y[1]) + x[2] * y[2])
-
-    v0, v1 = (row0, col0, c000), (row, col, c00)
-    m3 = total(row * row_img - row_n * x_far) + share * (
-        total(col * col_img - col_n * y_far) + c00 * q00 - c0y * row_end1 - cx0 * col_end1
-    )
-    tail = [-col_end1, -col_end1n, c00, c00, dot(v0, v0), dot(v0, v1), dot(v1, v1), m3]
-    nx = with_tail(-x_far, tail)
-    moments[...] = nx[rows:]
-    for ref, value in zip(outs, (px, nx, py, ny)):
+    if want_moments:
+        row0, _, col0, _, c000, _, _ = unpacked_state(before, rows, cols)
+        share = depth / 128.0
+
+        def dot(x, y):
+            return total(x[0] * y[0]) + share * (total(x[1] * y[1]) + x[2] * y[2])
+
+        v0, v1 = (row0, col0, c000), (row, col, c00)
+        m3 = total(row * row_img - row_n * x_far) + share * (
+            total(col * col_img - col_n * y_far) + c00 * q00 - c0y * row_end1 - cx0 * col_end1
+        )
+        moments = [dot(v0, v0), dot(v0, v1), dot(v1, v1), m3]
+        px = with_tail(row_img, [q00, q00, q00, q00] + moments)
+        nx = with_tail(-x_far, [-col_end1, -col_end1n, c00, c00] + moments)
+    sides = (ny, py) if want_moments else swapped("gy", ny, py)
+    for ref, value in zip(outs, swapped("gx", nx, px) + sides):
         ref[...] = value
 
 
@@ -415,10 +412,12 @@
     cells_from(out, work, spectrum, exw[...], eyw[...])
 
 
-def rims_kernel(depth, s0, s1, px, py, from_px, from_py, ey, ex, cz, czt, out_rows, out_cols):
+def rims_kernel(depth, s0, s1, bx, ax, py, got_bx, got_ax, from_py, ey, ex, cz, czt, out_rows, out_cols):
     packed = py.shape[0] - 8
-    rows = px.shape[0] - 8
+    rows = bx.shape[0] - 8
     width = packed * 128 // depth
+    _, px = swapped("gx", bx[...], ax[...])
+    _, from_px = swapped("gx", got_bx[...], got_ax[...])
     v0 = unpacked_state(s0, rows, width)
     v1 = unpacked_state(s1, rows, width)
     v2 = (
@@ -495,21 +494,31 @@
     return swap(bx, "gx", 1), swap(ax, "gx", 0), swap(by, "gy", 1), swap(ay, "gy", 0)
 
 
-def pieces_over(value, axis, first=None):
-    n, stride, kept = lax.axis_size(axis), 1, None
+def pieces_over(value, axis):
+    n, stride = lax.axis_size(axis), 1
     while True:
         radix = 4 if n % 4 == 0 else 2 if n % 2 == 0 else n
-        parts = [value]
-        for j in range(1, radix):
-            if first is not None and stride * j == 1:
-                kept = shifted(first, axis, 1)
-                parts.append(kept[-value.shape[0]:])
-            else:
-                parts.append(shifted(value, axis, stride * j))
+        parts = [value] + [shifted(value, axis, stride * j) for j in range(1, radix)]
         n, stride = n // radix, stride * radix
         if n == 1:
-            return parts, kept
+            return parts
         value = sum(parts[1:], parts[0])
+
+
+def reduced_x(bx, ax):
+    got_bx, got_ax = swap(bx, "gx", 1), swap(ax, "gx", 0)
+    if lax.axis_size("gx") == 4:
+        parts = [bx, got_ax, shifted(bx, "gx", 2), got_bx]
+        parts = [part[-8:] for part in parts]
+    else:
+        parts = pieces_over(bx[-8:], "gx")
+    return parts, got_bx, got_ax
+
+
+def reduced_y(value):
+    if lax.axis_size("gy") == 4:
+        return [value, swap(value, "gy", 0), shifted(value, "gy", 2), swap(value, "gy", 1)]
+    return pieces_over(value, "gy")
 
 
 def call(kernel, outs, scratch, in_specs=None, out_specs=None):
@@ -555,16 +564,14 @@
     backs = tuple(tab[n] for n in ("eyw", "exw", "inv", "sx0", "sy0"))
     cells_0 = extend(s0, *backs)[0]
     *got, cells_0 = lax.optimization_barrier((*got, cells_0))
-    s1, px, nx, py, ny, moments = call(
-        lambda *r: schur_kernel(depth, True, *r), [state] + msgs + [(8, 128)], scratch
-    )(*own, *got, *tables, s0)
-    parts, from_px = pieces_over(moments, "gx", nx)
-    from_py = shifted(ny, "gy", 1)
+    s1, *own = call(lambda *r: schur_kernel(depth, True, *r), [state] + msgs, scratch)(*own, *got, *tables, s0)
+    parts, got_bx, got_ax = reduced_x(*own[:2])
+    from_py = shifted(own[2], "gy", 1)
     cells_1 = extend(s1, *backs)[0]
     *parts, cells_1 = lax.optimization_barrier((*parts, cells_1))
-    parts, _ = pieces_over(sum(parts[1:], parts[0]), "gy")
+    parts = reduced_y(sum(parts[1:], parts[0]))
     rim = call(lambda *r: rims_kernel(depth, *r), [(3, depth, height), (3, width, 128)], [])(
-        s0, s1, px, py, from_px, from_py, tab["ey"], tab["ex"], tab["cz"], tab["czt"]
+        s0, s1, own[0], own[1], own[3], got_bx, got_ax, from_py, tab["ey"], tab["ex"], tab["cz"], tab["czt"]
     )
     return call(
         lambda *r: final_kernel(len(parts), *r), [block, block], [block, block, pltpu.SemaphoreType.DMA((8,))],

time: 34.6 us -> 34.1 us (0.986)
  starting transfers between devices: 16.5 us -> 16.1 us
    ppermute x7 -> x3, starting transfers between devices: 6.33 us -> 0.76 us  [shifted(): return lax.ppermute(value, axis, [(i, (i + by) % n) for i in range(n)])]
    ppermute x8 -> x12, starting transfers between devices: 10.2 us -> 15.4 us  [swap(): return lax.ppermute(value, axis, pairs + [(j, i) for i, j in pairs])]
    ppermute x7 -> x3, waiting for transfers between devices: 3.38 us -> 1.76 us  [shifted(): return lax.ppermute(value, axis, [(i, (i + by) % n) for i in range(n)])]
    ppermute x8 -> x12, waiting for transfers between devices: 0.69 us -> 2.14 us  [swap(): return lax.ppermute(value, axis, pairs + [(j, i) for i, j in pairs])]
  transfers between devices with their start and end apart: 15 -> 15, of which waited for: 5 -> 6; matrix products, arithmetic and copies ran while one was open for 0% -> 0% of each run, Pallas kernels for 20% -> 20%
where the time goes in v3:
time: 34.1 us; the launch traced here: 34 us
  starting transfers between devices  16.1 us (47%)
  Pallas kernels  13 us (38%)
  waiting for transfers between devices  3.9 us (11%)
  between operations  0.87 us (3%)
    ppermute x12, starting transfers between devices, swap(): return lax.ppermute(value, axis, pairs + [(j, i) for i, j in pairs])  15.4 us
    pallas_call x1, Pallas kernels, on_device(): call(front_kernel, [block] + msgs, landing + [block, (depth, 8, height),...  3.64 us
    pallas_call x1, Pallas kernels, on_device(): cells_1 = extend(s1, *backs)[0]  2.27 us
    pallas_call x1, Pallas kernels, on_device(): cells_0 = extend(s0, *backs)[0]  2.27 us
    ppermute x12, waiting for transfers between devices, swap(): return lax.ppermute(value, axis, pairs + [(j, i) for i, j in pairs])  2.14 us
    ppermute x3, waiting for transfers between devices, shifted(): return lax.ppermute(value, axis, [(i, (i + by) % n) for i in range(n)])  1.76 us
    pallas_call x1, Pallas kernels, on_device(): call(lambda *r: final_kernel(len(parts), *r), [block, block], [block, blo...  1.53 us
    pallas_call x1, Pallas kernels, on_device(): call(base_kernel, [block], [block])(base, tab['eyw'], tab['exw'])[0]  1.48 us
  transfers between devices with their start and end apart: 15, of which 6 were waited for; matrix products, arithmetic and copies ran while one was open for 0% of the time, Pallas kernels for 20%

profile of v3, /device:TPU:0, one launch (start us, length us, event | category | flops | bytes accessed | tf_op | source)
XLA Modules:
  0.0 34.0 jit_solution(15274775370015220893)
XLA Ops:
  0.6 0.0 copy-start.2
  0.6 0.0 copy-start.4
  0.7 3.6 %shard_map.158 = (f32[32,64,128]{2,1,0:T(8,128)S(1)}, f32[40,128]{1,0:T(8,128)S(1)}, f32[40,128]{1,0:T(8,128)S(1)}, f32[24,128]{1,0:T(8,128)S(1)}, f32[24,128]{1,0:T(8,128)S(1)}) custom-call(f32[32,64,128]{2,1,0:T(8,128)} %charge_h.1, f32[2,64,128]{2,1,0:T(8,128)} %surf_h.1, bf16[256,256]{1,0:T(8,128)(2,1)} %constant.26.clone.eyw_h.eyw, ...), custom_call_target="tpu_custom_call" | custom-call | tf_op jit(solution)/shard_map/pallas_call | solution.py:551
  4.3 5.1 %collective-permute-start = (f32[40,128]{1,0:T(8,128)S(1)}, f32[40,128]{1,0:T(8,128)S(1)}, u32[]{:S(2)}, u32[]{:S(2)}) collective-permute-start(f32[40,128]{1,0:T(8,128)S(1)} %get-tuple-element.34.r_0_), channel_id=1, source_target_pairs={{4,8},{12,0},{8,4},{0,12},{5,9},{13,1},{9,5},{1,13},{6,10},{14,2},... | collective-permute-start | bytes 61448 | tf_op jit(solution)/shard_map/ppermute | solution.py:490
  9.4 0.0 collective-permute-start.1
  9.4 0.6 %collective-permute-start.2 = (f32[24,128]{1,0:T(8,128)S(1)}, f32[24,128]{1,0:T(8,128)S(1)}, u32[]{:S(2)}, u32[]{:S(2)}) collective-permute-start(f32[24,128]{1,0:T(8,128)S(1)} %get-tuple-element.36.r_2_), channel_id=1, source_target_pairs={{1,2},{3,0},{2,1},{0,3},{5,6},{7,4},{6,5},{4,7},{9,10},{11,8},{10,... | collective-permute-start | bytes 36872 | tf_op jit(solution)/shard_map/ppermute | solution.py:490
  10.1 1.0 %collective-permute-start.3 = (f32[24,128]{1,0:T(8,128)S(1)}, f32[24,128]{1,0:T(8,128)S(1)}, u32[]{:S(2)}, u32[]{:S(2)}) collective-permute-start(f32[24,128]{1,0:T(8,128)S(1)} %get-tuple-element.37.r_3_), channel_id=1, source_target_pairs={{0,1},{2,3},{1,0},{3,2},{4,5},{6,7},{5,4},{7,6},{8,9},{10,11},{9,8... | collective-permute-start | bytes 36872 | tf_op jit(solution)/shard_map/ppermute | solution.py:490
  11.0 0.0 copy-start.5
  11.1 0.0 copy-start.11
  11.1 1.5 %shard_map.159.r_0_ = f32[32,64,128]{2,1,0:T(8,128)S(1)} custom-call(f32[32,64,128]{2,1,0:T(8,128)S(1)} %get-tuple-element.38.base, bf16[256,256]{1,0:T(8,128)(2,1)S(1)} %copy-done.2, bf16[64,192]{1,0:T(8,128)(2,1)S(1)} %copy-done.4), custom_call_target="tpu_custom_call" | custom-call | tf_op jit(solution)/shard_map/pallas_call | solution.py:557
  12.6 0.0 copy-start
  12.6 0.0 copy-start.6
  12.6 0.0 collective-permute-done.2.r_6_
  12.6 0.0 collective-permute-done.3.r_7_
  12.6 0.0 collective-permute-done.r_4_
  12.6 0.6 %collective-permute-done.1.r_5_ = f32[40,128]{1,0:T(8,128)S(1)} collective-permute-done((f32[40,128]{1,0:T(8,128)S(1)}, f32[40,128]{1,0:T(8,128)S(1)}, u32[]{:S(2)}, u32[]{:S(2)}) %collective-permute-start.1) | collective-permute-done | bytes 20512 | tf_op jit(solution)/shard_map/ppermute | solution.py:490
  13.2 0.4 %shard_map.160 = (f32[200,128]{1,0:T(8,128)S(1)}, f32[40,128]{1,0:T(8,128)S(1)}, f32[40,128]{1,0:T(8,128)S(1)}, f32[24,128]{1,0:T(8,128)S(1)}, f32[24,128]{1,0:T(8,128)S(1)}) custom-call(f32[40,128]{1,0:T(8,128)S(1)} %get-tuple-element.34.r_0_, f32[40,128]{1,0:T(8,128)S(1)} %get-tuple-element.35.r_1_, f32[24,128]{1,0:T(8,128)S(1)} %get-tuple-element.36.r_2_, ...), custom_call_target="tpu_custom_call" | custom-call | tf_op jit(solution)/shard_map/pallas_call | solution.py:561
  13.7 0.0 copy-start.9
  13.7 1.9 %collective-permute-start.4 = (f32[40,128]{1,0:T(8,128)S(1)}, f32[40,128]{1,0:T(8,128)S(1)}, u32[]{:S(2)}, u32[]{:S(2)}) collective-permute-start(f32[40,128]{1,0:T(8,128)S(1)} %get-tuple-element.44.r_0_), channel_id=1, source_target_pairs={{4,8},{12,0},{8,4},{0,12},{5,9},{13,1},{9,5},{1,13},{6,10},{14,2},... | collective-permute-start | bytes 61448 | tf_op jit(solution)/shard_map/ppermute | solution.py:490
  15.5 0.0 collective-permute-start.5
  15.6 0.0 collective-permute-start.6
  15.6 1.6 %collective-permute-start.7 = (f32[24,128]{1,0:T(8,128)S(1)}, f32[24,128]{1,0:T(8,128)S(1)}, u32[]{:S(2)}, u32[]{:S(2)}) collective-permute-start(f32[24,128]{1,0:T(8,128)S(1)} %get-tuple-element.47.r_3_), channel_id=1, source_target_pairs={{0,1},{2,3},{1,0},{3,2},{4,5},{6,7},{5,4},{7,6},{8,9},{10,11},{9,8... | collective-permute-start | bytes 36872 | tf_op jit(solution)/shard_map/ppermute | solution.py:490
  17.2 2.3 %shard_map.161.r_1_ = f32[32,64,128]{2,1,0:T(8,128)S(1)} custom-call(f32[200,128]{1,0:T(8,128)S(1)} %get-tuple-element.48.state.r_12_.r_0_, bf16[256,256]{1,0:T(8,128)(2,1)S(1)} %copy-done.2, bf16[64,192]{1,0:T(8,128)(2,1)S(1)} %copy-done.4, f32[32,64,128]{2,1,0:T(8,128)S(1)} %copy-done, f32[64,128]{1,0:T(8,128)S(1)} %copy-done.6, f32[8,128]{1,0:T(8,128)S(1)} %copy-done.9), custom_call_target="tpu_custom_call" | custom-call | tf_op jit(solution)/shard_map/pallas_call | solution.py:565
  19.4 0.0 collective-permute-done.6.r_6_
  19.5 0.0 collective-permute-done.7.r_7_
  19.5 0.0 collective-permute-done.4.r_4_
  19.5 0.1 collective-permute-done.5.r_5_
  19.5 0.4 %shard_map.162 = (f32[200,128]{1,0:T(8,128)S(1)}, f32[40,128]{1,0:T(8,128)S(1)}, f32[40,128]{1,0:T(8,128)S(1)}, f32[24,128]{1,0:T(8,128)S(1)}, f32[24,128]{1,0:T(8,128)S(1)}) custom-call(f32[40,128]{1,0:T(8,128)S(1)} %get-tuple-element.44.r_0_, f32[40,128]{1,0:T(8,128)S(1)} %get-tuple-element.45.r_1_, f32[24,128]{1,0:T(8,128)S(1)} %get-tuple-element.46.r_2_, ...), custom_call_target="tpu_custom_call" | custom-call | tf_op jit(solution)/shard_map/pallas_call | solution.py:567
  20.0 2.0 %collective-permute-start.8 = (f32[40,128]{1,0:T(8,128)S(1)}, f32[40,128]{1,0:T(8,128)S(1)}, u32[]{:S(2)}, u32[]{:S(2)}) collective-permute-start(f32[40,128]{1,0:T(8,128)S(1)} %get-tuple-element.55.r_3_), channel_id=1, source_target_pairs={{0,4},{8,12},{4,0},{12,8},{1,5},{9,13},{5,1},{13,9},{2,6},{10,14},... | collective-permute-start | bytes 61448 | tf_op jit(solution)/shard_map/ppermute | solution.py:490
  22.0 2.0 %collective-permute-start.10 = (f32[40,128]{1,0:T(8,128)S(1)}, f32[40,128]{1,0:T(8,128)S(1)}, u32[]{:S(2)}, u32[]{:S(2)}) collective-permute-start(f32[40,128]{1,0:T(8,128)S(1)} %get-tuple-element.54.r_2_), channel_id=1, source_target_pairs={{4,8},{12,0},{8,4},{0,12},{5,9},{13,1},{9,5},{1,13},{6,10},{14,2},... | collective-permute-start | bytes 61448 | tf_op jit(solution)/shard_map/ppermute | solution.py:490
  24.1 0.0 collective-permute-start.9
  24.1 0.0 collective-permute-start.11
  24.1 0.0 copy-start.7
  24.1 0.0 copy-start.8
  24.1 0.0 copy-start.12
  24.1 2.3 %shard_map.163.r_2_ = f32[32,64,128]{2,1,0:T(8,128)S(1)} custom-call(f32[200,128]{1,0:T(8,128)S(1)} %get-tuple-element.56.state.r_1_, bf16[256,256]{1,0:T(8,128)(2,1)S(1)} %copy-done.2, bf16[64,192]{1,0:T(8,128)(2,1)S(1)} %copy-done.4, f32[32,64,128]{2,1,0:T(8,128)S(1)} %copy-done, f32[64,128]{1,0:T(8,128)S(1)} %copy-done.6, f32[8,128]{1,0:T(8,128)S(1)} %copy-done.9), custom_call_target="tpu_custom_call" | custom-call | tf_op jit(solution)/shard_map/pallas_call | solution.py:570
  26.4 0.0 copy-start.10
  26.4 0.0 collective-permute-done.8.r_6_
  26.4 1.2 %collective-permute-done.10.r_5_ = f32[40,128]{1,0:T(8,128)S(1)} collective-permute-done((f32[40,128]{1,0:T(8,128)S(1)}, f32[40,128]{1,0:T(8,128)S(1)}, u32[]{:S(2)}, u32[]{:S(2)}) %collective-permute-start.10) | collective-permute-done | bytes 20512 | tf_op jit(solution)/shard_map/ppermute | solution.py:490
  27.6 1.1 %collective-permute-done.9 = f32[40,128]{1,0:T(8,128)S(1)} collective-permute-done((f32[40,128]{1,0:T(8,128)S(1)}, f32[40,128]{1,0:T(8,128)S(1)}, u32[]{:S(2)}, u32[]{:S(2)}) %collective-permute-start.9) | collective-permute-done | bytes 20512 | tf_op jit(solution)/shard_map/ppermute | solution.py:484
  28.7 0.0 collective-permute-start.14
  28.7 0.8 %collective-permute-start.13 = (f32[8,128]{1,0:T(8,128)S(1)}, f32[8,128]{1,0:T(8,128)S(1)}, u32[]{:S(2)}, u32[]{:S(2)}) collective-permute-start(f32[8,128]{1,0:T(8,128)S(1)} %add_add_fusion.r_5_), channel_id=1, source_target_pairs={{0,2},{1,3},{2,0},{3,1},{4,6},{5,7},{6,4},{7,5},{8,10},{9,11},{10,... | collective-permute-start | bytes 12296 | tf_op jit(solution)/shard_map/ppermute | solution.py:484
  29.5 1.1 %collective-permute-start.12 = (f32[8,128]{1,0:T(8,128)S(1)}, f32[8,128]{1,0:T(8,128)S(1)}, u32[]{:S(2)}, u32[]{:S(2)}) collective-permute-start(f32[8,128]{1,0:T(8,128)S(1)} %add_add_fusion.r_5_), channel_id=1, source_target_pairs={{0,1},{2,3},{1,0},{3,2},{4,5},{6,7},{5,4},{7,6},{8,9},{10,11},{9,8... | collective-permute-start | bytes 12296 | tf_op jit(solution)/shard_map/ppermute | solution.py:490
  30.6 0.9 %shard_map.164 = (f32[3,32,128]{2,1,0:T(8,128)S(1)}, f32[3,64,128]{2,1,0:T(8,128)S(1)}) custom-call(f32[200,128]{1,0:T(8,128)S(1)} %get-tuple-element.48.state.r_12_.r_0_, f32[200,128]{1,0:T(8,128)S(1)} %get-tuple-element.56.state.r_1_, f32[40,128]{1,0:T(8,128)S(1)} %get-tuple-element.54.r_2_, f32[40,128]{1,0:T(8,128)S(1)} %get-tuple-element.55.r_3_, ...), custom_call_target="tpu_custom_call" | custom-call | tf_op jit(solution)/shard_map/pallas_call | solution.py:573
  31.5 0.2 collective-permute-done.14.r_8_
  31.8 0.6 %collective-permute-done.13.r_7_ = f32[8,128]{1,0:T(8,128)S(1)} collective-permute-done((f32[8,128]{1,0:T(8,128)S(1)}, f32[8,128]{1,0:T(8,128)S(1)}, u32[]{:S(2)}, u32[]{:S(2)}) %collective-permute-start.13) | collective-permute-done | bytes 4128 | tf_op jit(solution)/shard_map/ppermute | solution.py:484
  32.4 0.0 collective-permute-done.12.r_6_
  32.4 1.5 %shard_map.165 = (f32[32,64,128]{2,1,0:T(8,128)}, f32[32,64,128]{2,1,0:T(8,128)}) custom-call(f32[32,64,128]{2,1,0:T(8,128)S(1)} %shard_map.159.r_0_, f32[32,64,128]{2,1,0:T(8,128)S(1)} %shard_map.161.r_1_, f32[32,64,128]{2,1,0:T(8,128)S(1)} %shard_map.163.r_2_, f32[3,32,128]{2,1,0:T(8,128)S(1)} %get-tuple-element.60.r_3_, ...), custom_call_target="tpu_custom_call" | custom-call | tf_op jit(solution)/shard_map/pallas_call | solution.py:576
  (21 shorter events, 0.0 us)
Async XLA Ops:
  0.6 10.4 %copy-start.2 = (bf16[256,256]{1,0:T(8,128)(2,1)S(1)}, bf16[256,256]{1,0:T(8,128)(2,1)}, u32[]{:S(2)}) copy-start(bf16[256,256]{1,0:T(8,128)(2,1)} %constant.26.clone.eyw_h.eyw) | copy-start | bytes 393220
  0.6 10.4 %copy-start.4 = (bf16[64,192]{1,0:T(8,128)(2,1)S(1)}, bf16[64,192]{1,0:T(8,128)(2,1)}, u32[]{:S(2)}) copy-start(bf16[64,192]{1,0:T(8,128)(2,1)} %constant.27.clone.exw_h.exw) | copy-start | bytes 73732
  4.3 8.3 %collective-permute-start = (f32[40,128]{1,0:T(8,128)S(1)}, f32[40,128]{1,0:T(8,128)S(1)}, u32[]{:S(2)}, u32[]{:S(2)}) collective-permute-start(f32[40,128]{1,0:T(8,128)S(1)} %get-tuple-element.34.r_0_), channel_id=1, source_target_pairs={{4,8},{12,0},{8,4},{0,12},{5,9},{13,1},{9,5},{1,13},{6,10},{14,2},... | collective-permute-start | bytes 61448 | tf_op jit(solution)/shard_map/ppermute | solution.py:490
  9.4 3.8 %collective-permute-start.1 = (f32[40,128]{1,0:T(8,128)S(1)}, f32[40,128]{1,0:T(8,128)S(1)}, u32[]{:S(2)}, u32[]{:S(2)}) collective-permute-start(f32[40,128]{1,0:T(8,128)S(1)} %get-tuple-element.35.r_1_), channel_id=1, source_target_pairs={{0,4},{8,12},{4,0},{12,8},{1,5},{9,13},{5,1},{13,9},{2,6},{10,14},... | collective-permute-start | bytes 61448 | tf_op jit(solution)/shard_map/ppermute | solution.py:490
  9.4 3.2 %collective-permute-start.2 = (f32[24,128]{1,0:T(8,128)S(1)}, f32[24,128]{1,0:T(8,128)S(1)}, u32[]{:S(2)}, u32[]{:S(2)}) collective-permute-start(f32[24,128]{1,0:T(8,128)S(1)} %get-tuple-element.36.r_2_), channel_id=1, source_target_pairs={{1,2},{3,0},{2,1},{0,3},{5,6},{7,4},{6,5},{4,7},{9,10},{11,8},{10,... | collective-permute-start | bytes 36872 | tf_op jit(solution)/shard_map/ppermute | solution.py:490
  10.1 2.6 %collective-permute-start.3 = (f32[24,128]{1,0:T(8,128)S(1)}, f32[24,128]{1,0:T(8,128)S(1)}, u32[]{:S(2)}, u32[]{:S(2)}) collective-permute-start(f32[24,128]{1,0:T(8,128)S(1)} %get-tuple-element.37.r_3_), channel_id=1, source_target_pairs={{0,1},{2,3},{1,0},{3,2},{4,5},{6,7},{5,4},{7,6},{8,9},{10,11},{9,8... | collective-permute-start | bytes 36872 | tf_op jit(solution)/shard_map/ppermute | solution.py:490
  11.0 2.2 %copy-start.1 = (f32[32,64,128]{2,1,0:T(8,128)S(1)}, f32[32,64,128]{2,1,0:T(8,128)}, u32[]{:S(2)}) copy-start(f32[32,64,128]{2,1,0:T(8,128)} %constant.33.clone.r_8_) | copy-start | bytes 3145732
  11.0 2.2 %copy-start.3 = (f32[5,64,128]{2,1,0:T(8,128)S(1)}, f32[5,64,128]{2,1,0:T(8,128)}, u32[]{:S(2)}) copy-start(f32[5,64,128]{2,1,0:T(8,128)} %constant.35.clone.r_10_) | copy-start | bytes 491524
  11.0 2.2 %copy-start.5 = (f32[5,32,128]{2,1,0:T(8,128)S(1)}, f32[5,32,128]{2,1,0:T(8,128)}, u32[]{:S(2)}) copy-start(f32[5,32,128]{2,1,0:T(8,128)} %constant.34.clone.r_9_) | copy-start | bytes 245764
  11.1 2.2 %copy-start.11 = (f32[8,128]{1,0:T(8,128)S(1)}, f32[8,128]{1,0:T(8,128)}, u32[]{:S(2)}) copy-start(f32[8,128]{1,0:T(8,128)} %constant.36.clone.r_11_) | copy-start | bytes 12292
  12.6 4.6 %copy-start = (f32[32,64,128]{2,1,0:T(8,128)S(1)}, f32[32,64,128]{2,1,0:T(8,128)}, u32[]{:S(2)}) copy-start(f32[32,64,128]{2,1,0:T(8,128)} %constant.32.clone.inv_h.inv) | copy-start | bytes 3145732
  12.6 4.6 %copy-start.6 = (f32[64,128]{1,0:T(8,128)S(1)}, f32[64,128]{1,0:T(8,128)}, u32[]{:S(2)}) copy-start(f32[64,128]{1,0:T(8,128)} %constant.37.clone.sx0_h.sx0) | copy-start | bytes 98308
  13.7 3.5 %copy-start.9 = (f32[8,128]{1,0:T(8,128)S(1)}, f32[8,128]{1,0:T(8,128)}, u32[]{:S(2)}) copy-start(f32[8,128]{1,0:T(8,128)} %constant.38.clone.sy0_h.sy0) | copy-start | bytes 12292
  13.7 5.8 %collective-permute-start.4 = (f32[40,128]{1,0:T(8,128)S(1)}, f32[40,128]{1,0:T(8,128)S(1)}, u32[]{:S(2)}, u32[]{:S(2)}) collective-permute-start(f32[40,128]{1,0:T(8,128)S(1)} %get-tuple-element.44.r_0_), channel_id=1, source_target_pairs={{4,8},{12,0},{8,4},{0,12},{5,9},{13,1},{9,5},{1,13},{6,10},{14,2},... | collective-permute-start | bytes 61448 | tf_op jit(solution)/shard_map/ppermute | solution.py:490
  15.5 4.0 %collective-permute-start.5 = (f32[40,128]{1,0:T(8,128)S(1)}, f32[40,128]{1,0:T(8,128)S(1)}, u32[]{:S(2)}, u32[]{:S(2)}) collective-permute-start(f32[40,128]{1,0:T(8,128)S(1)} %get-tuple-element.45.r_1_), channel_id=1, source_target_pairs={{0,4},{8,12},{4,0},{12,8},{1,5},{9,13},{5,1},{13,9},{2,6},{10,14},... | collective-permute-start | bytes 61448 | tf_op jit(solution)/shard_map/ppermute | solution.py:490
  15.6 3.9 %collective-permute-start.6 = (f32[24,128]{1,0:T(8,128)S(1)}, f32[24,128]{1,0:T(8,128)S(1)}, u32[]{:S(2)}, u32[]{:S(2)}) collective-permute-start(f32[24,128]{1,0:T(8,128)S(1)} %get-tuple-element.46.r_2_), channel_id=1, source_target_pairs={{1,2},{3,0},{2,1},{0,3},{5,6},{7,4},{6,5},{4,7},{9,10},{11,8},{10,... | collective-permute-start | bytes 36872 | tf_op jit(solution)/shard_map/ppermute | solution.py:490
  15.6 3.9 %collective-permute-start.7 = (f32[24,128]{1,0:T(8,128)S(1)}, f32[24,128]{1,0:T(8,128)S(1)}, u32[]{:S(2)}, u32[]{:S(2)}) collective-permute-start(f32[24,128]{1,0:T(8,128)S(1)} %get-tuple-element.47.r_3_), channel_id=1, source_target_pairs={{0,1},{2,3},{1,0},{3,2},{4,5},{6,7},{5,4},{7,6},{8,9},{10,11},{9,8... | collective-permute-start | bytes 36872 | tf_op jit(solution)/shard_map/ppermute | solution.py:490
  20.0 6.4 %collective-permute-start.8 = (f32[40,128]{1,0:T(8,128)S(1)}, f32[40,128]{1,0:T(8,128)S(1)}, u32[]{:S(2)}, u32[]{:S(2)}) collective-permute-start(f32[40,128]{1,0:T(8,128)S(1)} %get-tuple-element.55.r_3_), channel_id=1, source_target_pairs={{0,4},{8,12},{4,0},{12,8},{1,5},{9,13},{5,1},{13,9},{2,6},{10,14},... | collective-permute-start | bytes 61448 | tf_op jit(solution)/shard_map/ppermute | solution.py:490
  22.0 5.6 %collective-permute-start.10 = (f32[40,128]{1,0:T(8,128)S(1)}, f32[40,128]{1,0:T(8,128)S(1)}, u32[]{:S(2)}, u32[]{:S(2)}) collective-permute-start(f32[40,128]{1,0:T(8,128)S(1)} %get-tuple-element.54.r_2_), channel_id=1, source_target_pairs={{4,8},{12,0},{8,4},{0,12},{5,9},{13,1},{9,5},{1,13},{6,10},{14,2},... | collective-permute-start | bytes 61448 | tf_op jit(solution)/shard_map/ppermute | solution.py:490
  24.1 4.7 %collective-permute-start.9 = (f32[40,128]{1,0:T(8,128)S(1)}, f32[40,128]{1,0:T(8,128)S(1)}, u32[]{:S(2)}, u32[]{:S(2)}) collective-permute-start(f32[40,128]{1,0:T(8,128)S(1)} %get-tuple-element.54.r_2_), channel_id=1, source_target_pairs={{0,8},{4,12},{8,0},{12,4},{1,9},{5,13},{9,1},{13,5},{2,10},{6,14},... | collective-permute-start | bytes 61448 | tf_op jit(solution)/shard_map/ppermute | solution.py:484
  24.1 6.6 %collective-permute-start.11 = (f32[24,128]{1,0:T(8,128)S(1)}, f32[24,128]{1,0:T(8,128)S(1)}, u32[]{:S(2)}, u32[]{:S(2)}) collective-permute-start(f32[24,128]{1,0:T(8,128)S(1)} %get-tuple-element.59), channel_id=1, source_target_pairs={{0,1},{1,2},{2,3},{3,0},{4,5},{5,6},{6,7},{7,4},{8,9},{9,10},{10,1... | collective-permute-start | bytes 36872 | tf_op jit(solution)/shard_map/ppermute | solution.py:484
  24.1 6.5 %copy-start.7 = (f32[128,128]{1,0:T(8,128)S(1)}, f32[128,128]{1,0:T(8,128)}, u32[]{:S(2)}) copy-start(f32[128,128]{1,0:T(8,128)} %constant.31.clone.r_11_) | copy-start | bytes 196612
  24.1 6.5 %copy-start.8 = (f32[128,128]{1,0:T(8,128)S(1)}, f32[128,128]{1,0:T(8,128)}, u32[]{:S(2)}) copy-start(f32[128,128]{1,0:T(8,128)} %constant.28.clone.r_8_) | copy-start | bytes 196612
  24.1 6.5 %copy-start.12 = (f32[32,32]{1,0:T(8,128)S(1)}, f32[32,32]{1,0:T(8,128)}, u32[]{:S(2)}) copy-start(f32[32,32]{1,0:T(8,128)} %constant.30.clone.r_10_) | copy-start | bytes 12292
  26.4 4.3 %copy-start.10 = (f32[64,64]{1,0:T(8,128)S(1)}, f32[64,64]{1,0:T(8,128)}, u32[]{:S(2)}) copy-start(f32[64,64]{1,0:T(8,128)} %constant.29.clone.r_9_) | copy-start | bytes 49156
  28.7 3.0 %collective-permute-start.14 = (f32[8,128]{1,0:T(8,128)S(1)}, f32[8,128]{1,0:T(8,128)S(1)}, u32[]{:S(2)}, u32[]{:S(2)}) collective-permute-start(f32[8,128]{1,0:T(8,128)S(1)} %add_add_fusion.r_5_), channel_id=1, source_target_pairs={{1,2},{3,0},{2,1},{0,3},{5,6},{7,4},{6,5},{4,7},{9,10},{11,8},{10,... | collective-permute-start | bytes 12296 | tf_op jit(solution)/shard_map/ppermute | solution.py:490
  28.7 3.7 %collective-permute-start.13 = (f32[8,128]{1,0:T(8,128)S(1)}, f32[8,128]{1,0:T(8,128)S(1)}, u32[]{:S(2)}, u32[]{:S(2)}) collective-permute-start(f32[8,128]{1,0:T(8,128)S(1)} %add_add_fusion.r_5_), channel_id=1, source_target_pairs={{0,2},{1,3},{2,0},{3,1},{4,6},{5,7},{6,4},{7,5},{8,10},{9,11},{10,... | collective-permute-start | bytes 12296 | tf_op jit(solution)/shard_map/ppermute | solution.py:484
  29.5 2.9 %collective-permute-start.12 = (f32[8,128]{1,0:T(8,128)S(1)}, f32[8,128]{1,0:T(8,128)S(1)}, u32[]{:S(2)}, u32[]{:S(2)}) collective-permute-start(f32[8,128]{1,0:T(8,128)S(1)} %add_add_fusion.r_5_), channel_id=1, source_target_pairs={{0,1},{2,3},{1,0},{3,2},{4,5},{6,7},{5,4},{7,6},{8,9},{10,11},{9,8... | collective-permute-start | bytes 12296 | tf_op jit(solution)/shard_map/ppermute | solution.py:490

commit v4 on v3

--- a/solution.py
+++ b/solution.py
@@ -32,8 +32,17 @@
     tab = {}
     hi, lo = split_bf16(sine_ext(height))
     tab["eyw"] = np.block([[hi, lo], [hi, np.zeros_like(lo)]])
-    hi, lo = split_bf16(sine_ext(width))
+    hi, lo = split_bf16(sine_ext(width) * np.sqrt(2.0 / depth))
     tab["exw"] = np.concatenate([hi, lo, hi], 1)
+    sign = np.where(np.arange(height) % 2 == 1, 1.0, -1.0)
+    unit = (np.arange(height) == 0) * 1.0
+    wide = np.zeros((height, lanes))
+    for g, values in enumerate((1.0 - unit, sign * (1.0 - unit), unit)):
+        wide[:, g * depth:(g + 1) * depth] = values[:, None]
+    tab["rimw"] = np.concatenate([wide, wide], 0).astype(ml_dtypes.bfloat16)
+    wide[0, :depth] = 1.0
+    wide[:, 2 * depth:] = 0.0
+    tab["colw"] = np.concatenate([wide.T, wide.T], 0).astype(ml_dtypes.bfloat16)
     tab["ey"], tab["ex"] = sine_ext(height).astype(np.float32), sine_ext(width).astype(np.float32)
     z = np.arange(depth)
     cos = np.cos(np.pi * np.outer(z + 0.5, z) / depth) * np.sqrt(2.0 / depth)
@@ -54,6 +63,7 @@
     inside = (a[:, None] > 0) & (b[None, :] > 0)
     inv = np.where(inside[None], 1.0 / (lz[:, None, None] + lx[None, :, None] + ly[None, None, :]), 0.0)
     tab["inv"] = inv.astype(np.float32)
+    tab["lxy"] = np.where(inside, lx[:, None] + ly[None, :], 1e30).astype(np.float32)
 
     def to_rows(kb):
         return kb.T.reshape(groups, rows, depth).transpose(1, 0, 2).reshape(rows, lanes)
@@ -81,47 +91,53 @@
         to_cols((lz[:, None] + 2.0 + lx) * (a > 0)),
     ]).astype(np.float32)
     tab["crnt"] = np.tile(np.tile(lz + 4.0, groups)[None], (8, 1)).astype(np.float32)
+    line = np.where(b > 0, sy, 1.0)[None]
+    tab["line"] = np.tile(line, (8, 1)).astype(np.float32)
     tab["sx0"] = np.tile(sx[:, None], (1, height)).astype(np.float32)
-    lane = np.zeros((8, height))
-    lane[0], lane[1] = sy, sy * sgb
-    lane[2], lane[3] = np.where(b > 0, sy, 1.0), sy * sgb
-    tab["sy0"] = lane.astype(np.float32)
     return tab
 
 
-def cosine_fwd(xs, scale):
+def cosine_two(xs):
     n = len(xs)
     if n == 1:
-        return [xs[0] * (scale / np.sqrt(2.0))]
+        return list(xs)
     half = n // 2
-    even = cosine_fwd([xs[j] + xs[n - 1 - j] for j in range(half)], scale)
-    diff = [xs[j] - xs[n - 1 - j] for j in range(half)]
     out = [None] * n
-    for m in range(half):
-        out[2 * m] = even[m]
-        acc = None
-        for j in range(half):
-            term = diff[j] * float(scale * np.cos(np.pi * (2 * m + 1) * (2 * j + 1) / (2 * n)))
-            acc = term if acc is None else acc + term
-        out[2 * m + 1] = acc
+    out[0::2] = cosine_two([xs[j] + xs[n - 1 - j] for j in range(half)])
+    out[1::2] = cosine_four([xs[j] - xs[n - 1 - j] for j in range(half)])
     return out
 
 
-def cosine_back(ys, scale):
+def cosine_three(ys):
     n = len(ys)
     if n == 1:
-        return [ys[0] * (scale / np.sqrt(2.0))]
+        return list(ys)
     half = n // 2
-    even = cosine_back(ys[0::2], scale)
+    even, odd = cosine_three(ys[0::2]), cosine_four(ys[1::2])
+    return [even[j] + odd[j] for j in range(half)] + [even[j] - odd[j] for j in reversed(range(half))]
+
+
+def cosine_four(xs):
+    n = len(xs)
+    if n == 1:
+        return [xs[0] * float(np.cos(np.pi / 4))]
+    half = n // 2
+    plus, minus = [], []
+    for j in range(half):
+        c, s = (float(f(np.pi * (2 * j + 1) / (4 * n))) for f in (np.cos, np.sin))
+        x, y = xs[j], xs[n - 1 - j]
+        plus.append(x * c + y * s)
+        minus.append(x * s - y * c if j % 2 == 0 else y * c - x * s)
+    c, s = cosine_two(plus), cosine_two(minus)[::-1]
     out = [None] * n
-    for j in range(half):
-        acc = None
-        for m in range(half):
-            term = ys[2 * m + 1] * float(scale * np.cos(np.pi * (2 * m + 1) * (2 * j + 1) / (2 * n)))
-            acc = term if acc is None else acc + term
-        out[j] = even[j] + acc
-        out[n - 1 - j] = even[j] - acc
+    out[0], out[n - 1] = c[0], s[half - 1]
+    for k in range(1, half):
+        out[2 * k] = c[k] - s[k - 1]
+        out[2 * k - 1] = c[k] + s[k - 1]
     return out
+
+
+ROOT_HALF = float(np.sqrt(0.5))
 
 
 def halves(x):
@@ -215,36 +231,36 @@
     return jnp.concatenate([body, jnp.concatenate(rows, 0)], 0)
 
 
-def front_kernel(charge_h, surf_h, eyw_h, exw_h, inv_h, sx0_h, sy0_h, base, *rest):
+def front_kernel(charge_h, surf_h, eyw_h, exw_h, lxy_h, sx0_h, rimw_h, line_h, base, *rest):
     msgs = rest[:4]
-    charge, surf, eyw, exw, inv, sx0, sy0, work, part, first, sems = rest[4:]
+    charge, surf, eyw, exw, lxy, sx0, rimw, line, work, inv, rims, part, first, sems = rest[4:]
     depth, width, height = charge.shape
-    scale = np.sqrt(2.0 / depth)
     tiles = width // 8
-    pairs = [(surf_h, surf)]
+    pairs = [(lxy_h, lxy), (surf_h, surf)]
     pairs += [(charge_h.at[:, 8 * i:8 * i + 8, :], charge.at[:, 8 * i:8 * i + 8, :]) for i in range(tiles)]
-    pairs += [(eyw_h, eyw), (exw_h, exw), (sx0_h, sx0), (sy0_h, sy0), (inv_h, inv)]
+    pairs += [(eyw_h, eyw), (exw_h, exw), (sx0_h, sx0), (rimw_h, rimw), (line_h, line)]
     copies = [pltpu.make_async_copy(src, dst, sems.at[i]) for i, (src, dst) in enumerate(pairs)]
     for copy in copies:
         copy.start()
     copies[0].wait()
+    for k in range(depth):
+        inv[k] = 1.0 / (lxy[...] + float(SCREEN + 2.0 - 2.0 * np.cos(np.pi * k / depth)))
+    copies[1].wait()
+
     for i in range(tiles):
-        copies[1 + i].wait()
+        copies[2 + i].wait()
         at = slice(8 * i, 8 * i + 8)
         xs = [charge[z, at, :] for z in range(depth)]
         xs[0] = xs[0] + surf[0, at, :]
         xs[-1] = xs[-1] + surf[1, at, :]
-        for k, value in enumerate(cosine_fwd(xs, scale)):
-            work[k, at, :] = value
-    for copy in copies[1 + tiles:]:
+        for k, value in enumerate(cosine_two(xs)):
+            work[k, at, :] = value * ROOT_HALF if k == 0 else value
+    for copy in copies[2 + tiles:]:
         copy.wait()
-    step = 4
-    for c in range(0, depth, step):
-        block = work[c:c + step].reshape(step * width, height)
-        work[c:c + step] = times_sy(block, eyw[...]).reshape(step, width, height)
+    for c in range(0, depth, 4):
+        block = work[c:c + 4].reshape(4 * width, height)
+        work[c:c + 4] = times_sy(block, eyw[...]).reshape(4, width, height)
     lane = lane_id((width, 128))
-    zero = jnp.zeros((width, 128), F32)
-    near, far, own = zero, zero, zero
     for c in range(0, depth, 2):
         pair = sx_times(exw[...], jnp.concatenate([work[c], work[c + 1]], 1))
         for k in (c, c + 1):
@@ -253,10 +269,16 @@
             base[k] = inner
             first[k] = spec[0:8]
             part[k] = jnp.sum((inner * sx0[...]).reshape(width // 8, 8, height), 0)
-            here = lane % depth == k
-            near = jnp.where(here, jnp.sum(inner * sy0[0:1, :], 1, keepdims=True), near)
-            far = jnp.where(here, jnp.sum(inner * sy0[1:2, :], 1, keepdims=True), far)
-            own = jnp.where(here, spec[:, 0:1], own)
+            hi, lo = halves(jnp.where(lane == 0, spec, inner * line[0:1, :]))
+            rims[k * width:(k + 1) * width, :] = jnp.concatenate([hi, lo], 1)
+    step = 8
+    found = jnp.zeros((width, 128), F32)
+    for c in range(0, depth, step):
+        out = jnp.dot(rims[c * width:(c + step) * width, :], rimw[...], preferred_element_type=F32)
+        for k in range(c, c + step):
+            one = out[(k - c) * width:(k - c + 1) * width]
+            found = jnp.where(lane % depth == k, one, found)
+    near, far, own = (spread(jnp.where(lane // depth == g, found, 0.0), depth) for g in range(3))
     row_near, row_far = sub_sums(part)
     own_t = copies_t(first[:, 0, :])
     corner = own_t[0:1]
@@ -380,10 +402,10 @@
     for c in range(0, depth, step):
         block = work[c:c + step].reshape(step * width, height)
         work[c:c + step] = times_sy(block, eyw).reshape(step, width, height)
-    scale = np.sqrt(2.0 / depth)
     for i in range(width // 8):
         at = slice(8 * i, 8 * i + 8)
-        for z, value in enumerate(cosine_back([work[k, at, :] for k in range(depth)], scale)):
+        ys = [work[k, at, :] for k in range(depth)]
+        for z, value in enumerate(cosine_three([ys[0] * ROOT_HALF] + ys[1:])):
             out[z, at, :] = value
 
 
@@ -391,7 +413,7 @@
     cells_from(out, work, lambda k: base[k], exw[...], eyw[...])
 
 
-def extend_kernel(state, eyw, exw, inv, sx0, sy0, out, work):
+def extend_kernel(state, eyw, exw, inv, sx0, colw, line, out, work):
     depth, width, height = work.shape
     rows = height * depth // 128
     row, row_n, col, col_n, c00 = unpacked_state(state, rows, width)[:5]
@@ -400,16 +422,23 @@
     row_m = rows_back(row - row_n, depth)
     row_full = rows_back(jnp.where(at_zero, c00, row), depth)
     odd = lax.broadcasted_iota(jnp.int32, (8, height), 0) % 2 == 1
-    top = lax.broadcasted_iota(jnp.int32, (width, height), 0) == 0
+    top = lax.broadcasted_iota(jnp.int32, (8, height), 0) == 0
     lane0 = lane_id((width, height)) == 0
-
-    def spectrum(k):
-        pick = jnp.where(odd, row_p[k:k + 1], row_m[k:k + 1])
-        pick = jnp.broadcast_to(pick[None], (width // 8, 8, height)).reshape(width, height)
-        rim = sx0[...] * pick + col[:, k:k + 1] * sy0[2:3, :] + col_n[:, k:k + 1] * sy0[3:4, :]
-        return jnp.where(top, row_full[k:k + 1], jnp.where(lane0, 1.0, inv[k]) * rim)
-
-    cells_from(out, work, spectrum, exw[...], eyw[...])
+    lane = lane_id((width, 256)) % depth
+    hi, lo = halves(by_group([col, col_n] + [jnp.zeros_like(col)] * (128 // depth - 2), depth))
+    both = jnp.concatenate([hi, lo], 1)
+    step = 8
+    for c in range(0, depth, step):
+        rim = jnp.concatenate([jnp.where(lane == k, both, jnp.zeros_like(both)) for k in range(c, c + step)], 0)
+        rim = jnp.dot(rim, colw[...], preferred_element_type=F32)
+        for k in range(c, c + step):
+            side = rim[(k - c) * width:(k - c + 1) * width]
+            pick = jnp.where(odd, row_p[k:k + 1], row_m[k:k + 1])
+            pick = jnp.broadcast_to(pick[None], (width // 8, 8, height)).reshape(width, height)
+            value = jnp.where(lane0, 1.0, inv[k]) * (sx0[...] * pick + side * line[0:1, :])
+            work[k] = value
+            work[k, 0:8, :] = jnp.where(top, row_full[k:k + 1], value[0:8])
+    cells_from(out, work, lambda k: work[k], exw[...], eyw[...])
 
 
 def rims_kernel(depth, s0, s1, bx, ax, py, got_bx, got_ax, from_py, ey, ex, cz, czt, out_rows, out_cols):
@@ -508,7 +537,7 @@
 def reduced_x(bx, ax):
     got_bx, got_ax = swap(bx, "gx", 1), swap(ax, "gx", 0)
     if lax.axis_size("gx") == 4:
-        parts = [bx, got_ax, shifted(bx, "gx", 2), got_bx]
+        parts = [bx, got_ax, shifted(ax, "gx", 2), got_bx]
         parts = [part[-8:] for part in parts]
     else:
         parts = pieces_over(bx[-8:], "gx")
@@ -545,13 +574,14 @@
     block = (depth, width, height)
     anywhere = pl.BlockSpec(memory_space=pltpu.HBM)
     whole = pl.BlockSpec(memory_space=pltpu.VMEM)
-    fronts = (charge, surface_charge) + tuple(tab[n] for n in ("eyw", "exw", "inv", "sx0", "sy0"))
+    fronts = (charge, surface_charge) + tuple(tab[n] for n in ("eyw", "exw", "lxy", "sx0", "rimw", "line"))
     landing = [pltpu.VMEM(x.shape, x.dtype) for x in fronts]
     fronts = [pltpu.with_memory_space_constraint(x, pltpu.HBM) for x in fronts]
     base, *own = call(
         front_kernel, [block] + msgs,
-        landing + [block, (depth, 8, height), (depth, 8, height), pltpu.SemaphoreType.DMA((6 + width // 8,))],
-        in_specs=[anywhere] * 7,
+        landing + [block, block, pltpu.VMEM((depth * width, 2 * height), BF16), (depth, 8, height), (depth, 8, height),
+                   pltpu.SemaphoreType.DMA((7 + width // 8,))],
+        in_specs=[anywhere] * 8,
     )(*fronts)
     got = exchange(*own)
     cells_b = call(base_kernel, [block], [block])(base, tab["eyw"], tab["exw"])[0]
@@ -561,7 +591,7 @@
     s0, *own = call(lambda *r: schur_kernel(depth, False, *r), [state] + msgs, scratch)(*own, *got, *tables)
     got = exchange(*own)
     extend = call(extend_kernel, [block], [block])
-    backs = tuple(tab[n] for n in ("eyw", "exw", "inv", "sx0", "sy0"))
+    backs = tuple(tab[n] for n in ("eyw", "exw", "inv", "sx0", "colw", "line"))
     cells_0 = extend(s0, *backs)[0]
     *got, cells_0 = lax.optimization_barrier((*got, cells_0))
     s1, *own = call(lambda *r: schur_kernel(depth, True, *r), [state] + msgs, scratch)(*own, *got, *tables, s0)

time: 34.1 us -> 32.3 us (0.947)
  Pallas kernels: 13 us -> 10.1 us
  starting transfers between devices: 16.1 us -> 17.1 us
    ppermute x3, starting transfers between devices: 0.76 us -> 2.38 us  [shifted(): return lax.ppermute(value, axis, [(i, (i + by) % n) for i in range(n)])]
    pallas_call x1, Pallas kernels: 2.27 us -> 1.39 us  [on_device(): cells_1 = extend(s1, *backs)[0]]
    pallas_call x1, Pallas kernels: 2.27 us -> 1.4 us  [on_device(): cells_0 = extend(s0, *backs)[0]]
    pallas_call x1, Pallas kernels: 3.64 us -> 2.94 us  [on_device(): call(front_kernel, [block] + msgs, landing + [block, block, pltpu.VMEM((d...]
    ppermute x12, starting transfers between devices: 15.4 us -> 14.7 us  [swap(): return lax.ppermute(value, axis, pairs + [(j, i) for i, j in pairs])]
    pallas_call x1, Pallas kernels: 1.48 us -> 1.03 us  [on_device(): call(base_kernel, [block], [block])(base, tab['eyw'], tab['exw'])[0]]
  transfers between devices with their start and end apart: 15 -> 15, of which waited for: 6 -> 7; matrix products, arithmetic and copies ran while one was open for 0% -> 0% of each run, Pallas kernels for 20% -> 15%
where the time goes in v4:
time: 32.3 us; the launch traced here: 32.2 us
  starting transfers between devices  17.1 us (53%)
  Pallas kernels  10.1 us (31%)
  waiting for transfers between devices  4.08 us (13%)
  between operations  0.86 us (3%)
    ppermute x12, starting transfers between devices, swap(): return lax.ppermute(value, axis, pairs + [(j, i) for i, j in pairs])  14.7 us
    pallas_call x1, Pallas kernels, on_device(): call(front_kernel, [block] + msgs, landing + [block, block, pltpu.VMEM((d...  2.94 us
    ppermute x3, starting transfers between devices, shifted(): return lax.ppermute(value, axis, [(i, (i + by) % n) for i in range(n)])  2.38 us
    ppermute x3, waiting for transfers between devices, shifted(): return lax.ppermute(value, axis, [(i, (i + by) % n) for i in range(n)])  2.05 us
    ppermute x12, waiting for transfers between devices, swap(): return lax.ppermute(value, axis, pairs + [(j, i) for i, j in pairs])  2.02 us
    pallas_call x1, Pallas kernels, on_device(): call(lambda *r: final_kernel(len(parts), *r), [block, block], [block, blo...  1.53 us
    pallas_call x1, Pallas kernels, on_device(): cells_0 = extend(s0, *backs)[0]  1.4 us
    pallas_call x1, Pallas kernels, on_device(): cells_1 = extend(s1, *backs)[0]  1.39 us
  transfers between devices with their start and end apart: 15, of which 7 were waited for; matrix products, arithmetic and copies ran while one was open for 0% of the time, Pallas kernels for 15%

profile of v4, /device:TPU:0, one launch (start us, length us, event | category | flops | bytes accessed | tf_op | source)
XLA Modules:
  0.0 32.2 jit_solution(15865147000366432180)
XLA Ops:
  0.6 0.0 copy-start.2
  0.6 0.0 copy-start.4
  0.7 2.9 %shard_map.185 = (f32[32,64,128]{2,1,0:T(8,128)S(1)}, f32[40,128]{1,0:T(8,128)S(1)}, f32[40,128]{1,0:T(8,128)S(1)}, f32[24,128]{1,0:T(8,128)S(1)}, f32[24,128]{1,0:T(8,128)S(1)}) custom-call(f32[32,64,128]{2,1,0:T(8,128)} %charge_h.1, f32[2,64,128]{2,1,0:T(8,128)} %surf_h.1, bf16[256,256]{1,0:T(8,128)(2,1)} %constant.32.clone.eyw_h.eyw, ...), custom_call_target="tpu_custom_call" | custom-call | tf_op jit(solution)/shard_map/pallas_call | solution.py:580
  3.6 5.1 %collective-permute-start = (f32[40,128]{1,0:T(8,128)S(1)}, f32[40,128]{1,0:T(8,128)S(1)}, u32[]{:S(2)}, u32[]{:S(2)}) collective-permute-start(f32[40,128]{1,0:T(8,128)S(1)} %get-tuple-element.34.r_0_), channel_id=1, source_target_pairs={{4,8},{12,0},{8,4},{0,12},{5,9},{13,1},{9,5},{1,13},{6,10},{14,2},... | collective-permute-start | bytes 61448 | tf_op jit(solution)/shard_map/ppermute | solution.py:519
  8.7 0.0 collective-permute-start.1
  8.7 0.7 %collective-permute-start.2 = (f32[24,128]{1,0:T(8,128)S(1)}, f32[24,128]{1,0:T(8,128)S(1)}, u32[]{:S(2)}, u32[]{:S(2)}) collective-permute-start(f32[24,128]{1,0:T(8,128)S(1)} %get-tuple-element.36.r_2_), channel_id=1, source_target_pairs={{1,2},{3,0},{2,1},{0,3},{5,6},{7,4},{6,5},{4,7},{9,10},{11,8},{10,... | collective-permute-start | bytes 36872 | tf_op jit(solution)/shard_map/ppermute | solution.py:519
  9.4 1.0 %collective-permute-start.3 = (f32[24,128]{1,0:T(8,128)S(1)}, f32[24,128]{1,0:T(8,128)S(1)}, u32[]{:S(2)}, u32[]{:S(2)}) collective-permute-start(f32[24,128]{1,0:T(8,128)S(1)} %get-tuple-element.37.r_3_), channel_id=1, source_target_pairs={{0,1},{2,3},{1,0},{3,2},{4,5},{6,7},{5,4},{7,6},{8,9},{10,11},{9,8... | collective-permute-start | bytes 36872 | tf_op jit(solution)/shard_map/ppermute | solution.py:519
  10.3 0.0 copy-start.5
  10.4 0.0 copy-start.12
  10.4 1.0 %shard_map.186.r_0_ = f32[32,64,128]{2,1,0:T(8,128)S(1)} custom-call(f32[32,64,128]{2,1,0:T(8,128)S(1)} %get-tuple-element.38.base, bf16[256,256]{1,0:T(8,128)(2,1)S(1)} %copy-done.2, bf16[64,192]{1,0:T(8,128)(2,1)S(1)} %copy-done.4), custom_call_target="tpu_custom_call" | custom-call | tf_op jit(solution)/shard_map/pallas_call | solution.py:587
  11.4 0.0 copy-start
  11.4 0.0 copy-start.6
  11.4 0.0 copy-start.7
  11.5 0.5 %collective-permute-done.2.r_6_ = f32[24,128]{1,0:T(8,128)S(1)} collective-permute-done((f32[24,128]{1,0:T(8,128)S(1)}, f32[24,128]{1,0:T(8,128)S(1)}, u32[]{:S(2)}, u32[]{:S(2)}) %collective-permute-start.2) | collective-permute-done | bytes 12320 | tf_op jit(solution)/shard_map/ppermute | solution.py:519
  11.9 0.0 collective-permute-done.3.r_7_
  11.9 0.0 collective-permute-done.r_4_
  11.9 0.6 %collective-permute-done.1.r_5_ = f32[40,128]{1,0:T(8,128)S(1)} collective-permute-done((f32[40,128]{1,0:T(8,128)S(1)}, f32[40,128]{1,0:T(8,128)S(1)}, u32[]{:S(2)}, u32[]{:S(2)}) %collective-permute-start.1) | collective-permute-done | bytes 20512 | tf_op jit(solution)/shard_map/ppermute | solution.py:519
  12.5 0.4 %shard_map.187 = (f32[200,128]{1,0:T(8,128)S(1)}, f32[40,128]{1,0:T(8,128)S(1)}, f32[40,128]{1,0:T(8,128)S(1)}, f32[24,128]{1,0:T(8,128)S(1)}, f32[24,128]{1,0:T(8,128)S(1)}) custom-call(f32[40,128]{1,0:T(8,128)S(1)} %get-tuple-element.34.r_0_, f32[40,128]{1,0:T(8,128)S(1)} %get-tuple-element.35.r_1_, f32[24,128]{1,0:T(8,128)S(1)} %get-tuple-element.36.r_2_, ...), custom_call_target="tpu_custom_call" | custom-call | tf_op jit(solution)/shard_map/pallas_call | solution.py:591
  13.0 0.0 copy-start.10
  13.0 1.9 %collective-permute-start.4 = (f32[40,128]{1,0:T(8,128)S(1)}, f32[40,128]{1,0:T(8,128)S(1)}, u32[]{:S(2)}, u32[]{:S(2)}) collective-permute-start(f32[40,128]{1,0:T(8,128)S(1)} %get-tuple-element.44.r_0_), channel_id=1, source_target_pairs={{4,8},{12,0},{8,4},{0,12},{5,9},{13,1},{9,5},{1,13},{6,10},{14,2},... | collective-permute-start | bytes 61448 | tf_op jit(solution)/shard_map/ppermute | solution.py:519
  14.8 0.0 collective-permute-start.5
  14.8 0.0 collective-permute-start.6
  14.9 1.6 %collective-permute-start.7 = (f32[24,128]{1,0:T(8,128)S(1)}, f32[24,128]{1,0:T(8,128)S(1)}, u32[]{:S(2)}, u32[]{:S(2)}) collective-permute-start(f32[24,128]{1,0:T(8,128)S(1)} %get-tuple-element.47.r_3_), channel_id=1, source_target_pairs={{0,1},{2,3},{1,0},{3,2},{4,5},{6,7},{5,4},{7,6},{8,9},{10,11},{9,8... | collective-permute-start | bytes 36872 | tf_op jit(solution)/shard_map/ppermute | solution.py:519
  16.5 1.4 %shard_map.188.r_1_ = f32[32,64,128]{2,1,0:T(8,128)S(1)} custom-call(f32[200,128]{1,0:T(8,128)S(1)} %get-tuple-element.48.state.r_12_.r_0_, bf16[256,256]{1,0:T(8,128)(2,1)S(1)} %copy-done.2, bf16[64,192]{1,0:T(8,128)(2,1)S(1)} %copy-done.4, f32[32,64,128]{2,1,0:T(8,128)S(1)} %copy-done, f32[64,128]{1,0:T(8,128)S(1)} %copy-done.6, ...), custom_call_target="tpu_custom_call" | custom-call | tf_op jit(solution)/shard_map/pallas_call | solution.py:595
  17.9 0.2 collective-permute-done.6.r_6_
  18.1 0.0 collective-permute-done.7.r_7_
  18.1 0.6 %collective-permute-done.4.r_4_ = f32[40,128]{1,0:T(8,128)S(1)} collective-permute-done((f32[40,128]{1,0:T(8,128)S(1)}, f32[40,128]{1,0:T(8,128)S(1)}, u32[]{:S(2)}, u32[]{:S(2)}) %collective-permute-start.4) | collective-permute-done | bytes 20512 | tf_op jit(solution)/shard_map/ppermute | solution.py:519
  18.6 0.2 collective-permute-done.5.r_5_
  18.8 0.4 %shard_map.189 = (f32[200,128]{1,0:T(8,128)S(1)}, f32[40,128]{1,0:T(8,128)S(1)}, f32[40,128]{1,0:T(8,128)S(1)}, f32[24,128]{1,0:T(8,128)S(1)}, f32[24,128]{1,0:T(8,128)S(1)}) custom-call(f32[40,128]{1,0:T(8,128)S(1)} %get-tuple-element.44.r_0_, f32[40,128]{1,0:T(8,128)S(1)} %get-tuple-element.45.r_1_, f32[24,128]{1,0:T(8,128)S(1)} %get-tuple-element.46.r_2_, ...), custom_call_target="tpu_custom_call" | custom-call | tf_op jit(solution)/shard_map/pallas_call | solution.py:597
  19.3 1.9 %collective-permute-start.10 = (f32[40,128]{1,0:T(8,128)S(1)}, f32[40,128]{1,0:T(8,128)S(1)}, u32[]{:S(2)}, u32[]{:S(2)}) collective-permute-start(f32[40,128]{1,0:T(8,128)S(1)} %get-tuple-element.54.r_2_), channel_id=1, source_target_pairs={{4,8},{12,0},{8,4},{0,12},{5,9},{13,1},{9,5},{1,13},{6,10},{14,2},... | collective-permute-start | bytes 61448 | tf_op jit(solution)/shard_map/ppermute | solution.py:519
  21.2 0.9 %collective-permute-start.9 = (f32[40,128]{1,0:T(8,128)S(1)}, f32[40,128]{1,0:T(8,128)S(1)}, u32[]{:S(2)}, u32[]{:S(2)}) collective-permute-start(f32[40,128]{1,0:T(8,128)S(1)} %get-tuple-element.55.r_3_), channel_id=1, source_target_pairs={{0,8},{4,12},{8,0},{12,4},{1,9},{5,13},{9,1},{13,5},{2,10},{6,14},... | collective-permute-start | bytes 61448 | tf_op jit(solution)/shard_map/ppermute | solution.py:513
  22.1 1.7 %collective-permute-start.8 = (f32[40,128]{1,0:T(8,128)S(1)}, f32[40,128]{1,0:T(8,128)S(1)}, u32[]{:S(2)}, u32[]{:S(2)}) collective-permute-start(f32[40,128]{1,0:T(8,128)S(1)} %get-tuple-element.55.r_3_), channel_id=1, source_target_pairs={{0,4},{8,12},{4,0},{12,8},{1,5},{9,13},{5,1},{13,9},{2,6},{10,14},... | collective-permute-start | bytes 61448 | tf_op jit(solution)/shard_map/ppermute | solution.py:519
  23.7 0.0 collective-permute-start.11
  23.8 0.0 copy-start.13
  23.8 1.4 %shard_map.190.r_2_ = f32[32,64,128]{2,1,0:T(8,128)S(1)} custom-call(f32[200,128]{1,0:T(8,128)S(1)} %get-tuple-element.56.state.r_1_, bf16[256,256]{1,0:T(8,128)(2,1)S(1)} %copy-done.2, bf16[64,192]{1,0:T(8,128)(2,1)S(1)} %copy-done.4, f32[32,64,128]{2,1,0:T(8,128)S(1)} %copy-done, f32[64,128]{1,0:T(8,128)S(1)} %copy-done.6, bf16[256,128]{1,0:T(8,128)(2,1)S(1)} %copy-done.7, ...), custom_call_target="tpu_custom_call" | custom-call | tf_op jit(solution)/shard_map/pallas_call | solution.py:600
  25.2 0.0 copy-start.11
  25.2 0.0 collective-permute-done.10.r_5_
  25.2 0.9 %collective-permute-done.9 = f32[40,128]{1,0:T(8,128)S(1)} collective-permute-done((f32[40,128]{1,0:T(8,128)S(1)}, f32[40,128]{1,0:T(8,128)S(1)}, u32[]{:S(2)}, u32[]{:S(2)}) %collective-permute-start.9) | collective-permute-done | bytes 20512 | tf_op jit(solution)/shard_map/ppermute | solution.py:513
  26.1 0.0 collective-permute-done.8.r_6_
  26.1 1.0 %collective-permute-start.14 = (f32[8,128]{1,0:T(8,128)S(1)}, f32[8,128]{1,0:T(8,128)S(1)}, u32[]{:S(2)}, u32[]{:S(2)}) collective-permute-start(f32[8,128]{1,0:T(8,128)S(1)} %add_add_fusion.r_5_), channel_id=1, source_target_pairs={{1,2},{3,0},{2,1},{0,3},{5,6},{7,4},{6,5},{4,7},{9,10},{11,8},{10,... | collective-permute-start | bytes 12296 | tf_op jit(solution)/shard_map/ppermute | solution.py:519
  27.1 1.5 %collective-permute-start.13 = (f32[8,128]{1,0:T(8,128)S(1)}, f32[8,128]{1,0:T(8,128)S(1)}, u32[]{:S(2)}, u32[]{:S(2)}) collective-permute-start(f32[8,128]{1,0:T(8,128)S(1)} %add_add_fusion.r_5_), channel_id=1, source_target_pairs={{0,2},{1,3},{2,0},{3,1},{4,6},{5,7},{6,4},{7,5},{8,10},{9,11},{10,... | collective-permute-start | bytes 12296 | tf_op jit(solution)/shard_map/ppermute | solution.py:513
  28.5 0.0 collective-permute-start.12
  28.5 0.0 collective-permute-done.11.r_7_
  28.6 0.9 %shard_map.191 = (f32[3,32,128]{2,1,0:T(8,128)S(1)}, f32[3,64,128]{2,1,0:T(8,128)S(1)}) custom-call(f32[200,128]{1,0:T(8,128)S(1)} %get-tuple-element.48.state.r_12_.r_0_, f32[200,128]{1,0:T(8,128)S(1)} %get-tuple-element.56.state.r_1_, f32[40,128]{1,0:T(8,128)S(1)} %get-tuple-element.54.r_2_, f32[40,128]{1,0:T(8,128)S(1)} %get-tuple-element.55.r_3_, ...), custom_call_target="tpu_custom_call" | custom-call | tf_op jit(solution)/shard_map/pallas_call | solution.py:603
  29.5 0.0 collective-permute-done.14.r_8_
  29.5 1.2 %collective-permute-done.13.r_7_ = f32[8,128]{1,0:T(8,128)S(1)} collective-permute-done((f32[8,128]{1,0:T(8,128)S(1)}, f32[8,128]{1,0:T(8,128)S(1)}, u32[]{:S(2)}, u32[]{:S(2)}) %collective-permute-start.13) | collective-permute-done | bytes 4128 | tf_op jit(solution)/shard_map/ppermute | solution.py:513
  30.7 0.0 collective-permute-done.12.r_6_
  30.7 1.5 %shard_map.192 = (f32[32,64,128]{2,1,0:T(8,128)}, f32[32,64,128]{2,1,0:T(8,128)}) custom-call(f32[32,64,128]{2,1,0:T(8,128)S(1)} %shard_map.186.r_0_, f32[32,64,128]{2,1,0:T(8,128)S(1)} %shard_map.188.r_1_, f32[32,64,128]{2,1,0:T(8,128)S(1)} %shard_map.190.r_2_, f32[3,32,128]{2,1,0:T(8,128)S(1)} %get-tuple-element.60.r_3_, ...), custom_call_target="tpu_custom_call" | custom-call | tf_op jit(solution)/shard_map/pallas_call | solution.py:606
  (23 shorter events, 0.1 us)
Async XLA Ops:
  0.6 9.7 %copy-start.2 = (bf16[256,256]{1,0:T(8,128)(2,1)S(1)}, bf16[256,256]{1,0:T(8,128)(2,1)}, u32[]{:S(2)}) copy-start(bf16[256,256]{1,0:T(8,128)(2,1)} %constant.32.clone.eyw_h.eyw) | copy-start | bytes 393220
  0.6 9.7 %copy-start.4 = (bf16[64,192]{1,0:T(8,128)(2,1)S(1)}, bf16[64,192]{1,0:T(8,128)(2,1)}, u32[]{:S(2)}) copy-start(bf16[64,192]{1,0:T(8,128)(2,1)} %constant.33.clone.exw_h.exw) | copy-start | bytes 73732
  3.6 8.3 %collective-permute-start = (f32[40,128]{1,0:T(8,128)S(1)}, f32[40,128]{1,0:T(8,128)S(1)}, u32[]{:S(2)}, u32[]{:S(2)}) collective-permute-start(f32[40,128]{1,0:T(8,128)S(1)} %get-tuple-element.34.r_0_), channel_id=1, source_target_pairs={{4,8},{12,0},{8,4},{0,12},{5,9},{13,1},{9,5},{1,13},{6,10},{14,2},... | collective-permute-start | bytes 61448 | tf_op jit(solution)/shard_map/ppermute | solution.py:519
  8.7 3.8 %collective-permute-start.1 = (f32[40,128]{1,0:T(8,128)S(1)}, f32[40,128]{1,0:T(8,128)S(1)}, u32[]{:S(2)}, u32[]{:S(2)}) collective-permute-start(f32[40,128]{1,0:T(8,128)S(1)} %get-tuple-element.35.r_1_), channel_id=1, source_target_pairs={{0,4},{8,12},{4,0},{12,8},{1,5},{9,13},{5,1},{13,9},{2,6},{10,14},... | collective-permute-start | bytes 61448 | tf_op jit(solution)/shard_map/ppermute | solution.py:519
  8.7 3.2 %collective-permute-start.2 = (f32[24,128]{1,0:T(8,128)S(1)}, f32[24,128]{1,0:T(8,128)S(1)}, u32[]{:S(2)}, u32[]{:S(2)}) collective-permute-start(f32[24,128]{1,0:T(8,128)S(1)} %get-tuple-element.36.r_2_), channel_id=1, source_target_pairs={{1,2},{3,0},{2,1},{0,3},{5,6},{7,4},{6,5},{4,7},{9,10},{11,8},{10,... | collective-permute-start | bytes 36872 | tf_op jit(solution)/shard_map/ppermute | solution.py:519
  9.4 2.6 %collective-permute-start.3 = (f32[24,128]{1,0:T(8,128)S(1)}, f32[24,128]{1,0:T(8,128)S(1)}, u32[]{:S(2)}, u32[]{:S(2)}) collective-permute-start(f32[24,128]{1,0:T(8,128)S(1)} %get-tuple-element.37.r_3_), channel_id=1, source_target_pairs={{0,1},{2,3},{1,0},{3,2},{4,5},{6,7},{5,4},{7,6},{8,9},{10,11},{9,8... | collective-permute-start | bytes 36872 | tf_op jit(solution)/shard_map/ppermute | solution.py:519
  10.3 2.2 %copy-start.1 = (f32[32,64,128]{2,1,0:T(8,128)S(1)}, f32[32,64,128]{2,1,0:T(8,128)}, u32[]{:S(2)}) copy-start(f32[32,64,128]{2,1,0:T(8,128)} %constant.42.clone.r_8_) | copy-start | bytes 3145732
  10.3 2.2 %copy-start.3 = (f32[5,64,128]{2,1,0:T(8,128)S(1)}, f32[5,64,128]{2,1,0:T(8,128)}, u32[]{:S(2)}) copy-start(f32[5,64,128]{2,1,0:T(8,128)} %constant.44.clone.r_10_) | copy-start | bytes 491524
  10.3 2.2 %copy-start.5 = (f32[5,32,128]{2,1,0:T(8,128)S(1)}, f32[5,32,128]{2,1,0:T(8,128)}, u32[]{:S(2)}) copy-start(f32[5,32,128]{2,1,0:T(8,128)} %constant.43.clone.r_9_) | copy-start | bytes 245764
  10.4 2.2 %copy-start.12 = (f32[8,128]{1,0:T(8,128)S(1)}, f32[8,128]{1,0:T(8,128)}, u32[]{:S(2)}) copy-start(f32[8,128]{1,0:T(8,128)} %constant.45.clone.r_11_) | copy-start | bytes 12292
  11.4 5.0 %copy-start = (f32[32,64,128]{2,1,0:T(8,128)S(1)}, f32[32,64,128]{2,1,0:T(8,128)}, u32[]{:S(2)}) copy-start(f32[32,64,128]{2,1,0:T(8,128)} %constant.40.clone.inv) | copy-start | bytes 3145732
  11.4 5.0 %copy-start.6 = (f32[64,128]{1,0:T(8,128)S(1)}, f32[64,128]{1,0:T(8,128)}, u32[]{:S(2)}) copy-start(f32[64,128]{1,0:T(8,128)} %constant.47.clone.sx0_h.sx0) | copy-start | bytes 98308
  11.4 5.0 %copy-start.7 = (bf16[256,128]{1,0:T(8,128)(2,1)S(1)}, bf16[256,128]{1,0:T(8,128)(2,1)}, u32[]{:S(2)}) copy-start(bf16[256,128]{1,0:T(8,128)(2,1)} %constant.35.clone.colw) | copy-start | bytes 196612
  13.0 3.5 %copy-start.10 = (f32[8,128]{1,0:T(8,128)S(1)}, f32[8,128]{1,0:T(8,128)}, u32[]{:S(2)}) copy-start(f32[8,128]{1,0:T(8,128)} %constant.46.clone.line_h.line) | copy-start | bytes 12292
  13.0 5.7 %collective-permute-start.4 = (f32[40,128]{1,0:T(8,128)S(1)}, f32[40,128]{1,0:T(8,128)S(1)}, u32[]{:S(2)}, u32[]{:S(2)}) collective-permute-start(f32[40,128]{1,0:T(8,128)S(1)} %get-tuple-element.44.r_0_), channel_id=1, source_target_pairs={{4,8},{12,0},{8,4},{0,12},{5,9},{13,1},{9,5},{1,13},{6,10},{14,2},... | collective-permute-start | bytes 61448 | tf_op jit(solution)/shard_map/ppermute | solution.py:519
  14.8 4.0 %collective-permute-start.5 = (f32[40,128]{1,0:T(8,128)S(1)}, f32[40,128]{1,0:T(8,128)S(1)}, u32[]{:S(2)}, u32[]{:S(2)}) collective-permute-start(f32[40,128]{1,0:T(8,128)S(1)} %get-tuple-element.45.r_1_), channel_id=1, source_target_pairs={{0,4},{8,12},{4,0},{12,8},{1,5},{9,13},{5,1},{13,9},{2,6},{10,14},... | collective-permute-start | bytes 61448 | tf_op jit(solution)/shard_map/ppermute | solution.py:519
  14.8 3.2 %collective-permute-start.6 = (f32[24,128]{1,0:T(8,128)S(1)}, f32[24,128]{1,0:T(8,128)S(1)}, u32[]{:S(2)}, u32[]{:S(2)}) collective-permute-start(f32[24,128]{1,0:T(8,128)S(1)} %get-tuple-element.46.r_2_), channel_id=1, source_target_pairs={{1,2},{3,0},{2,1},{0,3},{5,6},{7,4},{6,5},{4,7},{9,10},{11,8},{10,... | collective-permute-start | bytes 36872 | tf_op jit(solution)/shard_map/ppermute | solution.py:519
  14.9 3.2 %collective-permute-start.7 = (f32[24,128]{1,0:T(8,128)S(1)}, f32[24,128]{1,0:T(8,128)S(1)}, u32[]{:S(2)}, u32[]{:S(2)}) collective-permute-start(f32[24,128]{1,0:T(8,128)S(1)} %get-tuple-element.47.r_3_), channel_id=1, source_target_pairs={{0,1},{2,3},{1,0},{3,2},{4,5},{6,7},{5,4},{7,6},{8,9},{10,11},{9,8... | collective-permute-start | bytes 36872 | tf_op jit(solution)/shard_map/ppermute | solution.py:519
  19.3 5.9 %collective-permute-start.10 = (f32[40,128]{1,0:T(8,128)S(1)}, f32[40,128]{1,0:T(8,128)S(1)}, u32[]{:S(2)}, u32[]{:S(2)}) collective-permute-start(f32[40,128]{1,0:T(8,128)S(1)} %get-tuple-element.54.r_2_), channel_id=1, source_target_pairs={{4,8},{12,0},{8,4},{0,12},{5,9},{13,1},{9,5},{1,13},{6,10},{14,2},... | collective-permute-start | bytes 61448 | tf_op jit(solution)/shard_map/ppermute | solution.py:519
  21.2 4.9 %collective-permute-start.9 = (f32[40,128]{1,0:T(8,128)S(1)}, f32[40,128]{1,0:T(8,128)S(1)}, u32[]{:S(2)}, u32[]{:S(2)}) collective-permute-start(f32[40,128]{1,0:T(8,128)S(1)} %get-tuple-element.55.r_3_), channel_id=1, source_target_pairs={{0,8},{4,12},{8,0},{12,4},{1,9},{5,13},{9,1},{13,5},{2,10},{6,14},... | collective-permute-start | bytes 61448 | tf_op jit(solution)/shard_map/ppermute | solution.py:513
  22.1 4.0 %collective-permute-start.8 = (f32[40,128]{1,0:T(8,128)S(1)}, f32[40,128]{1,0:T(8,128)S(1)}, u32[]{:S(2)}, u32[]{:S(2)}) collective-permute-start(f32[40,128]{1,0:T(8,128)S(1)} %get-tuple-element.55.r_3_), channel_id=1, source_target_pairs={{0,4},{8,12},{4,0},{12,8},{1,5},{9,13},{5,1},{13,9},{2,6},{10,14},... | collective-permute-start | bytes 61448 | tf_op jit(solution)/shard_map/ppermute | solution.py:519
  23.7 4.8 %collective-permute-start.11 = (f32[24,128]{1,0:T(8,128)S(1)}, f32[24,128]{1,0:T(8,128)S(1)}, u32[]{:S(2)}, u32[]{:S(2)}) collective-permute-start(f32[24,128]{1,0:T(8,128)S(1)} %get-tuple-element.59), channel_id=1, source_target_pairs={{0,1},{1,2},{2,3},{3,0},{4,5},{5,6},{6,7},{7,4},{8,9},{9,10},{10,1... | collective-permute-start | bytes 36872 | tf_op jit(solution)/shard_map/ppermute | solution.py:513
  23.7 4.8 %copy-start.8 = (f32[128,128]{1,0:T(8,128)S(1)}, f32[128,128]{1,0:T(8,128)}, u32[]{:S(2)}) copy-start(f32[128,128]{1,0:T(8,128)} %constant.39.clone.r_11_) | copy-start | bytes 196612
  23.7 4.8 %copy-start.9 = (f32[128,128]{1,0:T(8,128)S(1)}, f32[128,128]{1,0:T(8,128)}, u32[]{:S(2)}) copy-start(f32[128,128]{1,0:T(8,128)} %constant.36.clone.r_8_) | copy-start | bytes 196612
  23.8 4.8 %copy-start.13 = (f32[32,32]{1,0:T(8,128)S(1)}, f32[32,32]{1,0:T(8,128)}, u32[]{:S(2)}) copy-start(f32[32,32]{1,0:T(8,128)} %constant.38.clone.r_10_) | copy-start | bytes 12292
  25.2 3.4 %copy-start.11 = (f32[64,64]{1,0:T(8,128)S(1)}, f32[64,64]{1,0:T(8,128)}, u32[]{:S(2)}) copy-start(f32[64,64]{1,0:T(8,128)} %constant.37.clone.r_9_) | copy-start | bytes 49156
  26.1 3.4 %collective-permute-start.14 = (f32[8,128]{1,0:T(8,128)S(1)}, f32[8,128]{1,0:T(8,128)S(1)}, u32[]{:S(2)}, u32[]{:S(2)}) collective-permute-start(f32[8,128]{1,0:T(8,128)S(1)} %add_add_fusion.r_5_), channel_id=1, source_target_pairs={{1,2},{3,0},{2,1},{0,3},{5,6},{7,4},{6,5},{4,7},{9,10},{11,8},{10,... | collective-permute-start | bytes 12296 | tf_op jit(solution)/shard_map/ppermute | solution.py:519
  27.1 3.6 %collective-permute-start.13 = (f32[8,128]{1,0:T(8,128)S(1)}, f32[8,128]{1,0:T(8,128)S(1)}, u32[]{:S(2)}, u32[]{:S(2)}) collective-permute-start(f32[8,128]{1,0:T(8,128)S(1)} %add_add_fusion.r_5_), channel_id=1, source_target_pairs={{0,2},{1,3},{2,0},{3,1},{4,6},{5,7},{6,4},{7,5},{8,10},{9,11},{10,... | collective-permute-start | bytes 12296 | tf_op jit(solution)/shard_map/ppermute | solution.py:513
  28.5 2.1 %collective-permute-start.12 = (f32[8,128]{1,0:T(8,128)S(1)}, f32[8,128]{1,0:T(8,128)S(1)}, u32[]{:S(2)}, u32[]{:S(2)}) collective-permute-start(f32[8,128]{1,0:T(8,128)S(1)} %add_add_fusion.r_5_), channel_id=1, source_target_pairs={{0,1},{2,3},{1,0},{3,2},{4,5},{6,7},{5,4},{7,6},{8,9},{10,11},{9,8... | collective-permute-start | bytes 12296 | tf_op jit(solution)/shard_map/ppermute | solution.py:519

commit v5 on v4

--- a/solution.py
+++ b/solution.py
@@ -33,7 +33,8 @@
     hi, lo = split_bf16(sine_ext(height))
     tab["eyw"] = np.block([[hi, lo], [hi, np.zeros_like(lo)]])
     hi, lo = split_bf16(sine_ext(width) * np.sqrt(2.0 / depth))
-    tab["exw"] = np.concatenate([hi, lo, hi], 1)
+    half = np.block([[hi, hi], [lo, np.zeros_like(lo)]])
+    tab["exw"] = np.block([[half, np.zeros_like(half)], [np.zeros_like(half), half]])
     sign = np.where(np.arange(height) % 2 == 1, 1.0, -1.0)
     unit = (np.arange(height) == 0) * 1.0
     wide = np.zeros((height, lanes))
@@ -152,9 +153,18 @@
     return out[:, :n] + out[:, n:]
 
 
-def sx_times(exw, x):
-    hi, lo = halves(x)
-    return jnp.dot(exw, jnp.concatenate([hi, hi, lo], 0), preferred_element_type=F32)
+def sx_times(exw, xs):
+    n = xs[0].shape[0]
+    rhs = []
+    for x in (jnp.concatenate(xs[:2], 1), jnp.concatenate(xs[2:], 1)):
+        rhs += list(halves(x))
+    out = jnp.dot(exw, jnp.concatenate(rhs, 0), preferred_element_type=F32)
+    width = xs[0].shape[1]
+    res = []
+    for pair in range(2):
+        both = out[2 * pair * n:(2 * pair + 1) * n] + out[(2 * pair + 1) * n:(2 * pair + 2) * n]
+        res += [both[:, :width], both[:, width:]]
+    return res
 
 
 def lane_id(shape):
@@ -261,10 +271,9 @@
         block = work[c:c + 4].reshape(4 * width, height)
         work[c:c + 4] = times_sy(block, eyw[...]).reshape(4, width, height)
     lane = lane_id((width, 128))
-    for c in range(0, depth, 2):
-        pair = sx_times(exw[...], jnp.concatenate([work[c], work[c + 1]], 1))
-        for k in (c, c + 1):
-            spec = pair[:, (k - c) * height:(k - c + 1) * height]
+    for c in range(0, depth, 4):
+        specs = sx_times(exw[...], [work[k] for k in range(c, c + 4)])
+        for k, spec in zip(range(c, c + 4), specs):
             inner = spec * inv[k]
             base[k] = inner
             first[k] = spec[0:8]
@@ -394,10 +403,9 @@
 
 def cells_from(out, work, spectrum, exw, eyw):
     depth, width, height = work.shape
-    for c in range(0, depth, 2):
-        pair = sx_times(exw, jnp.concatenate([spectrum(c), spectrum(c + 1)], 1))
-        work[c] = pair[:, :height]
-        work[c + 1] = pair[:, height:]
+    for c in range(0, depth, 4):
+        for k, cells in zip(range(c, c + 4), sx_times(exw, [spectrum(k) for k in range(c, c + 4)])):
+            work[k] = cells
     step = 4
     for c in range(0, depth, step):
         block = work[c:c + step].reshape(step * width, height)
@@ -488,22 +496,26 @@
     c1 = jnp.where(fine, (n1 * n1 - n2) / safe, 0.0)
     rim_row = in_rows[0] - c0 * in_rows[1] - c1 * in_rows[2]
     rim_col = in_cols[0] - c0 * in_cols[1] - c1 * in_cols[2]
-    top = lax.broadcasted_iota(jnp.int32, (width, height), 0) == 0
+    top = lax.broadcasted_iota(jnp.int32, (8, height), 0) == 0
     lane0 = lane_id((width, height)) == 0
     step = depth // 4
     copies = []
+
+    def send(src, dst, c):
+        at = slice(c, c + step)
+        copies.append(pltpu.make_async_copy(src.at[at], dst.at[at], sems.at[len(copies)]))
+        copies[-1].start()
+
     for c in range(0, depth, step):
         for z in range(c, c + step):
             potential[z] = cells_b[z] + c0 * cells_0[z] + c1 * cells_1[z]
-        copies.append((potential.at[c:c + step], potential_h.at[c:c + step]))
-        copies[-1] = pltpu.make_async_copy(*copies[-1], sems.at[len(copies) - 1])
-        copies[-1].start()
+        send(potential, potential_h, c)
     for c in range(0, depth, step):
         for z in range(c, c + step):
-            residual[z] = jnp.where(top, rim_row[z:z + 1], jnp.where(lane0, rim_col[:, z:z + 1], 0.0))
-        copies.append((residual.at[c:c + step], residual_h.at[c:c + step]))
-        copies[-1] = pltpu.make_async_copy(*copies[-1], sems.at[len(copies) - 1])
-        copies[-1].start()
+            flat = jnp.where(lane0, rim_col[:, z:z + 1], 0.0)
+            residual[z, 8:, :] = flat[8:]
+            residual[z, 0:8, :] = jnp.where(top, rim_row[z:z + 1], flat[0:8])
+        send(residual, residual_h, c)
     for copy in copies:
         copy.wait()
 

time: 32.3 us -> 32.2 us (level)
  transfers between devices with their start and end apart: 15 -> 15, of which waited for: 7 -> 7; matrix products, arithmetic and copies ran while one was open for 0% -> 0% of each run, Pallas kernels for 15% -> 14%
where the time goes in v5:
time: 32.2 us; the launch traced here: 32.1 us
  starting transfers between devices  17.1 us (53%)
  Pallas kernels  9.87 us (31%)
  waiting for transfers between devices  4.2 us (13%)
  between operations  0.86 us (3%)
    ppermute x12, starting transfers between devices, swap(): return lax.ppermute(value, axis, pairs + [(j, i) for i, j in pairs])  14.7 us
    pallas_call x1, Pallas kernels, on_device(): call(front_kernel, [block] + msgs, landing + [block, block, pltpu.VMEM((d...  2.9 us
    ppermute x3, starting transfers between devices, shifted(): return lax.ppermute(value, axis, [(i, (i + by) % n) for i in range(n)])  2.38 us
    ppermute x12, waiting for transfers between devices, swap(): return lax.ppermute(value, axis, pairs + [(j, i) for i, j in pairs])  2.1 us
    ppermute x3, waiting for transfers between devices, shifted(): return lax.ppermute(value, axis, [(i, (i + by) % n) for i in range(n)])  2.1 us
    pallas_call x1, Pallas kernels, on_device(): call(lambda *r: final_kernel(len(parts), *r), [block, block], [block, blo...  1.53 us
    pallas_call x1, Pallas kernels, on_device(): cells_0 = extend(s0, *backs)[0]  1.34 us
    pallas_call x1, Pallas kernels, on_device(): cells_1 = extend(s1, *backs)[0]  1.34 us
  transfers between devices with their start and end apart: 15, of which 7 were waited for; matrix products, arithmetic and copies ran while one was open for 0% of the time, Pallas kernels for 14%

profile of v5, /device:TPU:0, one launch (start us, length us, event | category | flops | bytes accessed | tf_op | source)
XLA Modules:
  0.0 32.1 jit_solution(10520114243896193797)
XLA Ops:
  0.6 0.0 copy-start.2
  0.6 0.0 copy-start.3
  0.7 2.9 %shard_map.185 = (f32[32,64,128]{2,1,0:T(8,128)S(1)}, f32[40,128]{1,0:T(8,128)S(1)}, f32[40,128]{1,0:T(8,128)S(1)}, f32[24,128]{1,0:T(8,128)S(1)}, f32[24,128]{1,0:T(8,128)S(1)}) custom-call(f32[32,64,128]{2,1,0:T(8,128)} %charge_h.1, f32[2,64,128]{2,1,0:T(8,128)} %surf_h.1, bf16[256,256]{1,0:T(8,128)(2,1)} %constant.32.clone.eyw_h.eyw, ...), custom_call_target="tpu_custom_call" | custom-call | tf_op jit(solution)/shard_map/pallas_call | solution.py:592
  3.6 5.1 %collective-permute-start = (f32[40,128]{1,0:T(8,128)S(1)}, f32[40,128]{1,0:T(8,128)S(1)}, u32[]{:S(2)}, u32[]{:S(2)}) collective-permute-start(f32[40,128]{1,0:T(8,128)S(1)} %get-tuple-element.34.r_0_), channel_id=1, source_target_pairs={{4,8},{12,0},{8,4},{0,12},{5,9},{13,1},{9,5},{1,13},{6,10},{14,2},... | collective-permute-start | bytes 61448 | tf_op jit(solution)/shard_map/ppermute | solution.py:531
  8.7 0.0 collective-permute-start.1
  8.7 0.7 %collective-permute-start.2 = (f32[24,128]{1,0:T(8,128)S(1)}, f32[24,128]{1,0:T(8,128)S(1)}, u32[]{:S(2)}, u32[]{:S(2)}) collective-permute-start(f32[24,128]{1,0:T(8,128)S(1)} %get-tuple-element.36.r_2_), channel_id=1, source_target_pairs={{1,2},{3,0},{2,1},{0,3},{5,6},{7,4},{6,5},{4,7},{9,10},{11,8},{10,... | collective-permute-start | bytes 36872 | tf_op jit(solution)/shard_map/ppermute | solution.py:531
  9.3 1.0 %collective-permute-start.3 = (f32[24,128]{1,0:T(8,128)S(1)}, f32[24,128]{1,0:T(8,128)S(1)}, u32[]{:S(2)}, u32[]{:S(2)}) collective-permute-start(f32[24,128]{1,0:T(8,128)S(1)} %get-tuple-element.37.r_3_), channel_id=1, source_target_pairs={{0,1},{2,3},{1,0},{3,2},{4,5},{6,7},{5,4},{7,6},{8,9},{10,11},{9,8... | collective-permute-start | bytes 36872 | tf_op jit(solution)/shard_map/ppermute | solution.py:531
  10.3 0.0 copy-start.5
  10.3 0.0 copy-start.12
  10.3 1.0 %shard_map.186.r_0_ = f32[32,64,128]{2,1,0:T(8,128)S(1)} custom-call(f32[32,64,128]{2,1,0:T(8,128)S(1)} %get-tuple-element.38.base, bf16[256,256]{1,0:T(8,128)(2,1)S(1)} %copy-done.3, bf16[256,256]{1,0:T(8,128)(2,1)S(1)} %copy-done.2), custom_call_target="tpu_custom_call" | custom-call | tf_op jit(solution)/shard_map/pallas_call | solution.py:599
  11.3 0.0 copy-start
  11.3 0.0 copy-start.6
  11.4 0.0 copy-start.7
  11.4 0.5 %collective-permute-done.2.r_6_ = f32[24,128]{1,0:T(8,128)S(1)} collective-permute-done((f32[24,128]{1,0:T(8,128)S(1)}, f32[24,128]{1,0:T(8,128)S(1)}, u32[]{:S(2)}, u32[]{:S(2)}) %collective-permute-start.2) | collective-permute-done | bytes 12320 | tf_op jit(solution)/shard_map/ppermute | solution.py:531
  11.9 0.0 collective-permute-done.3.r_7_
  11.9 0.0 collective-permute-done.r_4_
  11.9 0.6 %collective-permute-done.1.r_5_ = f32[40,128]{1,0:T(8,128)S(1)} collective-permute-done((f32[40,128]{1,0:T(8,128)S(1)}, f32[40,128]{1,0:T(8,128)S(1)}, u32[]{:S(2)}, u32[]{:S(2)}) %collective-permute-start.1) | collective-permute-done | bytes 20512 | tf_op jit(solution)/shard_map/ppermute | solution.py:531
  12.5 0.4 %shard_map.187 = (f32[200,128]{1,0:T(8,128)S(1)}, f32[40,128]{1,0:T(8,128)S(1)}, f32[40,128]{1,0:T(8,128)S(1)}, f32[24,128]{1,0:T(8,128)S(1)}, f32[24,128]{1,0:T(8,128)S(1)}) custom-call(f32[40,128]{1,0:T(8,128)S(1)} %get-tuple-element.34.r_0_, f32[40,128]{1,0:T(8,128)S(1)} %get-tuple-element.35.r_1_, f32[24,128]{1,0:T(8,128)S(1)} %get-tuple-element.36.r_2_, ...), custom_call_target="tpu_custom_call" | custom-call | tf_op jit(solution)/shard_map/pallas_call | solution.py:603
  12.9 0.0 copy-start.10
  12.9 1.9 %collective-permute-start.4 = (f32[40,128]{1,0:T(8,128)S(1)}, f32[40,128]{1,0:T(8,128)S(1)}, u32[]{:S(2)}, u32[]{:S(2)}) collective-permute-start(f32[40,128]{1,0:T(8,128)S(1)} %get-tuple-element.44.r_0_), channel_id=1, source_target_pairs={{4,8},{12,0},{8,4},{0,12},{5,9},{13,1},{9,5},{1,13},{6,10},{14,2},... | collective-permute-start | bytes 61448 | tf_op jit(solution)/shard_map/ppermute | solution.py:531
  14.8 0.0 collective-permute-start.5
  14.8 0.0 collective-permute-start.6
  14.8 1.6 %collective-permute-start.7 = (f32[24,128]{1,0:T(8,128)S(1)}, f32[24,128]{1,0:T(8,128)S(1)}, u32[]{:S(2)}, u32[]{:S(2)}) collective-permute-start(f32[24,128]{1,0:T(8,128)S(1)} %get-tuple-element.47.r_3_), channel_id=1, source_target_pairs={{0,1},{2,3},{1,0},{3,2},{4,5},{6,7},{5,4},{7,6},{8,9},{10,11},{9,8... | collective-permute-start | bytes 36872 | tf_op jit(solution)/shard_map/ppermute | solution.py:531
  16.4 1.3 %shard_map.188.r_1_ = f32[32,64,128]{2,1,0:T(8,128)S(1)} custom-call(f32[200,128]{1,0:T(8,128)S(1)} %get-tuple-element.48.state.r_12_.r_0_, bf16[256,256]{1,0:T(8,128)(2,1)S(1)} %copy-done.3, bf16[256,256]{1,0:T(8,128)(2,1)S(1)} %copy-done.2, f32[32,64,128]{2,1,0:T(8,128)S(1)} %copy-done, f32[64,128]{1,0:T(8,128)S(1)} %copy-done.6, ...), custom_call_target="tpu_custom_call" | custom-call | tf_op jit(solution)/shard_map/pallas_call | solution.py:607
  17.8 0.2 collective-permute-done.6.r_6_
  18.0 0.0 collective-permute-done.7.r_7_
  18.0 0.6 %collective-permute-done.4.r_4_ = f32[40,128]{1,0:T(8,128)S(1)} collective-permute-done((f32[40,128]{1,0:T(8,128)S(1)}, f32[40,128]{1,0:T(8,128)S(1)}, u32[]{:S(2)}, u32[]{:S(2)}) %collective-permute-start.4) | collective-permute-done | bytes 20512 | tf_op jit(solution)/shard_map/ppermute | solution.py:531
  18.6 0.2 collective-permute-done.5.r_5_
  18.8 0.4 %shard_map.189 = (f32[200,128]{1,0:T(8,128)S(1)}, f32[40,128]{1,0:T(8,128)S(1)}, f32[40,128]{1,0:T(8,128)S(1)}, f32[24,128]{1,0:T(8,128)S(1)}, f32[24,128]{1,0:T(8,128)S(1)}) custom-call(f32[40,128]{1,0:T(8,128)S(1)} %get-tuple-element.44.r_0_, f32[40,128]{1,0:T(8,128)S(1)} %get-tuple-element.45.r_1_, f32[24,128]{1,0:T(8,128)S(1)} %get-tuple-element.46.r_2_, ...), custom_call_target="tpu_custom_call" | custom-call | tf_op jit(solution)/shard_map/pallas_call | solution.py:609
  19.2 1.9 %collective-permute-start.10 = (f32[40,128]{1,0:T(8,128)S(1)}, f32[40,128]{1,0:T(8,128)S(1)}, u32[]{:S(2)}, u32[]{:S(2)}) collective-permute-start(f32[40,128]{1,0:T(8,128)S(1)} %get-tuple-element.54.r_2_), channel_id=1, source_target_pairs={{4,8},{12,0},{8,4},{0,12},{5,9},{13,1},{9,5},{1,13},{6,10},{14,2},... | collective-permute-start | bytes 61448 | tf_op jit(solution)/shard_map/ppermute | solution.py:531
  21.1 0.9 %collective-permute-start.9 = (f32[40,128]{1,0:T(8,128)S(1)}, f32[40,128]{1,0:T(8,128)S(1)}, u32[]{:S(2)}, u32[]{:S(2)}) collective-permute-start(f32[40,128]{1,0:T(8,128)S(1)} %get-tuple-element.55.r_3_), channel_id=1, source_target_pairs={{0,8},{4,12},{8,0},{12,4},{1,9},{5,13},{9,1},{13,5},{2,10},{6,14},... | collective-permute-start | bytes 61448 | tf_op jit(solution)/shard_map/ppermute | solution.py:525
  22.0 1.7 %collective-permute-start.8 = (f32[40,128]{1,0:T(8,128)S(1)}, f32[40,128]{1,0:T(8,128)S(1)}, u32[]{:S(2)}, u32[]{:S(2)}) collective-permute-start(f32[40,128]{1,0:T(8,128)S(1)} %get-tuple-element.55.r_3_), channel_id=1, source_target_pairs={{0,4},{8,12},{4,0},{12,8},{1,5},{9,13},{5,1},{13,9},{2,6},{10,14},... | collective-permute-start | bytes 61448 | tf_op jit(solution)/shard_map/ppermute | solution.py:531
  23.7 0.0 collective-permute-start.11
  23.7 0.0 copy-start.13
  23.7 1.3 %shard_map.190.r_2_ = f32[32,64,128]{2,1,0:T(8,128)S(1)} custom-call(f32[200,128]{1,0:T(8,128)S(1)} %get-tuple-element.56.state.r_1_, bf16[256,256]{1,0:T(8,128)(2,1)S(1)} %copy-done.3, bf16[256,256]{1,0:T(8,128)(2,1)S(1)} %copy-done.2, f32[32,64,128]{2,1,0:T(8,128)S(1)} %copy-done, f32[64,128]{1,0:T(8,128)S(1)} %copy-done.6, ...), custom_call_target="tpu_custom_call" | custom-call | tf_op jit(solution)/shard_map/pallas_call | solution.py:612
  25.1 0.0 copy-start.11
  25.1 0.0 collective-permute-done.10.r_5_
  25.1 0.9 %collective-permute-done.9 = f32[40,128]{1,0:T(8,128)S(1)} collective-permute-done((f32[40,128]{1,0:T(8,128)S(1)}, f32[40,128]{1,0:T(8,128)S(1)}, u32[]{:S(2)}, u32[]{:S(2)}) %collective-permute-start.9) | collective-permute-done | bytes 20512 | tf_op jit(solution)/shard_map/ppermute | solution.py:525
  26.0 0.0 collective-permute-done.8.r_6_
  26.0 0.9 %collective-permute-start.14 = (f32[8,128]{1,0:T(8,128)S(1)}, f32[8,128]{1,0:T(8,128)S(1)}, u32[]{:S(2)}, u32[]{:S(2)}) collective-permute-start(f32[8,128]{1,0:T(8,128)S(1)} %add_add_fusion.r_5_), channel_id=1, source_target_pairs={{1,2},{3,0},{2,1},{0,3},{5,6},{7,4},{6,5},{4,7},{9,10},{11,8},{10,... | collective-permute-start | bytes 12296 | tf_op jit(solution)/shard_map/ppermute | solution.py:531
  26.9 1.5 %collective-permute-start.13 = (f32[8,128]{1,0:T(8,128)S(1)}, f32[8,128]{1,0:T(8,128)S(1)}, u32[]{:S(2)}, u32[]{:S(2)}) collective-permute-start(f32[8,128]{1,0:T(8,128)S(1)} %add_add_fusion.r_5_), channel_id=1, source_target_pairs={{0,2},{1,3},{2,0},{3,1},{4,6},{5,7},{6,4},{7,5},{8,10},{9,11},{10,... | collective-permute-start | bytes 12296 | tf_op jit(solution)/shard_map/ppermute | solution.py:525
  28.4 0.0 collective-permute-start.12
  28.4 0.0 collective-permute-done.11.r_7_
  28.5 0.9 %shard_map.191 = (f32[3,32,128]{2,1,0:T(8,128)S(1)}, f32[3,64,128]{2,1,0:T(8,128)S(1)}) custom-call(f32[200,128]{1,0:T(8,128)S(1)} %get-tuple-element.48.state.r_12_.r_0_, f32[200,128]{1,0:T(8,128)S(1)} %get-tuple-element.56.state.r_1_, f32[40,128]{1,0:T(8,128)S(1)} %get-tuple-element.54.r_2_, f32[40,128]{1,0:T(8,128)S(1)} %get-tuple-element.55.r_3_, ...), custom_call_target="tpu_custom_call" | custom-call | tf_op jit(solution)/shard_map/pallas_call | solution.py:615
  29.4 0.0 collective-permute-done.14.r_8_
  29.4 1.2 %collective-permute-done.13.r_7_ = f32[8,128]{1,0:T(8,128)S(1)} collective-permute-done((f32[8,128]{1,0:T(8,128)S(1)}, f32[8,128]{1,0:T(8,128)S(1)}, u32[]{:S(2)}, u32[]{:S(2)}) %collective-permute-start.13) | collective-permute-done | bytes 4128 | tf_op jit(solution)/shard_map/ppermute | solution.py:525
  30.5 0.0 collective-permute-done.12.r_6_
  30.6 1.5 %shard_map.192 = (f32[32,64,128]{2,1,0:T(8,128)}, f32[32,64,128]{2,1,0:T(8,128)}) custom-call(f32[32,64,128]{2,1,0:T(8,128)S(1)} %shard_map.186.r_0_, f32[32,64,128]{2,1,0:T(8,128)S(1)} %shard_map.188.r_1_, f32[32,64,128]{2,1,0:T(8,128)S(1)} %shard_map.190.r_2_, f32[3,32,128]{2,1,0:T(8,128)S(1)} %get-tuple-element.60.r_3_, ...), custom_call_target="tpu_custom_call" | custom-call | tf_op jit(solution)/shard_map/pallas_call | solution.py:618
  (23 shorter events, 0.1 us)
Async XLA Ops:
  0.6 9.7 %copy-start.2 = (bf16[256,256]{1,0:T(8,128)(2,1)S(1)}, bf16[256,256]{1,0:T(8,128)(2,1)}, u32[]{:S(2)}) copy-start(bf16[256,256]{1,0:T(8,128)(2,1)} %constant.33.clone.exw_h.exw) | copy-start | bytes 393220
  0.6 9.6 %copy-start.3 = (bf16[256,256]{1,0:T(8,128)(2,1)S(1)}, bf16[256,256]{1,0:T(8,128)(2,1)}, u32[]{:S(2)}) copy-start(bf16[256,256]{1,0:T(8,128)(2,1)} %constant.32.clone.eyw_h.eyw) | copy-start | bytes 393220
  3.6 8.3 %collective-permute-start = (f32[40,128]{1,0:T(8,128)S(1)}, f32[40,128]{1,0:T(8,128)S(1)}, u32[]{:S(2)}, u32[]{:S(2)}) collective-permute-start(f32[40,128]{1,0:T(8,128)S(1)} %get-tuple-element.34.r_0_), channel_id=1, source_target_pairs={{4,8},{12,0},{8,4},{0,12},{5,9},{13,1},{9,5},{1,13},{6,10},{14,2},... | collective-permute-start | bytes 61448 | tf_op jit(solution)/shard_map/ppermute | solution.py:531
  8.7 3.8 %collective-permute-start.1 = (f32[40,128]{1,0:T(8,128)S(1)}, f32[40,128]{1,0:T(8,128)S(1)}, u32[]{:S(2)}, u32[]{:S(2)}) collective-permute-start(f32[40,128]{1,0:T(8,128)S(1)} %get-tuple-element.35.r_1_), channel_id=1, source_target_pairs={{0,4},{8,12},{4,0},{12,8},{1,5},{9,13},{5,1},{13,9},{2,6},{10,14},... | collective-permute-start | bytes 61448 | tf_op jit(solution)/shard_map/ppermute | solution.py:531
  8.7 3.2 %collective-permute-start.2 = (f32[24,128]{1,0:T(8,128)S(1)}, f32[24,128]{1,0:T(8,128)S(1)}, u32[]{:S(2)}, u32[]{:S(2)}) collective-permute-start(f32[24,128]{1,0:T(8,128)S(1)} %get-tuple-element.36.r_2_), channel_id=1, source_target_pairs={{1,2},{3,0},{2,1},{0,3},{5,6},{7,4},{6,5},{4,7},{9,10},{11,8},{10,... | collective-permute-start | bytes 36872 | tf_op jit(solution)/shard_map/ppermute | solution.py:531
  9.3 2.6 %collective-permute-start.3 = (f32[24,128]{1,0:T(8,128)S(1)}, f32[24,128]{1,0:T(8,128)S(1)}, u32[]{:S(2)}, u32[]{:S(2)}) collective-permute-start(f32[24,128]{1,0:T(8,128)S(1)} %get-tuple-element.37.r_3_), channel_id=1, source_target_pairs={{0,1},{2,3},{1,0},{3,2},{4,5},{6,7},{5,4},{7,6},{8,9},{10,11},{9,8... | collective-permute-start | bytes 36872 | tf_op jit(solution)/shard_map/ppermute | solution.py:531
  10.3 2.2 %copy-start.1 = (f32[32,64,128]{2,1,0:T(8,128)S(1)}, f32[32,64,128]{2,1,0:T(8,128)}, u32[]{:S(2)}) copy-start(f32[32,64,128]{2,1,0:T(8,128)} %constant.42.clone.r_8_) | copy-start | bytes 3145732
  10.3 2.2 %copy-start.4 = (f32[5,64,128]{2,1,0:T(8,128)S(1)}, f32[5,64,128]{2,1,0:T(8,128)}, u32[]{:S(2)}) copy-start(f32[5,64,128]{2,1,0:T(8,128)} %constant.44.clone.r_10_) | copy-start | bytes 491524
  10.3 2.2 %copy-start.5 = (f32[5,32,128]{2,1,0:T(8,128)S(1)}, f32[5,32,128]{2,1,0:T(8,128)}, u32[]{:S(2)}) copy-start(f32[5,32,128]{2,1,0:T(8,128)} %constant.43.clone.r_9_) | copy-start | bytes 245764
  10.3 2.2 %copy-start.12 = (f32[8,128]{1,0:T(8,128)S(1)}, f32[8,128]{1,0:T(8,128)}, u32[]{:S(2)}) copy-start(f32[8,128]{1,0:T(8,128)} %constant.45.clone.r_11_) | copy-start | bytes 12292
  11.3 5.1 %copy-start = (f32[32,64,128]{2,1,0:T(8,128)S(1)}, f32[32,64,128]{2,1,0:T(8,128)}, u32[]{:S(2)}) copy-start(f32[32,64,128]{2,1,0:T(8,128)} %constant.40.clone.inv) | copy-start | bytes 3145732
  11.3 5.1 %copy-start.6 = (f32[64,128]{1,0:T(8,128)S(1)}, f32[64,128]{1,0:T(8,128)}, u32[]{:S(2)}) copy-start(f32[64,128]{1,0:T(8,128)} %constant.47.clone.sx0_h.sx0) | copy-start | bytes 98308
  11.4 5.1 %copy-start.7 = (bf16[256,128]{1,0:T(8,128)(2,1)S(1)}, bf16[256,128]{1,0:T(8,128)(2,1)}, u32[]{:S(2)}) copy-start(bf16[256,128]{1,0:T(8,128)(2,1)} %constant.35.clone.colw) | copy-start | bytes 196612
  12.9 3.5 %copy-start.10 = (f32[8,128]{1,0:T(8,128)S(1)}, f32[8,128]{1,0:T(8,128)}, u32[]{:S(2)}) copy-start(f32[8,128]{1,0:T(8,128)} %constant.46.clone.line_h.line) | copy-start | bytes 12292
  12.9 5.7 %collective-permute-start.4 = (f32[40,128]{1,0:T(8,128)S(1)}, f32[40,128]{1,0:T(8,128)S(1)}, u32[]{:S(2)}, u32[]{:S(2)}) collective-permute-start(f32[40,128]{1,0:T(8,128)S(1)} %get-tuple-element.44.r_0_), channel_id=1, source_target_pairs={{4,8},{12,0},{8,4},{0,12},{5,9},{13,1},{9,5},{1,13},{6,10},{14,2},... | collective-permute-start | bytes 61448 | tf_op jit(solution)/shard_map/ppermute | solution.py:531
  14.8 4.0 %collective-permute-start.5 = (f32[40,128]{1,0:T(8,128)S(1)}, f32[40,128]{1,0:T(8,128)S(1)}, u32[]{:S(2)}, u32[]{:S(2)}) collective-permute-start(f32[40,128]{1,0:T(8,128)S(1)} %get-tuple-element.45.r_1_), channel_id=1, source_target_pairs={{0,4},{8,12},{4,0},{12,8},{1,5},{9,13},{5,1},{13,9},{2,6},{10,14},... | collective-permute-start | bytes 61448 | tf_op jit(solution)/shard_map/ppermute | solution.py:531
  14.8 3.2 %collective-permute-start.6 = (f32[24,128]{1,0:T(8,128)S(1)}, f32[24,128]{1,0:T(8,128)S(1)}, u32[]{:S(2)}, u32[]{:S(2)}) collective-permute-start(f32[24,128]{1,0:T(8,128)S(1)} %get-tuple-element.46.r_2_), channel_id=1, source_target_pairs={{1,2},{3,0},{2,1},{0,3},{5,6},{7,4},{6,5},{4,7},{9,10},{11,8},{10,... | collective-permute-start | bytes 36872 | tf_op jit(solution)/shard_map/ppermute | solution.py:531
  14.8 3.2 %collective-permute-start.7 = (f32[24,128]{1,0:T(8,128)S(1)}, f32[24,128]{1,0:T(8,128)S(1)}, u32[]{:S(2)}, u32[]{:S(2)}) collective-permute-start(f32[24,128]{1,0:T(8,128)S(1)} %get-tuple-element.47.r_3_), channel_id=1, source_target_pairs={{0,1},{2,3},{1,0},{3,2},{4,5},{6,7},{5,4},{7,6},{8,9},{10,11},{9,8... | collective-permute-start | bytes 36872 | tf_op jit(solution)/shard_map/ppermute | solution.py:531
  19.2 5.8 %collective-permute-start.10 = (f32[40,128]{1,0:T(8,128)S(1)}, f32[40,128]{1,0:T(8,128)S(1)}, u32[]{:S(2)}, u32[]{:S(2)}) collective-permute-start(f32[40,128]{1,0:T(8,128)S(1)} %get-tuple-element.54.r_2_), channel_id=1, source_target_pairs={{4,8},{12,0},{8,4},{0,12},{5,9},{13,1},{9,5},{1,13},{6,10},{14,2},... | collective-permute-start | bytes 61448 | tf_op jit(solution)/shard_map/ppermute | solution.py:531
  21.1 4.9 %collective-permute-start.9 = (f32[40,128]{1,0:T(8,128)S(1)}, f32[40,128]{1,0:T(8,128)S(1)}, u32[]{:S(2)}, u32[]{:S(2)}) collective-permute-start(f32[40,128]{1,0:T(8,128)S(1)} %get-tuple-element.55.r_3_), channel_id=1, source_target_pairs={{0,8},{4,12},{8,0},{12,4},{1,9},{5,13},{9,1},{13,5},{2,10},{6,14},... | collective-permute-start | bytes 61448 | tf_op jit(solution)/shard_map/ppermute | solution.py:525
  22.0 4.0 %collective-permute-start.8 = (f32[40,128]{1,0:T(8,128)S(1)}, f32[40,128]{1,0:T(8,128)S(1)}, u32[]{:S(2)}, u32[]{:S(2)}) collective-permute-start(f32[40,128]{1,0:T(8,128)S(1)} %get-tuple-element.55.r_3_), channel_id=1, source_target_pairs={{0,4},{8,12},{4,0},{12,8},{1,5},{9,13},{5,1},{13,9},{2,6},{10,14},... | collective-permute-start | bytes 61448 | tf_op jit(solution)/shard_map/ppermute | solution.py:531
  23.7 4.8 %collective-permute-start.11 = (f32[24,128]{1,0:T(8,128)S(1)}, f32[24,128]{1,0:T(8,128)S(1)}, u32[]{:S(2)}, u32[]{:S(2)}) collective-permute-start(f32[24,128]{1,0:T(8,128)S(1)} %get-tuple-element.59), channel_id=1, source_target_pairs={{0,1},{1,2},{2,3},{3,0},{4,5},{5,6},{6,7},{7,4},{8,9},{9,10},{10,1... | collective-permute-start | bytes 36872 | tf_op jit(solution)/shard_map/ppermute | solution.py:525
  23.7 4.8 %copy-start.8 = (f32[128,128]{1,0:T(8,128)S(1)}, f32[128,128]{1,0:T(8,128)}, u32[]{:S(2)}) copy-start(f32[128,128]{1,0:T(8,128)} %constant.39.clone.r_11_) | copy-start | bytes 196612
  23.7 4.8 %copy-start.9 = (f32[128,128]{1,0:T(8,128)S(1)}, f32[128,128]{1,0:T(8,128)}, u32[]{:S(2)}) copy-start(f32[128,128]{1,0:T(8,128)} %constant.36.clone.r_8_) | copy-start | bytes 196612
  23.7 4.8 %copy-start.13 = (f32[32,32]{1,0:T(8,128)S(1)}, f32[32,32]{1,0:T(8,128)}, u32[]{:S(2)}) copy-start(f32[32,32]{1,0:T(8,128)} %constant.38.clone.r_10_) | copy-start | bytes 12292
  25.1 3.4 %copy-start.11 = (f32[64,64]{1,0:T(8,128)S(1)}, f32[64,64]{1,0:T(8,128)}, u32[]{:S(2)}) copy-start(f32[64,64]{1,0:T(8,128)} %constant.37.clone.r_9_) | copy-start | bytes 49156
  26.0 3.3 %collective-permute-start.14 = (f32[8,128]{1,0:T(8,128)S(1)}, f32[8,128]{1,0:T(8,128)S(1)}, u32[]{:S(2)}, u32[]{:S(2)}) collective-permute-start(f32[8,128]{1,0:T(8,128)S(1)} %add_add_fusion.r_5_), channel_id=1, source_target_pairs={{1,2},{3,0},{2,1},{0,3},{5,6},{7,4},{6,5},{4,7},{9,10},{11,8},{10,... | collective-permute-start | bytes 12296 | tf_op jit(solution)/shard_map/ppermute | solution.py:531
  26.9 3.6 %collective-permute-start.13 = (f32[8,128]{1,0:T(8,128)S(1)}, f32[8,128]{1,0:T(8,128)S(1)}, u32[]{:S(2)}, u32[]{:S(2)}) collective-permute-start(f32[8,128]{1,0:T(8,128)S(1)} %add_add_fusion.r_5_), channel_id=1, source_target_pairs={{0,2},{1,3},{2,0},{3,1},{4,6},{5,7},{6,4},{7,5},{8,10},{9,11},{10,... | collective-permute-start | bytes 12296 | tf_op jit(solution)/shard_map/ppermute | solution.py:525
  28.4 2.1 %collective-permute-start.12 = (f32[8,128]{1,0:T(8,128)S(1)}, f32[8,128]{1,0:T(8,128)S(1)}, u32[]{:S(2)}, u32[]{:S(2)}) collective-permute-start(f32[8,128]{1,0:T(8,128)S(1)} %add_add_fusion.r_5_), channel_id=1, source_target_pairs={{0,1},{2,3},{1,0},{3,2},{4,5},{6,7},{5,4},{7,6},{8,9},{10,11},{9,8... | collective-permute-start | bytes 12296 | tf_op jit(solution)/shard_map/ppermute | solution.py:531

commit v6 on v5

--- a/solution.py
+++ b/solution.py
@@ -63,7 +63,6 @@
     sgb = np.where(b % 2 == 1, 1.0, -1.0)
     inside = (a[:, None] > 0) & (b[None, :] > 0)
     inv = np.where(inside[None], 1.0 / (lz[:, None, None] + lx[None, :, None] + ly[None, None, :]), 0.0)
-    tab["inv"] = inv.astype(np.float32)
     tab["lxy"] = np.where(inside, lx[:, None] + ly[None, :], 1e30).astype(np.float32)
 
     def to_rows(kb):
@@ -72,8 +71,8 @@
     def to_cols(ka):
         return np.tile(ka.T, (1, groups))
 
-    inv2 = inv.transpose(2, 1, 0).reshape(groups, rows, width, depth)
-    tab["inv2"] = inv2.transpose(1, 2, 0, 3).reshape(rows, width, lanes).astype(np.float32)
+    tab["lxz"] = to_cols(np.where(a > 0, lz[:, None] + lx, 1e30)).astype(np.float32)
+    tab["ly"] = to_rows(np.ones((depth, 1)) * np.where(b > 0, ly, 1e30)).astype(np.float32)
     ones = np.ones((depth, 1))
     odd_a, odd_b = sga > 0, sgb > 0
     sx2, sy2 = (sx**2)[None, :, None] * inv, (sy**2)[None, None, :] * inv
@@ -241,14 +240,14 @@
     return jnp.concatenate([body, jnp.concatenate(rows, 0)], 0)
 
 
-def front_kernel(charge_h, surf_h, eyw_h, exw_h, lxy_h, sx0_h, rimw_h, line_h, base, *rest):
-    msgs = rest[:4]
-    charge, surf, eyw, exw, lxy, sx0, rimw, line, work, inv, rims, part, first, sems = rest[4:]
+def front_kernel(charge_h, surf_h, eyw_h, exw_h, lxy_h, sx0_h, line_h, base, inv, rims, *rest):
+    msgs = rest[:2]
+    charge, surf, eyw, exw, lxy, sx0, line, work, part, first, sems = rest[2:]
     depth, width, height = charge.shape
     tiles = width // 8
     pairs = [(lxy_h, lxy), (surf_h, surf)]
     pairs += [(charge_h.at[:, 8 * i:8 * i + 8, :], charge.at[:, 8 * i:8 * i + 8, :]) for i in range(tiles)]
-    pairs += [(eyw_h, eyw), (exw_h, exw), (sx0_h, sx0), (rimw_h, rimw), (line_h, line)]
+    pairs += [(eyw_h, eyw), (exw_h, exw), (sx0_h, sx0), (line_h, line)]
     copies = [pltpu.make_async_copy(src, dst, sems.at[i]) for i, (src, dst) in enumerate(pairs)]
     for copy in copies:
         copy.start()
@@ -280,6 +279,21 @@
             part[k] = jnp.sum((inner * sx0[...]).reshape(width // 8, 8, height), 0)
             hi, lo = halves(jnp.where(lane == 0, spec, inner * line[0:1, :]))
             rims[k * width:(k + 1) * width, :] = jnp.concatenate([hi, lo], 1)
+    row_near, row_far = sub_sums(part)
+    own_t = copies_t(first[:, 0, :])
+    corner = own_t[0:1]
+    row = rows_from(own_t + copies_t(row_near), depth)
+    at_zero = (lax.broadcasted_iota(jnp.int32, row.shape, 0) == 0) & (lane_id(row.shape) < depth)
+    row = jnp.where(at_zero, 0.0, row)
+    px = with_tail(row, [corner])
+    nx = with_tail(rows_from(copies_t(row_far), depth), [])
+    for ref, value in zip(msgs, swapped("gx", nx, px)):
+        ref[...] = value
+
+
+def sides_kernel(depth, rims, rimw, bx, ax, by, ay):
+    width = rims.shape[0] // depth
+    lane = lane_id((width, 128))
     step = 8
     found = jnp.zeros((width, 128), F32)
     for c in range(0, depth, step):
@@ -288,18 +302,12 @@
             one = out[(k - c) * width:(k - c + 1) * width]
             found = jnp.where(lane % depth == k, one, found)
     near, far, own = (spread(jnp.where(lane // depth == g, found, 0.0), depth) for g in range(3))
-    row_near, row_far = sub_sums(part)
-    own_t = copies_t(first[:, 0, :])
-    corner = own_t[0:1]
-    row = rows_from(own_t + copies_t(row_near), depth)
-    at_zero = (lax.broadcasted_iota(jnp.int32, row.shape, 0) == 0) & (lane_id(row.shape) < depth)
-    row = jnp.where(at_zero, 0.0, row)
+    _, px = swapped("gx", bx[...], ax[...])
+    corner = px[px.shape[0] - 8:px.shape[0] - 7]
     col = jnp.where(lax.broadcasted_iota(jnp.int32, own.shape, 0) == 0, 0.0, own + near)
-    px = with_tail(row, [corner])
-    nx = with_tail(rows_from(copies_t(row_far), depth), [])
     py = with_tail(pack(col, depth), [corner])
     ny = with_tail(pack(far, depth), [])
-    for ref, value in zip(msgs, swapped("gx", nx, px) + swapped("gy", ny, py)):
+    for ref, value in zip((by, ay), swapped("gy", ny, py)):
         ref[...] = value
 
 
@@ -417,7 +425,9 @@
             out[z, at, :] = value
 
 
-def base_kernel(base, eyw, exw, out, work):
+def base_kernel(base, eyw, exw, lxz, ly, out, inv2, work):
+    for r in range(inv2.shape[0]):
+        inv2[r] = 1.0 / (lxz[...] + ly[r:r + 1, :])
     cells_from(out, work, lambda k: base[k], exw[...], eyw[...])
 
 
@@ -570,7 +580,7 @@
         specs["out_specs"] = out_specs
     return pl.pallas_call(
         kernel,
-        out_shape=[jax.ShapeDtypeStruct(shape, F32) for shape in outs],
+        out_shape=[jax.ShapeDtypeStruct(o, F32) if isinstance(o, tuple) else o for o in outs],
         scratch_shapes=[pltpu.VMEM(s, F32) if isinstance(s, tuple) else s for s in scratch],
         compiler_params=pltpu.CompilerParams(vmem_limit_bytes=48 * 1024 * 1024),
         **specs,
@@ -586,24 +596,26 @@
     block = (depth, width, height)
     anywhere = pl.BlockSpec(memory_space=pltpu.HBM)
     whole = pl.BlockSpec(memory_space=pltpu.VMEM)
-    fronts = (charge, surface_charge) + tuple(tab[n] for n in ("eyw", "exw", "lxy", "sx0", "rimw", "line"))
+    fronts = (charge, surface_charge) + tuple(tab[n] for n in ("eyw", "exw", "lxy", "sx0", "line"))
     landing = [pltpu.VMEM(x.shape, x.dtype) for x in fronts]
     fronts = [pltpu.with_memory_space_constraint(x, pltpu.HBM) for x in fronts]
-    base, *own = call(
-        front_kernel, [block] + msgs,
-        landing + [block, block, pltpu.VMEM((depth * width, 2 * height), BF16), (depth, 8, height), (depth, 8, height),
-                   pltpu.SemaphoreType.DMA((7 + width // 8,))],
-        in_specs=[anywhere] * 8,
+    base, inv, rims, *own = call(
+        front_kernel, [block, block, jax.ShapeDtypeStruct((depth * width, 2 * height), BF16)] + msgs[:2],
+        landing + [block, (depth, 8, height), (depth, 8, height), pltpu.SemaphoreType.DMA((6 + width // 8,))],
+        in_specs=[anywhere] * 7,
     )(*fronts)
+    own += call(lambda *r: sides_kernel(depth, *r), msgs[2:], [])(rims, tab["rimw"], *own)
     got = exchange(*own)
-    cells_b = call(base_kernel, [block], [block])(base, tab["eyw"], tab["exw"])[0]
+    cells_b, inv2 = call(base_kernel, [block, (rows, width, 128)], [block])(
+        base, tab["eyw"], tab["exw"], tab["lxz"], tab["ly"]
+    )
     *got, cells_b = lax.optimization_barrier((*got, cells_b))
-    tables = (tab["inv2"], tab["rowt"], tab["colt"], tab["crnt"])
+    tables = (inv2, tab["rowt"], tab["colt"], tab["crnt"])
     scratch = [(rows, 8, 128), (rows, 128), (rows, 128)]
     s0, *own = call(lambda *r: schur_kernel(depth, False, *r), [state] + msgs, scratch)(*own, *got, *tables)
     got = exchange(*own)
     extend = call(extend_kernel, [block], [block])
-    backs = tuple(tab[n] for n in ("eyw", "exw", "inv", "sx0", "colw", "line"))
+    backs = (tab["eyw"], tab["exw"], inv, tab["sx0"], tab["colw"], tab["line"])
     cells_0 = extend(s0, *backs)[0]
     *got, cells_0 = lax.optimization_barrier((*got, cells_0))
     s1, *own = call(lambda *r: schur_kernel(depth, True, *r), [state] + msgs, scratch)(*own, *got, *tables, s0)

time: 32.2 us -> 32 us (level)
  waiting for transfers between devices: 4.2 us -> 3.75 us
  Pallas kernels: 9.87 us -> 10.2 us
    ppermute x3, starting transfers between devices: 2.38 us -> 1.62 us  [shifted(): return lax.ppermute(value, axis, [(i, (i + by) % n) for i in range(n)])]
    ppermute x12, waiting for transfers between devices: 2.1 us -> 1.43 us  [swap(): return lax.ppermute(value, axis, pairs + [(j, i) for i, j in pairs])]
    ppermute x12, starting transfers between devices: 14.7 us -> 15.3 us  [swap(): return lax.ppermute(value, axis, pairs + [(j, i) for i, j in pairs])]
    pallas_call x2 -> x3, Pallas kernels: 3.9 us -> 4.24 us  [the longest x1 2.57 us: on_device(): call(front_kernel, [block, block, jax.ShapeDtypeStruct((depth * width, 2...]
  transfers between devices with their start and end apart: 15 -> 15, of which waited for: 7 -> 6; matrix products, arithmetic and copies ran while one was open for 0% -> 0% of each run, Pallas kernels for 14% -> 17%
where the time goes in v6:
time: 32 us; the launch traced here: 31.9 us
  starting transfers between devices  17 us (53%)
  Pallas kernels  10.2 us (32%)
  waiting for transfers between devices  3.75 us (12%)
  between operations  0.87 us (3%)
    ppermute x12, starting transfers between devices, swap(): return lax.ppermute(value, axis, pairs + [(j, i) for i, j in pairs])  15.3 us
    pallas_call x1, Pallas kernels, on_device(): call(front_kernel, [block, block, jax.ShapeDtypeStruct((depth * width, 2...  2.57 us
    ppermute x3, waiting for transfers between devices, shifted(): return lax.ppermute(value, axis, [(i, (i + by) % n) for i in range(n)])  2.33 us
    ppermute x3, starting transfers between devices, shifted(): return lax.ppermute(value, axis, [(i, (i + by) % n) for i in range(n)])  1.62 us
    pallas_call x1, Pallas kernels, on_device(): call(lambda *r: final_kernel(len(parts), *r), [block, block], [block, blo...  1.53 us
    ppermute x12, waiting for transfers between devices, swap(): return lax.ppermute(value, axis, pairs + [(j, i) for i, j in pairs])  1.43 us
    pallas_call x1, Pallas kernels, on_device(): cells_1 = extend(s1, *backs)[0]  1.36 us
    pallas_call x1, Pallas kernels, on_device(): cells_0 = extend(s0, *backs)[0]  1.36 us
  transfers between devices with their start and end apart: 15, of which 6 were waited for; matrix products, arithmetic and copies ran while one was open for 0% of the time, Pallas kernels for 17%

profile of v6, /device:TPU:0, one launch (start us, length us, event | category | flops | bytes accessed | tf_op | source)
XLA Modules:
  0.0 31.9 jit_solution(11799020452215228263)
XLA Ops:
  0.6 0.0 copy-start.8
  0.6 2.6 %shard_map.185 = (f32[32,64,128]{2,1,0:T(8,128)S(1)}, f32[32,64,128]{2,1,0:T(8,128)S(1)}, bf16[2048,256]{1,0:T(8,128)(2,1)S(1)}, f32[40,128]{1,0:T(8,128)S(1)}, f32[40,128]{1,0:T(8,128)S(1)}) custom-call(f32[32,64,128]{2,1,0:T(8,128)} %charge_h.1, f32[2,64,128]{2,1,0:T(8,128)} %surf_h.1, bf16[256,256]{1,0:T(8,128)(2,1)} %constant.32.clone.eyw_h.eyw, ...), custom_call_target="tpu_custom_call" | custom-call | tf_op jit(solution)/shard_map/pallas_call | solution.py:602
  3.2 5.1 %collective-permute-start = (f32[40,128]{1,0:T(8,128)S(1)}, f32[40,128]{1,0:T(8,128)S(1)}, u32[]{:S(2)}, u32[]{:S(2)}) collective-permute-start(f32[40,128]{1,0:T(8,128)S(1)} %get-tuple-element.38.r_2_.r_0_), channel_id=1, source_target_pairs={{4,8},{12,0},{8,4},{0,12},{5,9},{13,1},{9,5},{1,13},{6,10},{14,2},... | collective-permute-start | bytes 61448 | tf_op jit(solution)/shard_map/ppermute | solution.py:541
  8.3 0.0 collective-permute-start.1
  8.3 0.0 copy-start.10
  8.4 0.0 copy-start.12
  8.4 0.6 %shard_map.186 = (f32[24,128]{1,0:T(8,128)S(1)}, f32[24,128]{1,0:T(8,128)S(1)}) custom-call(bf16[2048,256]{1,0:T(8,128)(2,1)S(1)} %get-tuple-element.40.r_0_, bf16[256,128]{1,0:T(8,128)(2,1)S(1)} %copy-done.8, f32[40,128]{1,0:T(8,128)S(1)} %get-tuple-element.38.r_2_.r_0_, f32[40,128]{1,0:T(8,128)S(1)} %get-tuple-element.39.r_3_.r_1_), custom_call_target="tpu_custom_call" | custom-call | tf_op jit(solution)/shard_map/pallas_call | solution.py:607
  9.0 0.7 %collective-permute-start.2 = (f32[24,128]{1,0:T(8,128)S(1)}, f32[24,128]{1,0:T(8,128)S(1)}, u32[]{:S(2)}, u32[]{:S(2)}) collective-permute-start(f32[24,128]{1,0:T(8,128)S(1)} %get-tuple-element.41.r_2_), channel_id=1, source_target_pairs={{1,2},{3,0},{2,1},{0,3},{5,6},{7,4},{6,5},{4,7},{9,10},{11,8},{10,... | collective-permute-start | bytes 36872 | tf_op jit(solution)/shard_map/ppermute | solution.py:541
  9.7 1.0 %collective-permute-start.3 = (f32[24,128]{1,0:T(8,128)S(1)}, f32[24,128]{1,0:T(8,128)S(1)}, u32[]{:S(2)}, u32[]{:S(2)}) collective-permute-start(f32[24,128]{1,0:T(8,128)S(1)} %get-tuple-element.42.r_3_), channel_id=1, source_target_pairs={{0,1},{2,3},{1,0},{3,2},{4,5},{6,7},{5,4},{7,6},{8,9},{10,11},{9,8... | collective-permute-start | bytes 36872 | tf_op jit(solution)/shard_map/ppermute | solution.py:541
  10.7 0.0 copy-start.2
  10.7 0.0 copy-start.3
  10.7 0.0 copy-start.13
  10.7 1.1 %shard_map.187 = (f32[32,64,128]{2,1,0:T(8,128)S(1)}, f32[32,64,128]{2,1,0:T(8,128)S(1)}) custom-call(f32[32,64,128]{2,1,0:T(8,128)S(1)} %get-tuple-element.43.base, bf16[256,256]{1,0:T(8,128)(2,1)S(1)} %copy-done.1, bf16[256,256]{1,0:T(8,128)(2,1)S(1)} %copy-done, f32[64,128]{1,0:T(8,128)S(1)} %copy-done.10, f32[32,128]{1,0:T(8,128)S(1)} %copy-done.12), custom_call_target="tpu_custom_call" | custom-call | tf_op jit(solution)/shard_map/pallas_call | solution.py:609
  11.8 0.5 %collective-permute-done.2.r_6_ = f32[24,128]{1,0:T(8,128)S(1)} collective-permute-done((f32[24,128]{1,0:T(8,128)S(1)}, f32[24,128]{1,0:T(8,128)S(1)}, u32[]{:S(2)}, u32[]{:S(2)}) %collective-permute-start.2) | collective-permute-done | bytes 12320 | tf_op jit(solution)/shard_map/ppermute | solution.py:541
  12.2 0.0 collective-permute-done.3.r_7_
  12.2 0.0 collective-permute-done.r_4_
  12.2 0.0 collective-permute-done.1.r_5_
  12.3 0.0 copy-start.4
  12.3 0.0 copy-start.5
  12.3 0.4 %shard_map.188 = (f32[200,128]{1,0:T(8,128)S(1)}, f32[40,128]{1,0:T(8,128)S(1)}, f32[40,128]{1,0:T(8,128)S(1)}, f32[24,128]{1,0:T(8,128)S(1)}, f32[24,128]{1,0:T(8,128)S(1)}) custom-call(f32[40,128]{1,0:T(8,128)S(1)} %get-tuple-element.38.r_2_.r_0_, f32[40,128]{1,0:T(8,128)S(1)} %get-tuple-element.39.r_3_.r_1_, f32[24,128]{1,0:T(8,128)S(1)} %get-tuple-element.41.r_2_, ...), custom_call_target="tpu_custom_call" | custom-call | tf_op jit(solution)/shard_map/pallas_call | solution.py:615
  12.7 1.7 %collective-permute-start.4 = (f32[40,128]{1,0:T(8,128)S(1)}, f32[40,128]{1,0:T(8,128)S(1)}, u32[]{:S(2)}, u32[]{:S(2)}) collective-permute-start(f32[40,128]{1,0:T(8,128)S(1)} %get-tuple-element.51.r_0_), channel_id=1, source_target_pairs={{4,8},{12,0},{8,4},{0,12},{5,9},{13,1},{9,5},{1,13},{6,10},{14,2},... | collective-permute-start | bytes 61448 | tf_op jit(solution)/shard_map/ppermute | solution.py:541
  14.4 0.4 %collective-permute-start.5 = (f32[40,128]{1,0:T(8,128)S(1)}, f32[40,128]{1,0:T(8,128)S(1)}, u32[]{:S(2)}, u32[]{:S(2)}) collective-permute-start(f32[40,128]{1,0:T(8,128)S(1)} %get-tuple-element.52.r_1_), channel_id=1, source_target_pairs={{0,4},{8,12},{4,0},{12,8},{1,5},{9,13},{5,1},{13,9},{2,6},{10,14},... | collective-permute-start | bytes 61448 | tf_op jit(solution)/shard_map/ppermute | solution.py:541
  14.9 0.0 collective-permute-start.6
  14.9 1.5 %collective-permute-start.7 = (f32[24,128]{1,0:T(8,128)S(1)}, f32[24,128]{1,0:T(8,128)S(1)}, u32[]{:S(2)}, u32[]{:S(2)}) collective-permute-start(f32[24,128]{1,0:T(8,128)S(1)} %get-tuple-element.54.r_3_), channel_id=1, source_target_pairs={{0,1},{2,3},{1,0},{3,2},{4,5},{6,7},{5,4},{7,6},{8,9},{10,11},{9,8... | collective-permute-start | bytes 36872 | tf_op jit(solution)/shard_map/ppermute | solution.py:541
  16.4 1.4 %shard_map.189.r_1_ = f32[32,64,128]{2,1,0:T(8,128)S(1)} custom-call(f32[200,128]{1,0:T(8,128)S(1)} %get-tuple-element.55.state.r_12_.r_0_, bf16[256,256]{1,0:T(8,128)(2,1)S(1)} %copy-done.1, bf16[256,256]{1,0:T(8,128)(2,1)S(1)} %copy-done, f32[32,64,128]{2,1,0:T(8,128)S(1)} %get-tuple-element.56.inv, f32[64,128]{1,0:T(8,128)S(1)} %copy-done.4, ...), custom_call_target="tpu_custom_call" | custom-call | tf_op jit(solution)/shard_map/pallas_call | solution.py:619
  17.8 0.3 %collective-permute-done.6.r_6_ = f32[24,128]{1,0:T(8,128)S(1)} collective-permute-done((f32[24,128]{1,0:T(8,128)S(1)}, f32[24,128]{1,0:T(8,128)S(1)}, u32[]{:S(2)}, u32[]{:S(2)}) %collective-permute-start.6) | collective-permute-done | bytes 12320 | tf_op jit(solution)/shard_map/ppermute | solution.py:541
  18.1 0.0 collective-permute-done.7.r_7_
  18.1 0.4 %collective-permute-done.4.r_4_ = f32[40,128]{1,0:T(8,128)S(1)} collective-permute-done((f32[40,128]{1,0:T(8,128)S(1)}, f32[40,128]{1,0:T(8,128)S(1)}, u32[]{:S(2)}, u32[]{:S(2)}) %collective-permute-start.4) | collective-permute-done | bytes 20512 | tf_op jit(solution)/shard_map/ppermute | solution.py:541
  18.6 0.0 collective-permute-done.5.r_5_
  18.6 0.4 %shard_map.190 = (f32[200,128]{1,0:T(8,128)S(1)}, f32[40,128]{1,0:T(8,128)S(1)}, f32[40,128]{1,0:T(8,128)S(1)}, f32[24,128]{1,0:T(8,128)S(1)}, f32[24,128]{1,0:T(8,128)S(1)}) custom-call(f32[40,128]{1,0:T(8,128)S(1)} %get-tuple-element.51.r_0_, f32[40,128]{1,0:T(8,128)S(1)} %get-tuple-element.52.r_1_, f32[24,128]{1,0:T(8,128)S(1)} %get-tuple-element.53.r_2_, ...), custom_call_target="tpu_custom_call" | custom-call | tf_op jit(solution)/shard_map/pallas_call | solution.py:621
  19.0 2.5 %collective-permute-start.10 = (f32[40,128]{1,0:T(8,128)S(1)}, f32[40,128]{1,0:T(8,128)S(1)}, u32[]{:S(2)}, u32[]{:S(2)}) collective-permute-start(f32[40,128]{1,0:T(8,128)S(1)} %get-tuple-element.62.r_2_), channel_id=1, source_target_pairs={{4,8},{12,0},{8,4},{0,12},{5,9},{13,1},{9,5},{1,13},{6,10},{14,2},... | collective-permute-start | bytes 61448 | tf_op jit(solution)/shard_map/ppermute | solution.py:541
  21.4 0.2 collective-permute-start.9
  21.6 1.8 %collective-permute-start.8 = (f32[40,128]{1,0:T(8,128)S(1)}, f32[40,128]{1,0:T(8,128)S(1)}, u32[]{:S(2)}, u32[]{:S(2)}) collective-permute-start(f32[40,128]{1,0:T(8,128)S(1)} %get-tuple-element.63.r_3_), channel_id=1, source_target_pairs={{0,4},{8,12},{4,0},{12,8},{1,5},{9,13},{5,1},{13,9},{2,6},{10,14},... | collective-permute-start | bytes 61448 | tf_op jit(solution)/shard_map/ppermute | solution.py:541
  23.5 1.4 %shard_map.191.r_2_ = f32[32,64,128]{2,1,0:T(8,128)S(1)} custom-call(f32[200,128]{1,0:T(8,128)S(1)} %get-tuple-element.64.state.r_1_, bf16[256,256]{1,0:T(8,128)(2,1)S(1)} %copy-done.1, bf16[256,256]{1,0:T(8,128)(2,1)S(1)} %copy-done, f32[32,64,128]{2,1,0:T(8,128)S(1)} %get-tuple-element.56.inv, f32[64,128]{1,0:T(8,128)S(1)} %copy-done.4, ...), custom_call_target="tpu_custom_call" | custom-call | tf_op jit(solution)/shard_map/pallas_call | solution.py:624
  24.8 0.0 copy-start.11
  24.8 0.1 collective-permute-start.11
  24.9 0.0 collective-permute-done.10.r_5_
  24.9 1.2 %collective-permute-done.9 = f32[40,128]{1,0:T(8,128)S(1)} collective-permute-done((f32[40,128]{1,0:T(8,128)S(1)}, f32[40,128]{1,0:T(8,128)S(1)}, u32[]{:S(2)}, u32[]{:S(2)}) %collective-permute-start.9) | collective-permute-done | bytes 20512 | tf_op jit(solution)/shard_map/ppermute | solution.py:535
  26.1 0.0 collective-permute-done.8.r_6_
  26.1 0.6 %collective-permute-start.14 = (f32[8,128]{1,0:T(8,128)S(1)}, f32[8,128]{1,0:T(8,128)S(1)}, u32[]{:S(2)}, u32[]{:S(2)}) collective-permute-start(f32[8,128]{1,0:T(8,128)S(1)} %add_add_fusion.r_5_), channel_id=1, source_target_pairs={{1,2},{3,0},{2,1},{0,3},{5,6},{7,4},{6,5},{4,7},{9,10},{11,8},{10,... | collective-permute-start | bytes 12296 | tf_op jit(solution)/shard_map/ppermute | solution.py:541
  26.8 1.4 %collective-permute-start.13 = (f32[8,128]{1,0:T(8,128)S(1)}, f32[8,128]{1,0:T(8,128)S(1)}, u32[]{:S(2)}, u32[]{:S(2)}) collective-permute-start(f32[8,128]{1,0:T(8,128)S(1)} %add_add_fusion.r_5_), channel_id=1, source_target_pairs={{0,2},{1,3},{2,0},{3,1},{4,6},{5,7},{6,4},{7,5},{8,10},{9,11},{10,... | collective-permute-start | bytes 12296 | tf_op jit(solution)/shard_map/ppermute | solution.py:535
  28.1 0.0 collective-permute-start.12
  28.1 0.0 collective-permute-done.11.r_7_
  28.2 0.9 %shard_map.192 = (f32[3,32,128]{2,1,0:T(8,128)S(1)}, f32[3,64,128]{2,1,0:T(8,128)S(1)}) custom-call(f32[200,128]{1,0:T(8,128)S(1)} %get-tuple-element.55.state.r_12_.r_0_, f32[200,128]{1,0:T(8,128)S(1)} %get-tuple-element.64.state.r_1_, f32[40,128]{1,0:T(8,128)S(1)} %get-tuple-element.62.r_2_, f32[40,128]{1,0:T(8,128)S(1)} %get-tuple-element.63.r_3_, ...), custom_call_target="tpu_custom_call" | custom-call | tf_op jit(solution)/shard_map/pallas_call | solution.py:627
  29.1 0.2 collective-permute-done.14.r_8_
  29.2 1.1 %collective-permute-done.13.r_7_ = f32[8,128]{1,0:T(8,128)S(1)} collective-permute-done((f32[8,128]{1,0:T(8,128)S(1)}, f32[8,128]{1,0:T(8,128)S(1)}, u32[]{:S(2)}, u32[]{:S(2)}) %collective-permute-start.13) | collective-permute-done | bytes 4128 | tf_op jit(solution)/shard_map/ppermute | solution.py:535
  30.4 0.0 collective-permute-done.12.r_6_
  30.4 1.5 %shard_map.193 = (f32[32,64,128]{2,1,0:T(8,128)}, f32[32,64,128]{2,1,0:T(8,128)}) custom-call(f32[32,64,128]{2,1,0:T(8,128)S(1)} %get-tuple-element.45.r_0_, f32[32,64,128]{2,1,0:T(8,128)S(1)} %shard_map.189.r_1_, f32[32,64,128]{2,1,0:T(8,128)S(1)} %shard_map.191.r_2_, f32[3,32,128]{2,1,0:T(8,128)S(1)} %get-tuple-element.68.r_3_, ...), custom_call_target="tpu_custom_call" | custom-call | tf_op jit(solution)/shard_map/pallas_call | solution.py:630
  (26 shorter events, 0.1 us)
Async XLA Ops:
  0.6 7.7 %copy-start.8 = (bf16[256,128]{1,0:T(8,128)(2,1)S(1)}, bf16[256,128]{1,0:T(8,128)(2,1)}, u32[]{:S(2)}) copy-start(bf16[256,128]{1,0:T(8,128)(2,1)} %constant.34.clone.r_1_) | copy-start | bytes 196612
  3.2 9.0 %collective-permute-start = (f32[40,128]{1,0:T(8,128)S(1)}, f32[40,128]{1,0:T(8,128)S(1)}, u32[]{:S(2)}, u32[]{:S(2)}) collective-permute-start(f32[40,128]{1,0:T(8,128)S(1)} %get-tuple-element.38.r_2_.r_0_), channel_id=1, source_target_pairs={{4,8},{12,0},{8,4},{0,12},{5,9},{13,1},{9,5},{1,13},{6,10},{14,2},... | collective-permute-start | bytes 61448 | tf_op jit(solution)/shard_map/ppermute | solution.py:541
  8.3 3.9 %collective-permute-start.1 = (f32[40,128]{1,0:T(8,128)S(1)}, f32[40,128]{1,0:T(8,128)S(1)}, u32[]{:S(2)}, u32[]{:S(2)}) collective-permute-start(f32[40,128]{1,0:T(8,128)S(1)} %get-tuple-element.39.r_3_.r_1_), channel_id=1, source_target_pairs={{0,4},{8,12},{4,0},{12,8},{1,5},{9,13},{5,1},{13,9},{2,6},{10,14},... | collective-permute-start | bytes 61448 | tf_op jit(solution)/shard_map/ppermute | solution.py:541
  8.3 2.3 %copy-start = (bf16[256,256]{1,0:T(8,128)(2,1)S(1)}, bf16[256,256]{1,0:T(8,128)(2,1)}, u32[]{:S(2)}) copy-start(bf16[256,256]{1,0:T(8,128)(2,1)} %constant.33.clone.exw_h.exw) | copy-start | bytes 393220
  8.3 2.3 %copy-start.1 = (bf16[256,256]{1,0:T(8,128)(2,1)S(1)}, bf16[256,256]{1,0:T(8,128)(2,1)}, u32[]{:S(2)}) copy-start(bf16[256,256]{1,0:T(8,128)(2,1)} %constant.32.clone.eyw_h.eyw) | copy-start | bytes 393220
  8.3 2.3 %copy-start.10 = (f32[64,128]{1,0:T(8,128)S(1)}, f32[64,128]{1,0:T(8,128)}, u32[]{:S(2)}) copy-start(f32[64,128]{1,0:T(8,128)} %constant.41.clone.lxz) | copy-start | bytes 98308
  8.4 2.3 %copy-start.12 = (f32[32,128]{1,0:T(8,128)S(1)}, f32[32,128]{1,0:T(8,128)}, u32[]{:S(2)}) copy-start(f32[32,128]{1,0:T(8,128)} %constant.42.clone.ly) | copy-start | bytes 49156
  9.0 3.3 %collective-permute-start.2 = (f32[24,128]{1,0:T(8,128)S(1)}, f32[24,128]{1,0:T(8,128)S(1)}, u32[]{:S(2)}, u32[]{:S(2)}) collective-permute-start(f32[24,128]{1,0:T(8,128)S(1)} %get-tuple-element.41.r_2_), channel_id=1, source_target_pairs={{1,2},{3,0},{2,1},{0,3},{5,6},{7,4},{6,5},{4,7},{9,10},{11,8},{10,... | collective-permute-start | bytes 36872 | tf_op jit(solution)/shard_map/ppermute | solution.py:541
  9.7 2.6 %collective-permute-start.3 = (f32[24,128]{1,0:T(8,128)S(1)}, f32[24,128]{1,0:T(8,128)S(1)}, u32[]{:S(2)}, u32[]{:S(2)}) collective-permute-start(f32[24,128]{1,0:T(8,128)S(1)} %get-tuple-element.42.r_3_), channel_id=1, source_target_pairs={{0,1},{2,3},{1,0},{3,2},{4,5},{6,7},{5,4},{7,6},{8,9},{10,11},{9,8... | collective-permute-start | bytes 36872 | tf_op jit(solution)/shard_map/ppermute | solution.py:541
  10.7 1.6 %copy-start.2 = (f32[5,64,128]{2,1,0:T(8,128)S(1)}, f32[5,64,128]{2,1,0:T(8,128)}, u32[]{:S(2)}) copy-start(f32[5,64,128]{2,1,0:T(8,128)} %constant.44.clone.r_10_) | copy-start | bytes 491524
  10.7 1.6 %copy-start.3 = (f32[5,32,128]{2,1,0:T(8,128)S(1)}, f32[5,32,128]{2,1,0:T(8,128)}, u32[]{:S(2)}) copy-start(f32[5,32,128]{2,1,0:T(8,128)} %constant.43.clone.r_9_) | copy-start | bytes 245764
  10.7 1.6 %copy-start.13 = (f32[8,128]{1,0:T(8,128)S(1)}, f32[8,128]{1,0:T(8,128)}, u32[]{:S(2)}) copy-start(f32[8,128]{1,0:T(8,128)} %constant.45.clone.r_11_) | copy-start | bytes 12292
  12.3 4.1 %copy-start.4 = (f32[64,128]{1,0:T(8,128)S(1)}, f32[64,128]{1,0:T(8,128)}, u32[]{:S(2)}) copy-start(f32[64,128]{1,0:T(8,128)} %constant.47.clone.sx0_h.sx0) | copy-start | bytes 98308
  12.3 4.1 %copy-start.5 = (bf16[256,128]{1,0:T(8,128)(2,1)S(1)}, bf16[256,128]{1,0:T(8,128)(2,1)}, u32[]{:S(2)}) copy-start(bf16[256,128]{1,0:T(8,128)(2,1)} %constant.35.clone.colw) | copy-start | bytes 196612
  12.7 5.8 %collective-permute-start.4 = (f32[40,128]{1,0:T(8,128)S(1)}, f32[40,128]{1,0:T(8,128)S(1)}, u32[]{:S(2)}, u32[]{:S(2)}) collective-permute-start(f32[40,128]{1,0:T(8,128)S(1)} %get-tuple-element.51.r_0_), channel_id=1, source_target_pairs={{4,8},{12,0},{8,4},{0,12},{5,9},{13,1},{9,5},{1,13},{6,10},{14,2},... | collective-permute-start | bytes 61448 | tf_op jit(solution)/shard_map/ppermute | solution.py:541
  14.4 2.0 %copy-start.9 = (f32[8,128]{1,0:T(8,128)S(1)}, f32[8,128]{1,0:T(8,128)}, u32[]{:S(2)}) copy-start(f32[8,128]{1,0:T(8,128)} %constant.46.clone.line_h.line) | copy-start | bytes 12292
  14.4 4.1 %collective-permute-start.5 = (f32[40,128]{1,0:T(8,128)S(1)}, f32[40,128]{1,0:T(8,128)S(1)}, u32[]{:S(2)}, u32[]{:S(2)}) collective-permute-start(f32[40,128]{1,0:T(8,128)S(1)} %get-tuple-element.52.r_1_), channel_id=1, source_target_pairs={{0,4},{8,12},{4,0},{12,8},{1,5},{9,13},{5,1},{13,9},{2,6},{10,14},... | collective-permute-start | bytes 61448 | tf_op jit(solution)/shard_map/ppermute | solution.py:541
  14.9 3.2 %collective-permute-start.6 = (f32[24,128]{1,0:T(8,128)S(1)}, f32[24,128]{1,0:T(8,128)S(1)}, u32[]{:S(2)}, u32[]{:S(2)}) collective-permute-start(f32[24,128]{1,0:T(8,128)S(1)} %get-tuple-element.53.r_2_), channel_id=1, source_target_pairs={{1,2},{3,0},{2,1},{0,3},{5,6},{7,4},{6,5},{4,7},{9,10},{11,8},{10,... | collective-permute-start | bytes 36872 | tf_op jit(solution)/shard_map/ppermute | solution.py:541
  14.9 3.2 %collective-permute-start.7 = (f32[24,128]{1,0:T(8,128)S(1)}, f32[24,128]{1,0:T(8,128)S(1)}, u32[]{:S(2)}, u32[]{:S(2)}) collective-permute-start(f32[24,128]{1,0:T(8,128)S(1)} %get-tuple-element.54.r_3_), channel_id=1, source_target_pairs={{0,1},{2,3},{1,0},{3,2},{4,5},{6,7},{5,4},{7,6},{8,9},{10,11},{9,8... | collective-permute-start | bytes 36872 | tf_op jit(solution)/shard_map/ppermute | solution.py:541
  19.0 5.9 %collective-permute-start.10 = (f32[40,128]{1,0:T(8,128)S(1)}, f32[40,128]{1,0:T(8,128)S(1)}, u32[]{:S(2)}, u32[]{:S(2)}) collective-permute-start(f32[40,128]{1,0:T(8,128)S(1)} %get-tuple-element.62.r_2_), channel_id=1, source_target_pairs={{4,8},{12,0},{8,4},{0,12},{5,9},{13,1},{9,5},{1,13},{6,10},{14,2},... | collective-permute-start | bytes 61448 | tf_op jit(solution)/shard_map/ppermute | solution.py:541
  21.4 4.7 %collective-permute-start.9 = (f32[40,128]{1,0:T(8,128)S(1)}, f32[40,128]{1,0:T(8,128)S(1)}, u32[]{:S(2)}, u32[]{:S(2)}) collective-permute-start(f32[40,128]{1,0:T(8,128)S(1)} %get-tuple-element.63.r_3_), channel_id=1, source_target_pairs={{0,8},{4,12},{8,0},{12,4},{1,9},{5,13},{9,1},{13,5},{2,10},{6,14},... | collective-permute-start | bytes 61448 | tf_op jit(solution)/shard_map/ppermute | solution.py:535
  21.6 4.5 %collective-permute-start.8 = (f32[40,128]{1,0:T(8,128)S(1)}, f32[40,128]{1,0:T(8,128)S(1)}, u32[]{:S(2)}, u32[]{:S(2)}) collective-permute-start(f32[40,128]{1,0:T(8,128)S(1)} %get-tuple-element.63.r_3_), channel_id=1, source_target_pairs={{0,4},{8,12},{4,0},{12,8},{1,5},{9,13},{5,1},{13,9},{2,6},{10,14},... | collective-permute-start | bytes 61448 | tf_op jit(solution)/shard_map/ppermute | solution.py:541
  23.4 4.7 %copy-start.6 = (f32[128,128]{1,0:T(8,128)S(1)}, f32[128,128]{1,0:T(8,128)}, u32[]{:S(2)}) copy-start(f32[128,128]{1,0:T(8,128)} %constant.39.clone.r_11_) | copy-start | bytes 196612
  23.4 4.7 %copy-start.7 = (f32[128,128]{1,0:T(8,128)S(1)}, f32[128,128]{1,0:T(8,128)}, u32[]{:S(2)}) copy-start(f32[128,128]{1,0:T(8,128)} %constant.36.clone.r_8_) | copy-start | bytes 196612
  23.5 4.7 %copy-start.14 = (f32[32,32]{1,0:T(8,128)S(1)}, f32[32,32]{1,0:T(8,128)}, u32[]{:S(2)}) copy-start(f32[32,32]{1,0:T(8,128)} %constant.38.clone.r_10_) | copy-start | bytes 12292
  24.8 3.3 %copy-start.11 = (f32[64,64]{1,0:T(8,128)S(1)}, f32[64,64]{1,0:T(8,128)}, u32[]{:S(2)}) copy-start(f32[64,64]{1,0:T(8,128)} %constant.37.clone.r_9_) | copy-start | bytes 49156
  24.8 3.3 %collective-permute-start.11 = (f32[24,128]{1,0:T(8,128)S(1)}, f32[24,128]{1,0:T(8,128)S(1)}, u32[]{:S(2)}, u32[]{:S(2)}) collective-permute-start(f32[24,128]{1,0:T(8,128)S(1)} %get-tuple-element.67), channel_id=1, source_target_pairs={{0,1},{1,2},{2,3},{3,0},{4,5},{5,6},{6,7},{7,4},{8,9},{9,10},{10,1... | collective-permute-start | bytes 36872 | tf_op jit(solution)/shard_map/ppermute | solution.py:535
  26.1 3.1 %collective-permute-start.14 = (f32[8,128]{1,0:T(8,128)S(1)}, f32[8,128]{1,0:T(8,128)S(1)}, u32[]{:S(2)}, u32[]{:S(2)}) collective-permute-start(f32[8,128]{1,0:T(8,128)S(1)} %add_add_fusion.r_5_), channel_id=1, source_target_pairs={{1,2},{3,0},{2,1},{0,3},{5,6},{7,4},{6,5},{4,7},{9,10},{11,8},{10,... | collective-permute-start | bytes 12296 | tf_op jit(solution)/shard_map/ppermute | solution.py:541
  26.8 3.6 %collective-permute-start.13 = (f32[8,128]{1,0:T(8,128)S(1)}, f32[8,128]{1,0:T(8,128)S(1)}, u32[]{:S(2)}, u32[]{:S(2)}) collective-permute-start(f32[8,128]{1,0:T(8,128)S(1)} %add_add_fusion.r_5_), channel_id=1, source_target_pairs={{0,2},{1,3},{2,0},{3,1},{4,6},{5,7},{6,4},{7,5},{8,10},{9,11},{10,... | collective-permute-start | bytes 12296 | tf_op jit(solution)/shard_map/ppermute | solution.py:535
  28.1 2.2 %collective-permute-start.12 = (f32[8,128]{1,0:T(8,128)S(1)}, f32[8,128]{1,0:T(8,128)S(1)}, u32[]{:S(2)}, u32[]{:S(2)}) collective-permute-start(f32[8,128]{1,0:T(8,128)S(1)} %add_add_fusion.r_5_), channel_id=1, source_target_pairs={{0,1},{2,3},{1,0},{3,2},{4,5},{6,7},{5,4},{7,6},{8,9},{10,11},{9,8... | collective-permute-start | bytes 12296 | tf_op jit(solution)/shard_map/ppermute | solution.py:541

commit v7 on v6

--- a/solution.py
+++ b/solution.py
@@ -341,44 +341,57 @@
     return tuple(state[s[i], :] for i in range(4)) + tuple(state[at + i:at + i + 1, :] for i in range(3))
 
 
-def schur_kernel(depth, want_moments, *refs):
-    own, got = [r[...] for r in refs[0:4]], [r[...] for r in refs[4:8]]
-    inv2, rowt, colt, crnt = refs[8:12]
-    rest = list(refs[12:])
-    before = rest.pop(0) if want_moments else None
-    state, *outs = rest[:5]
+def schur_kernel(depth, mode, *refs):
+    inv2, rowt, colt, crnt = refs[:4]
+    rest = list(refs[4:])
     part, odd_rows, even_rows = rest[-3:]
-    row, row_n, col, col_n, c00, cx0, c0y = assemble(depth, own, got)
-    rows, cols = row.shape[0], col.shape[0]
-    s = sizes(rows, cols)
-    for i, piece in enumerate((row, row_n, col, col_n)):
-        state[s[i], :] = piece
-    state[s[4]:s[4] + 8, :] = jnp.concatenate([c00, cx0, c0y, jnp.zeros((5, 128), F32)], 0)
+    with_rows, with_cols, want_moments = mode != "cols", mode != "rows", mode == "last"
+    if mode == "cols":
+        state, *outs = rest[:3]
+        cols = inv2.shape[1]
+        rows = inv2.shape[0]
+        row, row_n, col, col_n, c00, cx0, c0y = unpacked_state(state, rows, cols)
+    else:
+        own, got = [r[...] for r in rest[0:4]], [r[...] for r in rest[4:8]]
+        rest = rest[8:]
+        before = rest.pop(0) if want_moments else None
+        state, *outs = rest[:-3]
+        row, row_n, col, col_n, c00, cx0, c0y = assemble(depth, own, got)
+        rows, cols = row.shape[0], col.shape[0]
+        s = sizes(rows, cols)
+        for i, piece in enumerate((row, row_n, col, col_n)):
+            state[s[i], :] = piece
+        state[s[4]:s[4] + 8, :] = jnp.concatenate([c00, cx0, c0y, jnp.zeros((5, 128), F32)], 0)
     sy, sys, g_odd, g_even, d_row = (rowt[i] for i in range(5))
     sx, sxs, h_odd, h_even, d_col = (colt[i] for i in range(5))
     row_p, row_m, col_p, col_m = row + row_n, row - row_n, col + col_n, col - col_n
-    odd_rows[...] = row_p * sy
-    even_rows[...] = row_m * sy
+    if with_cols:
+        odd_rows[...] = row_p * sy
+        even_rows[...] = row_m * sy
     col_w = (col_m * sx, col_p * sx)
     odd = lax.broadcasted_iota(jnp.int32, (8, 128), 0) % 2 == 1
     acc = [None, None]
     for r in range(rows):
         table = inv2[r].reshape(cols // 8, 8, 128)
-        part[r] = jnp.sum(table * col_w[r % 2].reshape(cols // 8, 8, 128), 0)
-        pick = jnp.where(odd, odd_rows[r:r + 1, :], even_rows[r:r + 1, :])
-        term = table * pick[None]
-        acc[r % 2] = term if acc[r % 2] is None else acc[r % 2] + term
-    row_s, row_d = sub_sums(part)
-    acc_s = spread((acc[1] + acc[0]).reshape(cols, 128), depth)
-    acc_d = spread((acc[1] - acc[0]).reshape(cols, 128), depth)
-    diag_o, diag_e = g_odd * row_p, g_even * row_m
-    x_near = sy * row_s + (diag_o + diag_e)
-    x_far = sy * row_d + (diag_o - diag_e)
-    diag_o, diag_e = h_odd * col_p, h_even * col_m
-    y_near = sx * acc_s + (diag_o + diag_e)
-    y_far = sx * acc_d + (diag_o - diag_e)
-    row_img = d_row * row - sy * c00 - sys * c0y - x_near
-    col_img = d_col * col - sx * c00 - sxs * cx0 - y_near
+        if with_rows:
+            part[r] = jnp.sum(table * col_w[r % 2].reshape(cols // 8, 8, 128), 0)
+        if with_cols:
+            pick = jnp.where(odd, odd_rows[r:r + 1, :], even_rows[r:r + 1, :])
+            term = table * pick[None]
+            acc[r % 2] = term if acc[r % 2] is None else acc[r % 2] + term
+    if with_rows:
+        row_s, row_d = sub_sums(part)
+        diag_o, diag_e = g_odd * row_p, g_even * row_m
+        x_near = sy * row_s + (diag_o + diag_e)
+        x_far = sy * row_d + (diag_o - diag_e)
+        row_img = d_row * row - sy * c00 - sys * c0y - x_near
+    if with_cols:
+        acc_s = spread((acc[1] + acc[0]).reshape(cols, 128), depth)
+        acc_d = spread((acc[1] - acc[0]).reshape(cols, 128), depth)
+        diag_o, diag_e = h_odd * col_p, h_even * col_m
+        y_near = sx * acc_s + (diag_o + diag_e)
+        y_far = sx * acc_d + (diag_o - diag_e)
+        col_img = d_col * col - sx * c00 - sxs * cx0 - y_near
     row_end0 = spread(total(sy * row), depth)
     row_end1 = spread(total(sys * row), depth)
     row_end1n = spread(total(sys * row_n), depth)
@@ -386,10 +399,14 @@
     col_end1 = total(sxs * col)
     col_end1n = total(sxs * col_n)
     q00 = crnt[0:1, :] * c00 - row_end0 - col_end0
-    px = with_tail(row_img, [q00])
-    nx = with_tail(-x_far, [-col_end1, -col_end1n])
-    py = with_tail(pack(col_img, depth), [q00])
-    ny = with_tail(pack(-y_far, depth), [-row_end1, -row_end1n])
+    if mode == "rows":
+        px = with_tail(row_img, [q00])
+        nx = with_tail(-x_far, [-col_end1, -col_end1n])
+        values = swapped("gx", nx, px)
+    if with_cols:
+        py = with_tail(pack(col_img, depth), [q00])
+        ny = with_tail(pack(-y_far, depth), [-row_end1, -row_end1n])
+        values = swapped("gy", ny, py)
     if want_moments:
         row0, _, col0, _, c000, _, _ = unpacked_state(before, rows, cols)
         share = depth / 128.0
@@ -404,8 +421,8 @@
         moments = [dot(v0, v0), dot(v0, v1), dot(v1, v1), m3]
         px = with_tail(row_img, [q00, q00, q00, q00] + moments)
         nx = with_tail(-x_far, [-col_end1, -col_end1n, c00, c00] + moments)
-    sides = (ny, py) if want_moments else swapped("gy", ny, py)
-    for ref, value in zip(outs, swapped("gx", nx, px) + sides):
+        values = swapped("gx", nx, px) + (ny, py)
+    for ref, value in zip(outs, values):
         ref[...] = value
 
 
@@ -612,13 +629,14 @@
     *got, cells_b = lax.optimization_barrier((*got, cells_b))
     tables = (inv2, tab["rowt"], tab["colt"], tab["crnt"])
     scratch = [(rows, 8, 128), (rows, 128), (rows, 128)]
-    s0, *own = call(lambda *r: schur_kernel(depth, False, *r), [state] + msgs, scratch)(*own, *got, *tables)
+    s0, *own = call(lambda *r: schur_kernel(depth, "rows", *r), [state] + msgs[:2], scratch)(*tables, *own, *got)
+    own += call(lambda *r: schur_kernel(depth, "cols", *r), msgs[2:], scratch)(*tables, s0)
     got = exchange(*own)
     extend = call(extend_kernel, [block], [block])
     backs = (tab["eyw"], tab["exw"], inv, tab["sx0"], tab["colw"], tab["line"])
     cells_0 = extend(s0, *backs)[0]
     *got, cells_0 = lax.optimization_barrier((*got, cells_0))
-    s1, *own = call(lambda *r: schur_kernel(depth, True, *r), [state] + msgs, scratch)(*own, *got, *tables, s0)
+    s1, *own = call(lambda *r: schur_kernel(depth, "last", *r), [state] + msgs, scratch)(*tables, *own, *got, s0)
     parts, got_bx, got_ax = reduced_x(*own[:2])
     from_py = shifted(own[2], "gy", 1)
     cells_1 = extend(s1, *backs)[0]

time: 32 us -> 32 us (level)
    pallas_call x2 -> x3, Pallas kernels: 0.83 us -> 1.04 us  [the longest x1 0.45 us: on_device(): call(lambda *r: schur_kernel(depth, 'last', *r), [state] + msgs, scratch)]
where the time goes in v7:
time: 32 us; the launch traced here: 31.9 us
  starting transfers between devices  17 us (53%)
  Pallas kernels  10.5 us (33%)
  waiting for transfers between devices  3.46 us (11%)
  between operations  0.87 us (3%)
    ppermute x12, starting transfers between devices, swap(): return lax.ppermute(value, axis, pairs + [(j, i) for i, j in pairs])  15.3 us
    pallas_call x1, Pallas kernels, on_device(): call(front_kernel, [block, block, jax.ShapeDtypeStruct((depth * width, 2...  2.58 us
    ppermute x3, waiting for transfers between devices, shifted(): return lax.ppermute(value, axis, [(i, (i + by) % n) for i in range(n)])  2.33 us
    ppermute x3, starting transfers between devices, shifted(): return lax.ppermute(value, axis, [(i, (i + by) % n) for i in range(n)])  1.61 us
    pallas_call x1, Pallas kernels, on_device(): call(lambda *r: final_kernel(len(parts), *r), [block, block], [block, blo...  1.53 us
    pallas_call x1, Pallas kernels, on_device(): cells_1 = extend(s1, *backs)[0]  1.38 us
    pallas_call x1, Pallas kernels, on_device(): cells_0 = extend(s0, *backs)[0]  1.38 us
    ppermute x12, waiting for transfers between devices, swap(): return lax.ppermute(value, axis, pairs + [(j, i) for i, j in pairs])  1.13 us
  transfers between devices with their start and end apart: 15, of which 6 were waited for; matrix products, arithmetic and copies ran while one was open for 0% of the time, Pallas kernels for 17%

profile of v7, /device:TPU:0, one launch (start us, length us, event | category | flops | bytes accessed | tf_op | source)
XLA Modules:
  0.0 31.9 jit_solution(1451156156811228240)
XLA Ops:
  0.6 0.0 copy-start.8
  0.6 2.6 %shard_map.185 = (f32[32,64,128]{2,1,0:T(8,128)S(1)}, f32[32,64,128]{2,1,0:T(8,128)S(1)}, bf16[2048,256]{1,0:T(8,128)(2,1)S(1)}, f32[40,128]{1,0:T(8,128)S(1)}, f32[40,128]{1,0:T(8,128)S(1)}) custom-call(f32[32,64,128]{2,1,0:T(8,128)} %charge_h.1, f32[2,64,128]{2,1,0:T(8,128)} %surf_h.1, bf16[256,256]{1,0:T(8,128)(2,1)} %constant.32.clone.eyw_h.eyw, ...), custom_call_target="tpu_custom_call" | custom-call | tf_op jit(solution)/shard_map/pallas_call | solution.py:619
  3.2 5.1 %collective-permute-start = (f32[40,128]{1,0:T(8,128)S(1)}, f32[40,128]{1,0:T(8,128)S(1)}, u32[]{:S(2)}, u32[]{:S(2)}) collective-permute-start(f32[40,128]{1,0:T(8,128)S(1)} %get-tuple-element.38.r_2_.r_4_), channel_id=1, source_target_pairs={{4,8},{12,0},{8,4},{0,12},{5,9},{13,1},{9,5},{1,13},{6,10},{14,2},... | collective-permute-start | bytes 61448 | tf_op jit(solution)/shard_map/ppermute | solution.py:558
  8.3 0.0 collective-permute-start.1
  8.4 0.0 copy-start.11
  8.4 0.0 copy-start.13
  8.4 0.6 %shard_map.186 = (f32[24,128]{1,0:T(8,128)S(1)}, f32[24,128]{1,0:T(8,128)S(1)}) custom-call(bf16[2048,256]{1,0:T(8,128)(2,1)S(1)} %get-tuple-element.40.r_0_, bf16[256,128]{1,0:T(8,128)(2,1)S(1)} %copy-done.8, f32[40,128]{1,0:T(8,128)S(1)} %get-tuple-element.38.r_2_.r_4_, f32[40,128]{1,0:T(8,128)S(1)} %get-tuple-element.39.r_3_.r_5_), custom_call_target="tpu_custom_call" | custom-call | tf_op jit(solution)/shard_map/pallas_call | solution.py:624
  9.0 0.7 %collective-permute-start.2 = (f32[24,128]{1,0:T(8,128)S(1)}, f32[24,128]{1,0:T(8,128)S(1)}, u32[]{:S(2)}, u32[]{:S(2)}) collective-permute-start(f32[24,128]{1,0:T(8,128)S(1)} %get-tuple-element.41.r_6_), channel_id=1, source_target_pairs={{1,2},{3,0},{2,1},{0,3},{5,6},{7,4},{6,5},{4,7},{9,10},{11,8},{10,... | collective-permute-start | bytes 36872 | tf_op jit(solution)/shard_map/ppermute | solution.py:558
  9.7 1.0 %collective-permute-start.3 = (f32[24,128]{1,0:T(8,128)S(1)}, f32[24,128]{1,0:T(8,128)S(1)}, u32[]{:S(2)}, u32[]{:S(2)}) collective-permute-start(f32[24,128]{1,0:T(8,128)S(1)} %get-tuple-element.42.r_7_), channel_id=1, source_target_pairs={{0,1},{2,3},{1,0},{3,2},{4,5},{6,7},{5,4},{7,6},{8,9},{10,11},{9,8... | collective-permute-start | bytes 36872 | tf_op jit(solution)/shard_map/ppermute | solution.py:558
  10.7 0.0 copy-start.2
  10.7 0.0 copy-start.3
  10.7 0.0 copy-start.10
  10.7 1.1 %shard_map.187 = (f32[32,64,128]{2,1,0:T(8,128)S(1)}, f32[32,64,128]{2,1,0:T(8,128)S(1)}) custom-call(f32[32,64,128]{2,1,0:T(8,128)S(1)} %get-tuple-element.43.base, bf16[256,256]{1,0:T(8,128)(2,1)S(1)} %copy-done.1, bf16[256,256]{1,0:T(8,128)(2,1)S(1)} %copy-done, f32[64,128]{1,0:T(8,128)S(1)} %copy-done.11, f32[32,128]{1,0:T(8,128)S(1)} %copy-done.13), custom_call_target="tpu_custom_call" | custom-call | tf_op jit(solution)/shard_map/pallas_call | solution.py:626
  11.8 0.5 %collective-permute-done.2.r_10_ = f32[24,128]{1,0:T(8,128)S(1)} collective-permute-done((f32[24,128]{1,0:T(8,128)S(1)}, f32[24,128]{1,0:T(8,128)S(1)}, u32[]{:S(2)}, u32[]{:S(2)}) %collective-permute-start.2) | collective-permute-done | bytes 12320 | tf_op jit(solution)/shard_map/ppermute | solution.py:558
  12.3 0.0 collective-permute-done.3.r_11_
  12.3 0.0 collective-permute-done.r_8_
  12.3 0.0 collective-permute-done.1.r_9_
  12.3 0.3 %shard_map.188 = (f32[200,128]{1,0:T(8,128)S(1)}, f32[40,128]{1,0:T(8,128)S(1)}, f32[40,128]{1,0:T(8,128)S(1)}) custom-call(f32[32,64,128]{2,1,0:T(8,128)S(1)} %get-tuple-element.46.r_0_, f32[5,32,128]{2,1,0:T(8,128)S(1)} %copy-done.3, f32[5,64,128]{2,1,0:T(8,128)S(1)} %copy-done.2, f32[8,128]{1,0:T(8,128)S(1)} %copy-done.10, ...), custom_call_target="tpu_custom_call" | custom-call | tf_op jit(solution)/shard_map/pallas_call | solution.py:632
  12.6 1.7 %collective-permute-start.4 = (f32[40,128]{1,0:T(8,128)S(1)}, f32[40,128]{1,0:T(8,128)S(1)}, u32[]{:S(2)}, u32[]{:S(2)}) collective-permute-start(f32[40,128]{1,0:T(8,128)S(1)} %get-tuple-element.51.r_4_), channel_id=1, source_target_pairs={{4,8},{12,0},{8,4},{0,12},{5,9},{13,1},{9,5},{1,13},{6,10},{14,2},... | collective-permute-start | bytes 61448 | tf_op jit(solution)/shard_map/ppermute | solution.py:558
  14.4 0.4 %collective-permute-start.5 = (f32[40,128]{1,0:T(8,128)S(1)}, f32[40,128]{1,0:T(8,128)S(1)}, u32[]{:S(2)}, u32[]{:S(2)}) collective-permute-start(f32[40,128]{1,0:T(8,128)S(1)} %get-tuple-element.52.r_5_), channel_id=1, source_target_pairs={{0,4},{8,12},{4,0},{12,8},{1,5},{9,13},{5,1},{13,9},{2,6},{10,14},... | collective-permute-start | bytes 61448 | tf_op jit(solution)/shard_map/ppermute | solution.py:558
  14.8 0.3 shard_map.189
  15.1 0.0 copy-start.9
  15.1 0.1 collective-permute-start.6
  15.2 1.5 %collective-permute-start.7 = (f32[24,128]{1,0:T(8,128)S(1)}, f32[24,128]{1,0:T(8,128)S(1)}, u32[]{:S(2)}, u32[]{:S(2)}) collective-permute-start(f32[24,128]{1,0:T(8,128)S(1)} %get-tuple-element.55.r_7_), channel_id=1, source_target_pairs={{0,1},{2,3},{1,0},{3,2},{4,5},{6,7},{5,4},{7,6},{8,9},{10,11},{9,8... | collective-permute-start | bytes 36872 | tf_op jit(solution)/shard_map/ppermute | solution.py:558
  16.7 1.4 %shard_map.190.r_1_ = f32[32,64,128]{2,1,0:T(8,128)S(1)} custom-call(f32[200,128]{1,0:T(8,128)S(1)} %get-tuple-element.53.r_4_.state.r_12_.r_0_, bf16[256,256]{1,0:T(8,128)(2,1)S(1)} %copy-done.1, bf16[256,256]{1,0:T(8,128)(2,1)S(1)} %copy-done, f32[32,64,128]{2,1,0:T(8,128)S(1)} %get-tuple-element.56.inv, f32[64,128]{1,0:T(8,128)S(1)} %copy-done.4, ...), custom_call_target="tpu_custom_call" | custom-call | tf_op jit(solution)/shard_map/pallas_call | solution.py:637
  18.1 0.3 collective-permute-done.6.r_10_
  18.4 0.0 collective-permute-done.7.r_11_
  18.4 0.1 collective-permute-done.4.r_8_
  18.5 0.0 collective-permute-done.5.r_9_
  18.5 0.4 %shard_map.191 = (f32[200,128]{1,0:T(8,128)S(1)}, f32[40,128]{1,0:T(8,128)S(1)}, f32[40,128]{1,0:T(8,128)S(1)}, f32[24,128]{1,0:T(8,128)S(1)}, f32[24,128]{1,0:T(8,128)S(1)}) custom-call(f32[32,64,128]{2,1,0:T(8,128)S(1)} %get-tuple-element.46.r_0_, f32[5,32,128]{2,1,0:T(8,128)S(1)} %copy-done.3, f32[5,64,128]{2,1,0:T(8,128)S(1)} %copy-done.2, ...), custom_call_target="tpu_custom_call" | custom-call | tf_op jit(solution)/shard_map/pallas_call | solution.py:639
  18.9 2.8 %collective-permute-start.10 = (f32[40,128]{1,0:T(8,128)S(1)}, f32[40,128]{1,0:T(8,128)S(1)}, u32[]{:S(2)}, u32[]{:S(2)}) collective-permute-start(f32[40,128]{1,0:T(8,128)S(1)} %get-tuple-element.62.r_2_), channel_id=1, source_target_pairs={{4,8},{12,0},{8,4},{0,12},{5,9},{13,1},{9,5},{1,13},{6,10},{14,2},... | collective-permute-start | bytes 61448 | tf_op jit(solution)/shard_map/ppermute | solution.py:558
  21.7 0.2 collective-permute-start.9
  21.9 1.5 %collective-permute-start.8 = (f32[40,128]{1,0:T(8,128)S(1)}, f32[40,128]{1,0:T(8,128)S(1)}, u32[]{:S(2)}, u32[]{:S(2)}) collective-permute-start(f32[40,128]{1,0:T(8,128)S(1)} %get-tuple-element.63.r_3_), channel_id=1, source_target_pairs={{0,4},{8,12},{4,0},{12,8},{1,5},{9,13},{5,1},{13,9},{2,6},{10,14},... | collective-permute-start | bytes 61448 | tf_op jit(solution)/shard_map/ppermute | solution.py:558
  23.4 1.4 %shard_map.192.r_2_ = f32[32,64,128]{2,1,0:T(8,128)S(1)} custom-call(f32[200,128]{1,0:T(8,128)S(1)} %get-tuple-element.64.state.r_1_, bf16[256,256]{1,0:T(8,128)(2,1)S(1)} %copy-done.1, bf16[256,256]{1,0:T(8,128)(2,1)S(1)} %copy-done, f32[32,64,128]{2,1,0:T(8,128)S(1)} %get-tuple-element.56.inv, f32[64,128]{1,0:T(8,128)S(1)} %copy-done.4, ...), custom_call_target="tpu_custom_call" | custom-call | tf_op jit(solution)/shard_map/pallas_call | solution.py:642
  24.8 0.0 copy-start.12
  24.8 0.1 collective-permute-start.11
  24.9 0.0 collective-permute-done.10.r_5_
  24.9 1.5 %collective-permute-done.9 = f32[40,128]{1,0:T(8,128)S(1)} collective-permute-done((f32[40,128]{1,0:T(8,128)S(1)}, f32[40,128]{1,0:T(8,128)S(1)}, u32[]{:S(2)}, u32[]{:S(2)}) %collective-permute-start.9) | collective-permute-done | bytes 20512 | tf_op jit(solution)/shard_map/ppermute | solution.py:552
  26.4 0.0 collective-permute-done.8.r_6_
  26.4 0.3 collective-permute-start.14
  26.7 1.4 %collective-permute-start.13 = (f32[8,128]{1,0:T(8,128)S(1)}, f32[8,128]{1,0:T(8,128)S(1)}, u32[]{:S(2)}, u32[]{:S(2)}) collective-permute-start(f32[8,128]{1,0:T(8,128)S(1)} %add_add_fusion.r_5_), channel_id=1, source_target_pairs={{0,2},{1,3},{2,0},{3,1},{4,6},{5,7},{6,4},{7,5},{8,10},{9,11},{10,... | collective-permute-start | bytes 12296 | tf_op jit(solution)/shard_map/ppermute | solution.py:552
  28.1 0.3 collective-permute-start.12
  28.4 0.0 collective-permute-done.11.r_7_
  28.4 0.9 %shard_map.193 = (f32[3,32,128]{2,1,0:T(8,128)S(1)}, f32[3,64,128]{2,1,0:T(8,128)S(1)}) custom-call(f32[200,128]{1,0:T(8,128)S(1)} %get-tuple-element.53.r_4_.state.r_12_.r_0_, f32[200,128]{1,0:T(8,128)S(1)} %get-tuple-element.64.state.r_1_, f32[40,128]{1,0:T(8,128)S(1)} %get-tuple-element.62.r_2_, f32[40,128]{1,0:T(8,128)S(1)} %get-tuple-element.63.r_3_, ...), custom_call_target="tpu_custom_call" | custom-call | tf_op jit(solution)/shard_map/pallas_call | solution.py:645
  29.3 0.2 collective-permute-done.14.r_8_
  29.5 0.8 %collective-permute-done.13.r_7_ = f32[8,128]{1,0:T(8,128)S(1)} collective-permute-done((f32[8,128]{1,0:T(8,128)S(1)}, f32[8,128]{1,0:T(8,128)S(1)}, u32[]{:S(2)}, u32[]{:S(2)}) %collective-permute-start.13) | collective-permute-done | bytes 4128 | tf_op jit(solution)/shard_map/ppermute | solution.py:552
  30.3 0.0 collective-permute-done.12.r_6_
  30.3 1.5 %shard_map.194 = (f32[32,64,128]{2,1,0:T(8,128)}, f32[32,64,128]{2,1,0:T(8,128)}) custom-call(f32[32,64,128]{2,1,0:T(8,128)S(1)} %get-tuple-element.45.r_0_, f32[32,64,128]{2,1,0:T(8,128)S(1)} %shard_map.190.r_1_, f32[32,64,128]{2,1,0:T(8,128)S(1)} %shard_map.192.r_2_, f32[3,32,128]{2,1,0:T(8,128)S(1)} %get-tuple-element.68.r_3_, ...), custom_call_target="tpu_custom_call" | custom-call | tf_op jit(solution)/shard_map/pallas_call | solution.py:648
  (27 shorter events, 0.1 us)
Async XLA Ops:
  0.6 7.7 %copy-start.8 = (bf16[256,128]{1,0:T(8,128)(2,1)S(1)}, bf16[256,128]{1,0:T(8,128)(2,1)}, u32[]{:S(2)}) copy-start(bf16[256,128]{1,0:T(8,128)(2,1)} %constant.34.clone.r_1_) | copy-start | bytes 196612
  3.2 9.0 %collective-permute-start = (f32[40,128]{1,0:T(8,128)S(1)}, f32[40,128]{1,0:T(8,128)S(1)}, u32[]{:S(2)}, u32[]{:S(2)}) collective-permute-start(f32[40,128]{1,0:T(8,128)S(1)} %get-tuple-element.38.r_2_.r_4_), channel_id=1, source_target_pairs={{4,8},{12,0},{8,4},{0,12},{5,9},{13,1},{9,5},{1,13},{6,10},{14,2},... | collective-permute-start | bytes 61448 | tf_op jit(solution)/shard_map/ppermute | solution.py:558
  8.3 3.9 %collective-permute-start.1 = (f32[40,128]{1,0:T(8,128)S(1)}, f32[40,128]{1,0:T(8,128)S(1)}, u32[]{:S(2)}, u32[]{:S(2)}) collective-permute-start(f32[40,128]{1,0:T(8,128)S(1)} %get-tuple-element.39.r_3_.r_5_), channel_id=1, source_target_pairs={{0,4},{8,12},{4,0},{12,8},{1,5},{9,13},{5,1},{13,9},{2,6},{10,14},... | collective-permute-start | bytes 61448 | tf_op jit(solution)/shard_map/ppermute | solution.py:558
  8.4 2.3 %copy-start = (bf16[256,256]{1,0:T(8,128)(2,1)S(1)}, bf16[256,256]{1,0:T(8,128)(2,1)}, u32[]{:S(2)}) copy-start(bf16[256,256]{1,0:T(8,128)(2,1)} %constant.33.clone.exw_h.exw) | copy-start | bytes 393220
  8.4 2.3 %copy-start.1 = (bf16[256,256]{1,0:T(8,128)(2,1)S(1)}, bf16[256,256]{1,0:T(8,128)(2,1)}, u32[]{:S(2)}) copy-start(bf16[256,256]{1,0:T(8,128)(2,1)} %constant.32.clone.eyw_h.eyw) | copy-start | bytes 393220
  8.4 2.3 %copy-start.11 = (f32[64,128]{1,0:T(8,128)S(1)}, f32[64,128]{1,0:T(8,128)}, u32[]{:S(2)}) copy-start(f32[64,128]{1,0:T(8,128)} %constant.41.clone.lxz) | copy-start | bytes 98308
  8.4 2.3 %copy-start.13 = (f32[32,128]{1,0:T(8,128)S(1)}, f32[32,128]{1,0:T(8,128)}, u32[]{:S(2)}) copy-start(f32[32,128]{1,0:T(8,128)} %constant.42.clone.ly) | copy-start | bytes 49156
  9.0 3.3 %collective-permute-start.2 = (f32[24,128]{1,0:T(8,128)S(1)}, f32[24,128]{1,0:T(8,128)S(1)}, u32[]{:S(2)}, u32[]{:S(2)}) collective-permute-start(f32[24,128]{1,0:T(8,128)S(1)} %get-tuple-element.41.r_6_), channel_id=1, source_target_pairs={{1,2},{3,0},{2,1},{0,3},{5,6},{7,4},{6,5},{4,7},{9,10},{11,8},{10,... | collective-permute-start | bytes 36872 | tf_op jit(solution)/shard_map/ppermute | solution.py:558
  9.7 2.6 %collective-permute-start.3 = (f32[24,128]{1,0:T(8,128)S(1)}, f32[24,128]{1,0:T(8,128)S(1)}, u32[]{:S(2)}, u32[]{:S(2)}) collective-permute-start(f32[24,128]{1,0:T(8,128)S(1)} %get-tuple-element.42.r_7_), channel_id=1, source_target_pairs={{0,1},{2,3},{1,0},{3,2},{4,5},{6,7},{5,4},{7,6},{8,9},{10,11},{9,8... | collective-permute-start | bytes 36872 | tf_op jit(solution)/shard_map/ppermute | solution.py:558
  10.7 1.6 %copy-start.2 = (f32[5,64,128]{2,1,0:T(8,128)S(1)}, f32[5,64,128]{2,1,0:T(8,128)}, u32[]{:S(2)}) copy-start(f32[5,64,128]{2,1,0:T(8,128)} %constant.44.clone.r_2_) | copy-start | bytes 491524
  10.7 1.6 %copy-start.3 = (f32[5,32,128]{2,1,0:T(8,128)S(1)}, f32[5,32,128]{2,1,0:T(8,128)}, u32[]{:S(2)}) copy-start(f32[5,32,128]{2,1,0:T(8,128)} %constant.43.clone.r_1_) | copy-start | bytes 245764
  10.7 1.6 %copy-start.10 = (f32[8,128]{1,0:T(8,128)S(1)}, f32[8,128]{1,0:T(8,128)}, u32[]{:S(2)}) copy-start(f32[8,128]{1,0:T(8,128)} %constant.45.clone.r_3_) | copy-start | bytes 12292
  12.6 5.8 %collective-permute-start.4 = (f32[40,128]{1,0:T(8,128)S(1)}, f32[40,128]{1,0:T(8,128)S(1)}, u32[]{:S(2)}, u32[]{:S(2)}) collective-permute-start(f32[40,128]{1,0:T(8,128)S(1)} %get-tuple-element.51.r_4_), channel_id=1, source_target_pairs={{4,8},{12,0},{8,4},{0,12},{5,9},{13,1},{9,5},{1,13},{6,10},{14,2},... | collective-permute-start | bytes 61448 | tf_op jit(solution)/shard_map/ppermute | solution.py:558
  14.4 4.1 %collective-permute-start.5 = (f32[40,128]{1,0:T(8,128)S(1)}, f32[40,128]{1,0:T(8,128)S(1)}, u32[]{:S(2)}, u32[]{:S(2)}) collective-permute-start(f32[40,128]{1,0:T(8,128)S(1)} %get-tuple-element.52.r_5_), channel_id=1, source_target_pairs={{0,4},{8,12},{4,0},{12,8},{1,5},{9,13},{5,1},{13,9},{2,6},{10,14},... | collective-permute-start | bytes 61448 | tf_op jit(solution)/shard_map/ppermute | solution.py:558
  14.8 1.9 %copy-start.4 = (f32[64,128]{1,0:T(8,128)S(1)}, f32[64,128]{1,0:T(8,128)}, u32[]{:S(2)}) copy-start(f32[64,128]{1,0:T(8,128)} %constant.47.clone.sx0_h.sx0) | copy-start | bytes 98308
  14.8 1.9 %copy-start.5 = (bf16[256,128]{1,0:T(8,128)(2,1)S(1)}, bf16[256,128]{1,0:T(8,128)(2,1)}, u32[]{:S(2)}) copy-start(bf16[256,128]{1,0:T(8,128)(2,1)} %constant.35.clone.colw) | copy-start | bytes 196612
  15.1 1.6 %copy-start.9 = (f32[8,128]{1,0:T(8,128)S(1)}, f32[8,128]{1,0:T(8,128)}, u32[]{:S(2)}) copy-start(f32[8,128]{1,0:T(8,128)} %constant.46.clone.line_h.line) | copy-start | bytes 12292
  15.1 3.3 %collective-permute-start.6 = (f32[24,128]{1,0:T(8,128)S(1)}, f32[24,128]{1,0:T(8,128)S(1)}, u32[]{:S(2)}, u32[]{:S(2)}) collective-permute-start(f32[24,128]{1,0:T(8,128)S(1)} %get-tuple-element.54.r_6_), channel_id=1, source_target_pairs={{1,2},{3,0},{2,1},{0,3},{5,6},{7,4},{6,5},{4,7},{9,10},{11,8},{10,... | collective-permute-start | bytes 36872 | tf_op jit(solution)/shard_map/ppermute | solution.py:558
  15.2 3.2 %collective-permute-start.7 = (f32[24,128]{1,0:T(8,128)S(1)}, f32[24,128]{1,0:T(8,128)S(1)}, u32[]{:S(2)}, u32[]{:S(2)}) collective-permute-start(f32[24,128]{1,0:T(8,128)S(1)} %get-tuple-element.55.r_7_), channel_id=1, source_target_pairs={{0,1},{2,3},{1,0},{3,2},{4,5},{6,7},{5,4},{7,6},{8,9},{10,11},{9,8... | collective-permute-start | bytes 36872 | tf_op jit(solution)/shard_map/ppermute | solution.py:558
  18.9 5.9 %collective-permute-start.10 = (f32[40,128]{1,0:T(8,128)S(1)}, f32[40,128]{1,0:T(8,128)S(1)}, u32[]{:S(2)}, u32[]{:S(2)}) collective-permute-start(f32[40,128]{1,0:T(8,128)S(1)} %get-tuple-element.62.r_2_), channel_id=1, source_target_pairs={{4,8},{12,0},{8,4},{0,12},{5,9},{13,1},{9,5},{1,13},{6,10},{14,2},... | collective-permute-start | bytes 61448 | tf_op jit(solution)/shard_map/ppermute | solution.py:558
  21.7 4.7 %collective-permute-start.9 = (f32[40,128]{1,0:T(8,128)S(1)}, f32[40,128]{1,0:T(8,128)S(1)}, u32[]{:S(2)}, u32[]{:S(2)}) collective-permute-start(f32[40,128]{1,0:T(8,128)S(1)} %get-tuple-element.63.r_3_), channel_id=1, source_target_pairs={{0,8},{4,12},{8,0},{12,4},{1,9},{5,13},{9,1},{13,5},{2,10},{6,14},... | collective-permute-start | bytes 61448 | tf_op jit(solution)/shard_map/ppermute | solution.py:552
  21.9 4.5 %collective-permute-start.8 = (f32[40,128]{1,0:T(8,128)S(1)}, f32[40,128]{1,0:T(8,128)S(1)}, u32[]{:S(2)}, u32[]{:S(2)}) collective-permute-start(f32[40,128]{1,0:T(8,128)S(1)} %get-tuple-element.63.r_3_), channel_id=1, source_target_pairs={{0,4},{8,12},{4,0},{12,8},{1,5},{9,13},{5,1},{13,9},{2,6},{10,14},... | collective-permute-start | bytes 61448 | tf_op jit(solution)/shard_map/ppermute | solution.py:558
  23.4 5.0 %copy-start.6 = (f32[128,128]{1,0:T(8,128)S(1)}, f32[128,128]{1,0:T(8,128)}, u32[]{:S(2)}) copy-start(f32[128,128]{1,0:T(8,128)} %constant.39.clone.r_11_) | copy-start | bytes 196612
  23.4 5.0 %copy-start.7 = (f32[128,128]{1,0:T(8,128)S(1)}, f32[128,128]{1,0:T(8,128)}, u32[]{:S(2)}) copy-start(f32[128,128]{1,0:T(8,128)} %constant.36.clone.r_8_) | copy-start | bytes 196612
  23.4 5.0 %copy-start.14 = (f32[32,32]{1,0:T(8,128)S(1)}, f32[32,32]{1,0:T(8,128)}, u32[]{:S(2)}) copy-start(f32[32,32]{1,0:T(8,128)} %constant.38.clone.r_10_) | copy-start | bytes 12292
  24.8 3.6 %copy-start.12 = (f32[64,64]{1,0:T(8,128)S(1)}, f32[64,64]{1,0:T(8,128)}, u32[]{:S(2)}) copy-start(f32[64,64]{1,0:T(8,128)} %constant.37.clone.r_9_) | copy-start | bytes 49156
  24.8 3.6 %collective-permute-start.11 = (f32[24,128]{1,0:T(8,128)S(1)}, f32[24,128]{1,0:T(8,128)S(1)}, u32[]{:S(2)}, u32[]{:S(2)}) collective-permute-start(f32[24,128]{1,0:T(8,128)S(1)} %get-tuple-element.67), channel_id=1, source_target_pairs={{0,1},{1,2},{2,3},{3,0},{4,5},{5,6},{6,7},{7,4},{8,9},{9,10},{10,1... | collective-permute-start | bytes 36872 | tf_op jit(solution)/shard_map/ppermute | solution.py:552
  26.4 3.1 %collective-permute-start.14 = (f32[8,128]{1,0:T(8,128)S(1)}, f32[8,128]{1,0:T(8,128)S(1)}, u32[]{:S(2)}, u32[]{:S(2)}) collective-permute-start(f32[8,128]{1,0:T(8,128)S(1)} %add_add_fusion.r_5_), channel_id=1, source_target_pairs={{1,2},{3,0},{2,1},{0,3},{5,6},{7,4},{6,5},{4,7},{9,10},{11,8},{10,... | collective-permute-start | bytes 12296 | tf_op jit(solution)/shard_map/ppermute | solution.py:558
  26.7 3.6 %collective-permute-start.13 = (f32[8,128]{1,0:T(8,128)S(1)}, f32[8,128]{1,0:T(8,128)S(1)}, u32[]{:S(2)}, u32[]{:S(2)}) collective-permute-start(f32[8,128]{1,0:T(8,128)S(1)} %add_add_fusion.r_5_), channel_id=1, source_target_pairs={{0,2},{1,3},{2,0},{3,1},{4,6},{5,7},{6,4},{7,5},{8,10},{9,11},{10,... | collective-permute-start | bytes 12296 | tf_op jit(solution)/shard_map/ppermute | solution.py:552
  28.1 2.2 %collective-permute-start.12 = (f32[8,128]{1,0:T(8,128)S(1)}, f32[8,128]{1,0:T(8,128)S(1)}, u32[]{:S(2)}, u32[]{:S(2)}) collective-permute-start(f32[8,128]{1,0:T(8,128)S(1)} %add_add_fusion.r_5_), channel_id=1, source_target_pairs={{0,1},{2,3},{1,0},{3,2},{4,5},{6,7},{5,4},{7,6},{8,9},{10,11},{9,8... | collective-permute-start | bytes 12296 | tf_op jit(solution)/shard_map/ppermute | solution.py:558
